TPU v7x, 128 devices: a whole 4x4x4 slice. The times are simulated.
128 devices in a mesh: grp: 4 (over z_hi, core), blk: 32 (over x, z_lo, y).
Axes of the slice: x: 4, y: 4, z: 4 (z_hi: 2, z_lo: 2; z = z_hi * 2 + z_lo), core: 2. Of those that a mesh axis runs over, the one named last changes fastest.
Arguments:
- integrals: bfloat16 [32768, 32768], P('blk', 'grp'), may hold values from -0.046875 to 0.046875
- block_mask: int32 [256, 256], P('blk', 'grp'), may hold values from 0 to 1, as said below
- amplitudes: bfloat16 [32768, 1024], P(('grp', 'blk')), may hold values from -6 to 6
- pair_batches: int32 [8], replicated, may hold values from 0 to 7, each once
Outputs:
- ladder: bfloat16 [1024, 32768], P('grp', 'blk')
Inputs may be any that keep to these rules, and one draw needn't show every extreme that they name: `block_mask`: 0 or 1; the share of kept tiles rises from about a quarter in the first tile row to about three quarters in the last. `pair_batches`: each batch number once.
All inputs are finite; a program needn't handle non-finite values.
Results may differ from a plain program's by a relative error of at most 0.001.
Values may be sent and summed in bfloat16 or wider, within the bound.
No kernel may reach another device: no remote copies, remote signals or barrier semaphores. Data moves between devices by JAX's collectives and lax.ppermute only.
A program may use at most 128 MiB of HBM per device.

v0:
```python
import jax
import jax.numpy as jnp
from jax import lax
from jax.sharding import PartitionSpec as P

BLOCK = 128
BATCH = 128
NB = 8


def on_device(integrals, block_mask, amplitudes, pair_batches):
    rows_in = amplitudes.shape[0]
    grouped = amplitudes.reshape(rows_in, NB, BATCH)
    selector = (pair_batches[:, None] == jnp.arange(NB, dtype=jnp.int32)[None, :]).astype(
        jnp.bfloat16
    )
    picked = jnp.einsum("rnb,mn->rmb", grouped, selector, preferred_element_type=jnp.float32)
    chosen = picked.astype(jnp.bfloat16).reshape(rows_in, NB * BATCH)
    out_rows = integrals.shape[0]
    fragment = lax.all_gather(chosen, "blk", axis=0, tiled=True)
    number = fragment.shape[0]
    mcols = block_mask.astype(jnp.bfloat16)
    tiled = (
        integrals.reshape(out_rows // BLOCK, BLOCK, number // BLOCK, BLOCK)
        * mcols[:, None, :, None]
    )
    masked = tiled.reshape(out_rows, number)
    partial_sum = lax.dot_general(
        fragment, masked, (((0,), (1,)), ((), ())), preferred_element_type=jnp.float32
    )
    owned = lax.psum_scatter(partial_sum, "grp", scatter_dimension=0, tiled=True)
    return owned.astype(jnp.bfloat16)


def solution(mesh):
    in_specs = (P("blk", "grp"), P("blk", "grp"), P(("grp", "blk"), None), P())
    out_specs = P("grp", "blk")
    return jax.shard_map(
        on_device, mesh=mesh, in_specs=in_specs, out_specs=out_specs, check_vma=False
    )
```

profile of v0, /device:TPU:1, one launch (start us, length us, event | category | flops | bytes accessed | tf_op | source)
XLA Modules:
  0.0 298.4 jit_solution(4227521799634697145)
XLA Ops:
  6.5 0.0 all-gather.2.cloned.1.call-start
  6.5 1.1 copy.5
  7.7 1.0 convolution_convert_fusion
  8.7 0.9 copy.13
  9.6 0.0 all-gather.2.cloned.1.call-update
  9.6 0.0 reduce-scatter.2.cloned.1.call-start
  9.7 0.7 convert_element_type.15
  10.3 192.8 %all-gather.2.cloned.1.call-done = bf16[8192,1024]{1,0:T(8,128)(2,1)} async-done(((bf16[256,1024]{1,0:T(8,128)(2,1)}), bf16[8192,1024]{1,0:T(8,128)(2,1)}) %all-gather.2.cloned.1.call-update) | async-done | bytes 16777232 | tf_op jit(solution)/shard_map/all_gather | solution.py:20
  203.2 6.5 %mul.11 = bf16[8,128,64,128]{3,2,1,0:T(8,128)(2,1)} broadcast(bf16[8,64]{1,0:T(8,128)(2,1)S(1)} %convert_element_type.15), dimensions={0,2} | broadcast | bytes 16778240 | tf_op jit(solution)/shard_map/mul | solution.py:24
  209.6 29.5 %fusion = f32[1024,1024]{1,0:T(8,128)} fusion(bf16[8192,1024]{1,0:T(8,128)(2,1)} %all-gather.2.cloned.1.call-done, bf16[1024,8192]{1,0:T(8,128)(2,1)} %param.4, bf16[128,8,64,128]{3,2,1,0:T(8,128)(2,1)} %bitcast.17), kind=kOutput, calls=%fused_computation.1 | convolution fusion | flops 17188257792 | bytes 54525952 | tf_op jit(solution)/shard_map/dot_general | solution.py:28
  239.1 0.0 reduce-scatter.2.cloned.1.call-update
  239.1 50.3 %reduce-scatter.2.cloned.1.call-done = f32[256,1024]{1,0:T(8,128)} async-done(((f32[1024,1024]{1,0:T(8,128)}), f32[256,1024]{1,0:T(8,128)}) %reduce-scatter.2.cloned.1.call-update) | async-done | bytes 1048592 | tf_op jit(solution)/shard_map/reduce_scatter | solution.py:31
  289.5 2.1 convert_element_type.16
Async XLA Ops:
  6.5 196.6 %all-gather.2.cloned.1.call-start = ((), (), s32[]{:S(2)}) async-start(), calls=%async_computation.1 | async-start | bytes 17301504 | tf_op jit(solution)/shard_map/all_gather | solution.py:20
  9.6 279.9 %reduce-scatter.2.cloned.1.call-start = ((), (), s32[]{:S(2)}) async-start(), calls=%async_computation.2 | async-start | bytes 5242880 | tf_op jit(solution)/shard_map/reduce_scatter | solution.py:31
Sparse Core Ops, SparseCore 0:
  9.7 193.3 all-gather.1
  239.3 50.1 reduce-scatter.1
where the time goes:
time: 299 us; the launch traced here: 298 us
  waiting for transfers between devices  243 us (81%)
  matrix products  30.5 us (10%)
  between operations  13.4 us (4%)
  local copies, waits for them, and re-layouts  8.49 us (3%)
    all_gather x1, waiting for transfers between devices, on_device(): fragment = lax.all_gather(chosen, 'blk', axis=0, tiled=True)  193 us
    reduce_scatter x1, waiting for transfers between devices, on_device(): lax.psum_scatter(partial_sum, 'grp', scatter_dimension=0, tiled=True)  50.3 us
    dot_general x1, matrix products, on_device(): lax.dot_general(fragment, masked, (((0,), (1,)), ((), ())), preferred_ele...  29.5 us
    mul x1, local copies, waits for them, and re-layouts, on_device(): integrals.reshape(out_rows // BLOCK, BLOCK, number // BLOCK, BLOCK)  6.47 us
  transfers between devices with their start and end apart: 2, of which 2 were waited for; matrix products, arithmetic and copies ran while one was open for 0% of the time, Pallas kernels for 0%

commit v1 on v0

v1 whole, which is shorter than its diff:
```python
import functools

import jax
import jax.numpy as jnp
from jax import lax
from jax.experimental import pallas as pl
from jax.experimental.pallas import tpu as pltpu
from jax.sharding import PartitionSpec as P


BLOCK = 128
BATCH = 128
NB = 8
NX, NZ, NY = 4, 2, 4
F32, BF16 = jnp.float32, jnp.bfloat16

LIMIT = 6 << 20
LINE = (-1, 1, 2)


def blk(x, z, y):
    return (x % NX) * (NZ * NY) + z * NY + y % NY


def perm(dx, dz, dy):
    cells = [(x, z, y) for x in range(NX) for z in range(NZ) for y in range(NY)]
    return [(blk(x, z, y), blk(x + dx, z ^ dz, y + dy)) for x, z, y in cells]


XP, XM, YP, YM, ZX = perm(1, 0, 0), perm(-1, 0, 0), perm(0, 0, 1), perm(0, 0, -1), perm(0, 1, 0)
CORE = [(g, g ^ 1) for g in range(4)]
ZHI = [(g, g ^ 2) for g in range(4)]


def send(array, pairs):
    return lax.ppermute(array, "blk", pairs)


def off_chip(array):
    return pltpu.with_memory_space_constraint(array, pltpu.HBM)


def vmem(count):
    return [pl.BlockSpec(memory_space=pltpu.VMEM)] * count


def params():
    return pltpu.CompilerParams(vmem_limit_bytes=LIMIT)


def pick_kernel(batches, amp_ref, out_ref, sems):
    g = lax.axis_index("grp")

    def copy(k):
        owner = g ^ (2 * (k & 1) + (k >> 2))
        at = batches[2 * owner + ((k >> 1) & 1)]
        src = amp_ref.at[:, pl.ds(pl.multiple_of(at * BATCH, BATCH), BATCH)]
        return pltpu.make_async_copy(src, out_ref.at[:, pl.ds(k * BATCH, BATCH)], sems.at[k])

    for k in range(NB):
        copy(k).start()
    for k in range(NB):
        copy(k).wait()


def pick(amplitudes, batches):
    return pl.pallas_call(
        pick_kernel,
        out_shape=jax.ShapeDtypeStruct(amplitudes.shape, BF16),
        grid_spec=pltpu.PrefetchScalarGridSpec(
            num_scalar_prefetch=1,
            grid=(),
            in_specs=[pl.BlockSpec(memory_space=pltpu.HBM)],
            out_specs=pl.BlockSpec(memory_space=pltpu.VMEM),
            scratch_shapes=[pltpu.SemaphoreType.DMA((NB,))],
        ),
        cost_estimate=pl.CostEstimate(flops=1000, bytes_accessed=1 << 20, transcendentals=0),
        compiler_params=params(),
        name="pick",
    )(batches, off_chip(amplitudes))


def keep_kernel(first, mask_ref, v_ref, out_ref, sems):
    tiles = out_ref.shape[0] // BLOCK

    def copy(r):
        rows = pl.ds((first + r) * BLOCK, BLOCK)
        return pltpu.make_async_copy(v_ref.at[rows], out_ref.at[pl.ds(r * BLOCK, BLOCK)], sems.at[r])

    for r in range(tiles):
        copy(r).start()
    for r in range(tiles):
        copy(r).wait()

        def body(c, carry, r=r):
            for k in range(8):
                at = pl.ds(pl.multiple_of((c * 8 + k) * BLOCK, BLOCK), BLOCK)
                tile = out_ref[r * BLOCK : (r + 1) * BLOCK, at]
                kept = mask_ref[first + r, c * 8 + k] != 0
                out_ref[r * BLOCK : (r + 1) * BLOCK, at] = jnp.where(kept, tile, jnp.zeros_like(tile))
            return carry

        lax.fori_loop(0, out_ref.shape[1] // (8 * BLOCK), body, 0)


def keep(first, tiles, v, mask):
    return pl.pallas_call(
        functools.partial(keep_kernel, first),
        out_shape=jax.ShapeDtypeStruct((tiles * BLOCK, v.shape[1]), BF16),
        grid_spec=pltpu.PrefetchScalarGridSpec(
            num_scalar_prefetch=1,
            grid=(),
            in_specs=[pl.BlockSpec(memory_space=pltpu.HBM)],
            out_specs=pl.BlockSpec(memory_space=pltpu.VMEM),
            scratch_shapes=[pltpu.SemaphoreType.DMA((tiles,))],
        ),
        cost_estimate=pl.CostEstimate(flops=1000, bytes_accessed=tiles << 21, transcendentals=0),
        compiler_params=params(),
    )(mask, off_chip(v))


def lay_kernel(slots, base, *refs):
    sources, outs = refs[: len(slots)], refs[-2:]
    for slot, source in zip(slots, sources):
        for k in range(2):
            at = base + 2 * BATCH * k
            outs[k][slot] = source[:, at : at + 2 * BATCH]


def lay(slots, base, arrays, before=()):
    out = jax.ShapeDtypeStruct((6, arrays[0].shape[0], 2 * BATCH), BF16)
    return pl.pallas_call(
        functools.partial(lay_kernel, slots, base),
        out_shape=(out, out),
        in_specs=vmem(len(arrays)) + [pl.BlockSpec(memory_space=pl.ANY)] * len(before),
        out_specs=vmem(2),
        input_output_aliases={len(arrays) + k: k for k in range(len(before))},
        cost_estimate=pl.CostEstimate(flops=1000, bytes_accessed=1 << 20, transcendentals=0),
        compiler_params=params(),
    )(*arrays, *before)


def dot(a, b):
    return jnp.dot(a, b, preferred_element_type=F32)


def column(offset):
    b = lax.axis_index("blk")
    x, z, y = b // (NZ * NY), (b // NY) % NZ, b % NY
    dx, dz, dy = offset
    at = ((x + dx) & 3) * (NZ * NY) + (z ^ dz) * NY + ((y + dy) & 3)
    return pl.ds(pl.multiple_of(at * 256, 256), 256)


def cross_kernel(offsets, *refs):
    steps = len(offsets)
    parts, (top, bottom), before, acc_ref = refs[:steps], refs[steps : steps + 2], refs[steps + 2 : -1], refs[-1]
    rows = top.shape[0]
    for i, offset in enumerate(offsets):
        for k, v_ref in enumerate((top, bottom)):
            at = slice(k * rows, (k + 1) * rows)
            product = dot(v_ref[:, column(offset)], parts[i][...])
            if i > 0:
                acc_ref[at, :] += product
            else:
                acc_ref[at, :] = before[0][at, :] + product if before else product


def cross(offsets, parts, v, before=()):
    rows = 2 * v[0].shape[0]
    steps = len(parts)
    return pl.pallas_call(
        functools.partial(cross_kernel, offsets),
        out_shape=jax.ShapeDtypeStruct((rows, NB * BATCH), F32),
        in_specs=vmem(steps + 2 + len(before)),
        out_specs=pl.BlockSpec(memory_space=pltpu.VMEM),
        cost_estimate=pl.CostEstimate(
            flops=2 * rows * steps * 256 * 1024, bytes_accessed=steps << 20, transcendentals=0
        ),
        compiler_params=params(),
    )(*parts, *v, *before)


def group_kernel(index, *refs):
    ys, xs, (top, bottom, acc_ref, mine, theirs) = refs[:3], refs[3:6], refs[6:]
    cols, rows = mine.shape[1], top.shape[0]
    for k, v_ref in enumerate((top, bottom)):
        at = slice(k * rows, (k + 1) * rows)
        first = True
        for j, dy in enumerate(LINE):
            for i, dx in enumerate(LINE):
                for dz in (0, 1):
                    tile = v_ref[:, column((dx, dz, dy))]
                    for out, part, slot, base in (
                        (mine, ys[j], 2 * i + dz, index),
                        (theirs, xs[i], 2 * j + dz, 2 + index),
                    ):
                        product = dot(tile, part[slot])
                        if first:
                            out[at, :] = acc_ref[at, base * cols : (base + 1) * cols] + product
                        else:
                            out[at, :] += product
                    first = False


def group(index, ys, xs, v, acc):
    rows = 2 * v[0].shape[0]
    cols = ys[0].shape[2]
    out = jax.ShapeDtypeStruct((rows, cols), F32)
    return pl.pallas_call(
        functools.partial(group_kernel, index),
        out_shape=(out, out),
        in_specs=vmem(9),
        out_specs=vmem(2),
        cost_estimate=pl.CostEstimate(
            flops=2 * rows * 18 * 256 * 512, bytes_accessed=18 << 20, transcendentals=0
        ),
        compiler_params=params(),
    )(*ys, *xs, *v, acc)


def finish_kernel(*refs):
    out_ref = refs[-1]
    for k in range(2):
        mine, got, far = refs[3 * k : 3 * k + 3]
        total = mine[:, :BATCH] + got[:, :BATCH] + far[...]
        out_ref[k * BATCH : (k + 1) * BATCH, :] = total.T.astype(BF16)


def finish(parts):
    rows = parts[0].shape[0]
    return pl.pallas_call(
        finish_kernel,
        out_shape=jax.ShapeDtypeStruct((2 * BATCH, rows), BF16),
        in_specs=vmem(6),
        out_specs=pl.BlockSpec(memory_space=pltpu.VMEM),
        cost_estimate=pl.CostEstimate(flops=1000000, bytes_accessed=3 << 20, transcendentals=0),
        compiler_params=params(),
        name="finish",
    )(*parts)


def on_device(integrals, block_mask, amplitudes, pair_batches):
    own = pick(amplitudes, pair_batches)
    near = send(own, ZX)
    xp0, yp0 = send(own, XM), send(own, YM)
    xm0, ym0 = send(own, XP), send(own, YP)
    xp1, yp1 = send(near, XM), send(near, YM)
    xm1, ym1 = send(near, XP), send(near, YP)
    x20, y20 = send(xm0, XP), send(ym0, YP)
    x21, y21 = send(xp1, XM), send(yp1, YM)

    early_x = lay((0, 1, 2, 3), 0, [xm0, xm1, xp0, xp1])
    early_y = lay((0, 1, 2, 3), 512, [ym0, ym1, yp0, yp1])
    along_x = lay((4, 5), 0, [x20, x21], early_x)
    along_y = lay((4, 5), 512, [y20, y21], early_y)

    pieces = []
    for k in range(2):
        ym, yp = send(along_x[k], YP), send(along_x[k], YM)
        xm, xp = send(along_y[k], XP), send(along_y[k], XM)
        if k == 0:
            y2, x2 = send(ym, YP), send(xm, XP)
        else:
            y2, x2 = send(yp, YM), send(xp, XM)
        pieces.append(([ym, yp, y2], [xm, xp, x2]))

    v = [keep(4 * k, 4, integrals, block_mask) for k in range(2)]
    near_at = [(-1, 0, 0), (1, 0, 0), (0, 0, -1), (0, 0, 1)]
    far_at = [(dx, 1, dy) for dx, dz, dy in near_at] + [(2, 0, 0), (2, 1, 0), (0, 0, 2), (0, 1, 2)]
    acc = cross([(0, 0, 0), (0, 1, 0)] + near_at, [own, near, xm0, xp0, ym0, yp0], v)
    acc = cross(far_at, [xm1, xp1, ym1, yp1, x20, x21, y20, y21], v, [acc])

    parts = []
    for k in range(2):
        mine, theirs = group(k, *pieces[k], v, acc)
        got = lax.ppermute(theirs, "grp", CORE)
        far = lax.ppermute(mine[:, BATCH:] + got[:, BATCH:], "grp", ZHI)
        parts += [mine, got, far]
    return finish(parts)


def solution(mesh):
    in_specs = (P("blk", "grp"), P("blk", "grp"), P(("grp", "blk"), None), P())
    out_specs = P("grp", "blk")

    return jax.shard_map(on_device, mesh=mesh, in_specs=in_specs, out_specs=out_specs, check_vma=False)
```

time: 299 us -> 159 us (0.53)
  waiting for transfers between devices: 243 us -> 74.8 us
  starting transfers between devices: 0.04 us -> 50.3 us
  Pallas kernels: 0 us -> 32.3 us
  matrix products: 30.5 us -> 0 us
  between operations: 13.4 us -> 0.15 us
  local copies, waits for them, and re-layouts: 8.49 us -> 0.66 us
    all_gather x1 -> x0, waiting for transfers between devices: 193 us -> none  [on_device(): fragment = lax.all_gather(chosen, 'blk', axis=0, tiled=True)]
    ppermute x0 -> x29, waiting for transfers between devices: none -> 74.8 us  [the longest x25 53.6 us: send(): return lax.ppermute(array, 'blk', pairs)]
    reduce_scatter x1 -> x0, waiting for transfers between devices: 50.3 us -> none  [on_device(): lax.psum_scatter(partial_sum, 'grp', scatter_dimension=0, tiled=True)]
    ppermute x0 -> x29, starting transfers between devices: none -> 50.3 us  [the longest x25 31.9 us: send(): return lax.ppermute(array, 'blk', pairs)]
    pallas_call x0 -> x12, Pallas kernels: none -> 32.3 us  [the longest x2 11.1 us: keep(): pl.pallas_call(functools.partial(keep_kernel, first), out_shape=jax.Shape...]
    dot_general x2 -> x0, matrix products: 30.5 us -> none  [the longest x1 29.5 us: on_device(): lax.dot_general(fragment, masked, (((0,), (1,)), ((), ())), preferred_ele...]
    mul x1 -> x0, local copies, waits for them, and re-layouts: 6.47 us -> none  [on_device(): integrals.reshape(out_rows // BLOCK, BLOCK, number // BLOCK, BLOCK)]
  transfers between devices with their start and end apart: 2 -> 29, of which waited for: 2 -> 10; matrix products, arithmetic and copies ran while one was open for 0% -> 0% of each run, Pallas kernels for 0% -> 19%
where the time goes in v1:
time: 159 us; the launch traced here: 158 us
  waiting for transfers between devices  74.8 us (47%)
  starting transfers between devices  50.3 us (32%)
  Pallas kernels  32.3 us (20%)
    ppermute x25, waiting for transfers between devices, send(): return lax.ppermute(array, 'blk', pairs)  53.6 us
    ppermute x25, starting transfers between devices, send(): return lax.ppermute(array, 'blk', pairs)  31.9 us
    ppermute x2, waiting for transfers between devices, on_device(): far = lax.ppermute(mine[:, BATCH:] + got[:, BATCH:], 'grp', ZHI)  21.2 us
    ppermute x2, starting transfers between devices, on_device(): got = lax.ppermute(theirs, 'grp', CORE)  12.8 us
    pallas_call x2, Pallas kernels, keep(): pl.pallas_call(functools.partial(keep_kernel, first), out_shape=jax.Shape...  11.1 us
    pallas_call x2, Pallas kernels, group(): pl.pallas_call(functools.partial(group_kernel, index), out_shape=(out, ou...  10.1 us
    pallas_call x2, Pallas kernels, cross(): pl.pallas_call(functools.partial(cross_kernel, offsets), out_shape=jax.Sh...  8.05 us
    ppermute x2, starting transfers between devices, on_device(): far = lax.ppermute(mine[:, BATCH:] + got[:, BATCH:], 'grp', ZHI)  5.68 us
  transfers between devices with their start and end apart: 29, of which 10 were waited for; matrix products, arithmetic and copies ran while one was open for 0% of the time, Pallas kernels for 19%

profile of v1, /device:TPU:1, one launch (start us, length us, event | category | flops | bytes accessed | tf_op | source)
XLA Modules:
  0.0 158.4 jit_solution(11874271584717331290)
XLA Ops:
  0.0 0.7 copy-done.1
  0.7 1.7 %pick.1.refs_0_ = bf16[256,1024]{1,0:T(8,128)(2,1)S(1)} custom-call(s32[8]{0:T(128)S(1)} %copy-done.1, bf16[256,1024]{1,0:T(8,128)(2,1)} %amp_ref.1), custom_call_target="tpu_custom_call" | custom-call | flops 1000 | bytes 1048576 | tf_op jit(solution)/shard_map/pick/pallas_call | solution.py:67
  2.4 2.5 %collective-permute-start.2 = (bf16[256,1024]{1,0:T(8,128)(2,1)S(1)}, bf16[256,1024]{1,0:T(8,128)(2,1)S(1)}, u32[]{:S(2)}, u32[]{:S(2)}) collective-permute-start(bf16[256,1024]{1,0:T(8,128)(2,1)S(1)} %pick.1.refs_0_), channel_id=1, source_target_pairs={{0,4},{1,5},{2,6},{3,7},{4,0},{5,1},{6,2},{7,3},{8,12},{9,13},{10,... | collective-permute-start | bytes 1572872 | tf_op jit(solution)/shard_map/ppermute | solution.py:36
  4.9 1.2 collective-permute-start
  6.1 1.3 collective-permute-start.10
  7.4 9.1 %collective-permute-done.2.refs_1_ = bf16[256,1024]{1,0:T(8,128)(2,1)S(1)} collective-permute-done((bf16[256,1024]{1,0:T(8,128)(2,1)S(1)}, bf16[256,1024]{1,0:T(8,128)(2,1)S(1)}, u32[]{:S(2)}, u32[]{:S(2)}) %collective-permute-start.2) | collective-permute-done | bytes 524320 | tf_op jit(solution)/shard_map/ppermute | solution.py:36
  16.5 2.6 %collective-permute-start.12 = (bf16[256,1024]{1,0:T(8,128)(2,1)S(1)}, bf16[256,1024]{1,0:T(8,128)(2,1)S(1)}, u32[]{:S(2)}, u32[]{:S(2)}) collective-permute-start(bf16[256,1024]{1,0:T(8,128)(2,1)S(1)} %collective-permute-done.2.refs_1_), channel_id=1, source_target_pairs={{0,3},{1,0},{2,1},{3,2},{4,7},{5,4},{6,5},{7,6},{8,11},{9,8},{10,9... | collective-permute-start | bytes 1572872 | tf_op jit(solution)/shard_map/ppermute | solution.py:36
  19.2 0.5 collective-permute-start.15
  19.6 2.5 %collective-permute-start.3 = (bf16[256,1024]{1,0:T(8,128)(2,1)S(1)}, bf16[256,1024]{1,0:T(8,128)(2,1)S(1)}, u32[]{:S(2)}, u32[]{:S(2)}) collective-permute-start(bf16[256,1024]{1,0:T(8,128)(2,1)S(1)} %collective-permute-done.2.refs_1_), channel_id=1, source_target_pairs={{0,24},{1,25},{2,26},{3,27},{4,28},{5,29},{6,30},{7,31},{8,0},{9,1... | collective-permute-start | bytes 1572872 | tf_op jit(solution)/shard_map/ppermute | solution.py:36
  22.1 0.0 collective-permute-done.refs_0_.refs_2_
  22.1 1.0 collective-permute-start.14
  23.1 0.0 collective-permute-done.10.refs_0_.refs_4_
  23.1 0.1 collective-permute-start.11
  23.2 5.9 %collective-permute-done.12.refs_3_ = bf16[256,1024]{1,0:T(8,128)(2,1)S(1)} collective-permute-done((bf16[256,1024]{1,0:T(8,128)(2,1)S(1)}, bf16[256,1024]{1,0:T(8,128)(2,1)S(1)}, u32[]{:S(2)}, u32[]{:S(2)}) %collective-permute-start.12) | collective-permute-done | bytes 524320 | tf_op jit(solution)/shard_map/ppermute | solution.py:36
  29.1 3.4 %collective-permute-start.13 = (bf16[256,1024]{1,0:T(8,128)(2,1)S(1)}, bf16[256,1024]{1,0:T(8,128)(2,1)S(1)}, u32[]{:S(2)}, u32[]{:S(2)}) collective-permute-start(bf16[256,1024]{1,0:T(8,128)(2,1)S(1)} %collective-permute-done.12.refs_3_), channel_id=1, source_target_pairs={{0,3},{1,0},{2,1},{3,2},{4,7},{5,4},{6,5},{7,6},{8,11},{9,8},{10,9... | collective-permute-start | bytes 1572872 | tf_op jit(solution)/shard_map/ppermute | solution.py:36
  32.5 7.8 %collective-permute-done.15.refs_2_.refs_5_ = bf16[256,1024]{1,0:T(8,128)(2,1)S(1)} collective-permute-done((bf16[256,1024]{1,0:T(8,128)(2,1)S(1)}, bf16[256,1024]{1,0:T(8,128)(2,1)S(1)}, u32[]{:S(2)}, u32[]{:S(2)}) %collective-permute-start.15) | collective-permute-done | bytes 524320 | tf_op jit(solution)/shard_map/ppermute | solution.py:36
  40.3 2.5 %collective-permute-start.6 = (bf16[256,1024]{1,0:T(8,128)(2,1)S(1)}, bf16[256,1024]{1,0:T(8,128)(2,1)S(1)}, u32[]{:S(2)}, u32[]{:S(2)}) collective-permute-start(bf16[256,1024]{1,0:T(8,128)(2,1)S(1)} %pick.1.refs_0_), channel_id=1, source_target_pairs={{0,24},{1,25},{2,26},{3,27},{4,28},{5,29},{6,30},{7,31},{8,0},{9,1... | collective-permute-start | bytes 1572872 | tf_op jit(solution)/shard_map/ppermute | solution.py:36
  42.8 0.0 collective-permute-done.3.refs_3_.refs_1_
  42.8 0.0 collective-permute-start.5
  42.8 0.0 collective-permute-done.14.refs_1_.refs_2_
  42.8 0.2 collective-permute-start.1
  43.0 2.8 %collective-permute-done.11.refs_0_.refs_6_ = bf16[256,1024]{1,0:T(8,128)(2,1)S(1)} collective-permute-done((bf16[256,1024]{1,0:T(8,128)(2,1)S(1)}, bf16[256,1024]{1,0:T(8,128)(2,1)S(1)}, u32[]{:S(2)}, u32[]{:S(2)}) %collective-permute-start.11) | collective-permute-done | bytes 524320 | tf_op jit(solution)/shard_map/ppermute | solution.py:36
  45.8 0.5 collective-permute-start.4
  46.4 0.1 shard_map.48
  46.5 5.1 %collective-permute-done.13.refs_1_.refs_7_ = bf16[256,1024]{1,0:T(8,128)(2,1)S(1)} collective-permute-done((bf16[256,1024]{1,0:T(8,128)(2,1)S(1)}, bf16[256,1024]{1,0:T(8,128)(2,1)S(1)}, u32[]{:S(2)}, u32[]{:S(2)}) %collective-permute-start.13) | collective-permute-done | bytes 524320 | tf_op jit(solution)/shard_map/ppermute | solution.py:36
  51.6 2.5 %collective-permute-start.25 = (bf16[6,256,256]{2,1,0:T(8,128)(2,1)S(1)}, bf16[6,256,256]{2,1,0:T(8,128)(2,1)S(1)}, u32[]{:S(2)}, u32[]{:S(2)}) collective-permute-start(bf16[6,256,256]{2,1,0:T(8,128)(2,1)S(1)} %get-tuple-element.26), channel_id=1, source_target_pairs={{0,24},{1,25},{2,26},{3,27},{4,28},{5,29},{6,30},{7,31},{8,0},{9,1... | collective-permute-start | bytes 2359304 | tf_op jit(solution)/shard_map/ppermute | solution.py:36
  54.1 0.0 collective-permute-done.6.refs_2_.refs_3_
  54.1 0.0 collective-permute-start.24
  54.2 0.0 collective-permute-done.5.refs_1_.refs_0_
  54.2 0.1 shard_map.46
  54.2 10.2 %collective-permute-done.1.refs_0_.refs_4_ = bf16[256,1024]{1,0:T(8,128)(2,1)S(1)} collective-permute-done((bf16[256,1024]{1,0:T(8,128)(2,1)S(1)}, bf16[256,1024]{1,0:T(8,128)(2,1)S(1)}, u32[]{:S(2)}, u32[]{:S(2)}) %collective-permute-start.1) | collective-permute-done | bytes 524320 | tf_op jit(solution)/shard_map/ppermute | solution.py:36
  64.4 0.0 collective-permute-done.4.refs_1_.refs_5_
  64.5 3.5 %collective-permute-start.22 = (bf16[6,256,256]{2,1,0:T(8,128)(2,1)S(1)}, bf16[6,256,256]{2,1,0:T(8,128)(2,1)S(1)}, u32[]{:S(2)}, u32[]{:S(2)}) collective-permute-start(bf16[6,256,256]{2,1,0:T(8,128)(2,1)S(1)} %get-tuple-element.25), channel_id=1, source_target_pairs={{0,3},{1,0},{2,1},{3,2},{4,7},{5,4},{6,5},{7,6},{8,11},{9,8},{10,9... | collective-permute-start | bytes 2359304 | tf_op jit(solution)/shard_map/ppermute | solution.py:36
  68.0 0.0 collective-permute-start.21
  68.0 0.0 collective-permute-start.16
  68.0 10.2 %collective-permute-done.25.refs_4_ = bf16[6,256,256]{2,1,0:T(8,128)(2,1)S(1)} collective-permute-done((bf16[6,256,256]{2,1,0:T(8,128)(2,1)S(1)}, bf16[6,256,256]{2,1,0:T(8,128)(2,1)S(1)}, u32[]{:S(2)}, u32[]{:S(2)}) %collective-permute-start.25) | collective-permute-done | bytes 786464 | tf_op jit(solution)/shard_map/ppermute | solution.py:36
  78.2 0.8 collective-permute-start.7
  78.9 2.4 %collective-permute-done.24.refs_3_ = bf16[6,256,256]{2,1,0:T(8,128)(2,1)S(1)} collective-permute-done((bf16[6,256,256]{2,1,0:T(8,128)(2,1)S(1)}, bf16[6,256,256]{2,1,0:T(8,128)(2,1)S(1)}, u32[]{:S(2)}, u32[]{:S(2)}) %collective-permute-start.24) | collective-permute-done | bytes 786464 | tf_op jit(solution)/shard_map/ppermute | solution.py:36
  81.3 1.0 collective-permute-start.26
  82.3 0.0 collective-permute-done.22.refs_1_
  82.3 2.7 %collective-permute-start.23 = (bf16[6,256,256]{2,1,0:T(8,128)(2,1)S(1)}, bf16[6,256,256]{2,1,0:T(8,128)(2,1)S(1)}, u32[]{:S(2)}, u32[]{:S(2)}) collective-permute-start(bf16[6,256,256]{2,1,0:T(8,128)(2,1)S(1)} %collective-permute-done.22.refs_1_), channel_id=1, source_target_pairs={{0,3},{1,0},{2,1},{3,2},{4,7},{5,4},{6,5},{7,6},{8,11},{9,8},{10,9... | collective-permute-start | bytes 2359304 | tf_op jit(solution)/shard_map/ppermute | solution.py:36
  85.0 5.6 %shard_map.50.refs_6_.refs_8_ = bf16[512,8192]{1,0:T(8,128)(2,1)S(1)} custom-call(s32[8,64]{1,0:T(8,128)S(1)} %copy-done, bf16[1024,8192]{1,0:T(8,128)(2,1)} %v_ref.3), custom_call_target="tpu_custom_call" | custom-call | flops 1000 | bytes 8388608 | tf_op jit(solution)/shard_map/pallas_call | solution.py:107
  90.6 5.6 %shard_map.51.refs_7_.refs_9_ = bf16[512,8192]{1,0:T(8,128)(2,1)S(1)} custom-call(s32[8,64]{1,0:T(8,128)S(1)} %copy-done, bf16[1024,8192]{1,0:T(8,128)(2,1)} %v_ref.3), custom_call_target="tpu_custom_call" | custom-call | flops 1000 | bytes 8388608 | tf_op jit(solution)/shard_map/pallas_call | solution.py:107
  96.1 3.5 %shard_map.52.refs_10_ = f32[1024,1024]{1,0:T(8,128)S(1)} custom-call(bf16[256,1024]{1,0:T(8,128)(2,1)S(1)} %pick.1.refs_0_, bf16[256,1024]{1,0:T(8,128)(2,1)S(1)} %collective-permute-done.2.refs_1_, bf16[256,1024]{1,0:T(8,128)(2,1)S(1)} %collective-permute-done.refs_0_.refs_2_, bf16[256,1024]{1,0:T(8,128)(2,1)S(1)} %collective-permute-done.6.refs_2_.refs_3_, ...), custom_call_target="tpu_custom_call" | custom-call | flops 3221225472 | bytes 6291456 | tf_op jit(solution)/shard_map/pallas_call | solution.py:172
  99.6 0.0 collective-permute-done.21.refs_0_
  99.6 0.3 collective-permute-start.17
  100.0 0.0 collective-permute-done.16.refs_3_
  100.0 1.6 collective-permute-start.8
  101.6 1.1 collective-permute-start.18
  102.7 0.0 collective-permute-start.9
  102.7 4.6 %shard_map.53.refs_8_ = f32[1024,1024]{1,0:T(8,128)S(1)} custom-call(bf16[256,1024]{1,0:T(8,128)(2,1)S(1)} %collective-permute-done.5.refs_1_.refs_0_, bf16[256,1024]{1,0:T(8,128)(2,1)S(1)} %collective-permute-done.3.refs_3_.refs_1_, bf16[256,1024]{1,0:T(8,128)(2,1)S(1)} %collective-permute-done.14.refs_1_.refs_2_, ...), custom_call_target="tpu_custom_call" | custom-call | flops 4294967296 | bytes 8388608 | tf_op jit(solution)/shard_map/pallas_call | solution.py:172
  107.3 0.0 collective-permute-done.23.refs_2_
  107.3 5.1 %shard_map.55 = (f32[1024,256]{1,0:T(8,128)S(1)}, f32[1024,256]{1,0:T(8,128)S(1)}) custom-call(bf16[6,256,256]{2,1,0:T(8,128)(2,1)S(1)} %collective-permute-done.21.refs_0_, bf16[6,256,256]{2,1,0:T(8,128)(2,1)S(1)} %collective-permute-done.22.refs_1_, bf16[6,256,256]{2,1,0:T(8,128)(2,1)S(1)} %collective-permute-done.23.refs_2_, ...), custom_call_target="tpu_custom_call" | custom-call | flops 4831838208 | bytes 18874368 | tf_op jit(solution)/shard_map/pallas_call | solution.py:210
  112.4 11.2 %collective-permute-start.27 = (f32[1024,256]{1,0:T(8,128)S(1)}, f32[1024,256]{1,0:T(8,128)S(1)}, u32[]{:S(2)}, u32[]{:S(2)}) collective-permute-start(f32[1024,256]{1,0:T(8,128)S(1)} %get-tuple-element.28), channel_id=1, source_target_pairs={{0,32},{32,0},{64,96},{96,64},{1,33},{33,1},{65,97},{97,65},{2,34}... | collective-permute-start | bytes 3145736 | tf_op jit(solution)/shard_map/ppermute | solution.py:277
  123.5 0.0 collective-permute-done.9.refs_2_
  123.5 5.1 %shard_map.54 = (f32[1024,256]{1,0:T(8,128)S(1)}, f32[1024,256]{1,0:T(8,128)S(1)}) custom-call(bf16[6,256,256]{2,1,0:T(8,128)(2,1)S(1)} %collective-permute-done.7.refs_0_, bf16[6,256,256]{2,1,0:T(8,128)(2,1)S(1)} %collective-permute-done.8.refs_1_, bf16[6,256,256]{2,1,0:T(8,128)(2,1)S(1)} %collective-permute-done.9.refs_2_, ...), custom_call_target="tpu_custom_call" | custom-call | flops 4831838208 | bytes 18874368 | tf_op jit(solution)/shard_map/pallas_call | solution.py:210
  128.6 1.6 %collective-permute-start.19 = (f32[1024,256]{1,0:T(8,128)S(1)}, f32[1024,256]{1,0:T(8,128)S(1)}, u32[]{:S(2)}, u32[]{:S(2)}) collective-permute-start(f32[1024,256]{1,0:T(8,128)S(1)} %get-tuple-element.24), channel_id=1, source_target_pairs={{0,32},{32,0},{64,96},{96,64},{1,33},{33,1},{65,97},{97,65},{2,34}... | collective-permute-start | bytes 3145736 | tf_op jit(solution)/shard_map/ppermute | solution.py:277
  130.2 0.1 slice_add_fusion
  130.3 3.5 %collective-permute-start.28 = (f32[1024,128]{1,0:T(8,128)S(1)}, f32[1024,128]{1,0:T(8,128)S(1)}, u32[]{:S(2)}, u32[]{:S(2)}) collective-permute-start(f32[1024,128]{1,0:T(8,128)S(1)} %slice_add_fusion), channel_id=1, source_target_pairs={{0,64},{32,96},{64,0},{96,32},{1,65},{33,97},{65,1},{97,33},{2,66}... | collective-permute-start | bytes 1572872 | tf_op jit(solution)/shard_map/ppermute | solution.py:278
  133.8 0.1 slice_add_fusion.1
  133.8 2.2 %collective-permute-start.20 = (f32[1024,128]{1,0:T(8,128)S(1)}, f32[1024,128]{1,0:T(8,128)S(1)}, u32[]{:S(2)}, u32[]{:S(2)}) collective-permute-start(f32[1024,128]{1,0:T(8,128)S(1)} %slice_add_fusion.1), channel_id=1, source_target_pairs={{0,64},{32,96},{64,0},{96,32},{1,65},{33,97},{65,1},{97,33},{2,66}... | collective-permute-start | bytes 1572872 | tf_op jit(solution)/shard_map/ppermute | solution.py:278
  136.0 10.0 %collective-permute-done.28.refs_5_ = f32[1024,128]{1,0:T(8,128)S(1)} collective-permute-done((f32[1024,128]{1,0:T(8,128)S(1)}, f32[1024,128]{1,0:T(8,128)S(1)}, u32[]{:S(2)}, u32[]{:S(2)}) %collective-permute-start.28) | collective-permute-done | bytes 524320 | tf_op jit(solution)/shard_map/ppermute | solution.py:278
  146.0 11.2 %collective-permute-done.20.refs_2_ = f32[1024,128]{1,0:T(8,128)S(1)} collective-permute-done((f32[1024,128]{1,0:T(8,128)S(1)}, f32[1024,128]{1,0:T(8,128)S(1)}, u32[]{:S(2)}, u32[]{:S(2)}) %collective-permute-start.20) | collective-permute-done | bytes 524320 | tf_op jit(solution)/shard_map/ppermute | solution.py:278
  157.3 1.1 finish.1
  (12 shorter events, 0.1 us)
Async XLA Ops:
  0.0 0.7 copy-start.1
  0.7 84.3 %copy-start = (s32[8,64]{1,0:T(8,128)S(1)}, s32[8,64]{1,0:T(8,128)}, u32[]{:S(2)}) copy-start(s32[8,64]{1,0:T(8,128)} %mask_ref.3) | copy-start | bytes 6148
  2.4 14.2 %collective-permute-start.2 = (bf16[256,1024]{1,0:T(8,128)(2,1)S(1)}, bf16[256,1024]{1,0:T(8,128)(2,1)S(1)}, u32[]{:S(2)}, u32[]{:S(2)}) collective-permute-start(bf16[256,1024]{1,0:T(8,128)(2,1)S(1)} %pick.1.refs_0_), channel_id=1, source_target_pairs={{0,4},{1,5},{2,6},{3,7},{4,0},{5,1},{6,2},{7,3},{8,12},{9,13},{10,... | collective-permute-start | bytes 1572872 | tf_op jit(solution)/shard_map/ppermute | solution.py:36
  4.9 17.2 %collective-permute-start = (bf16[256,1024]{1,0:T(8,128)(2,1)S(1)}, bf16[256,1024]{1,0:T(8,128)(2,1)S(1)}, u32[]{:S(2)}, u32[]{:S(2)}) collective-permute-start(bf16[256,1024]{1,0:T(8,128)(2,1)S(1)} %pick.1.refs_0_), channel_id=1, source_target_pairs={{0,8},{1,9},{2,10},{3,11},{4,12},{5,13},{6,14},{7,15},{8,16},{9,17... | collective-permute-start | bytes 1572872 | tf_op jit(solution)/shard_map/ppermute | solution.py:36
  6.1 17.0 %collective-permute-start.10 = (bf16[256,1024]{1,0:T(8,128)(2,1)S(1)}, bf16[256,1024]{1,0:T(8,128)(2,1)S(1)}, u32[]{:S(2)}, u32[]{:S(2)}) collective-permute-start(bf16[256,1024]{1,0:T(8,128)(2,1)S(1)} %pick.1.refs_0_), channel_id=1, source_target_pairs={{0,1},{1,2},{2,3},{3,0},{4,5},{5,6},{6,7},{7,4},{8,9},{9,10},{10,1... | collective-permute-start | bytes 1572872 | tf_op jit(solution)/shard_map/ppermute | solution.py:36
  16.5 12.6 %collective-permute-start.12 = (bf16[256,1024]{1,0:T(8,128)(2,1)S(1)}, bf16[256,1024]{1,0:T(8,128)(2,1)S(1)}, u32[]{:S(2)}, u32[]{:S(2)}) collective-permute-start(bf16[256,1024]{1,0:T(8,128)(2,1)S(1)} %collective-permute-done.2.refs_1_), channel_id=1, source_target_pairs={{0,3},{1,0},{2,1},{3,2},{4,7},{5,4},{6,5},{7,6},{8,11},{9,8},{10,9... | collective-permute-start | bytes 1572872 | tf_op jit(solution)/shard_map/ppermute | solution.py:36
  19.2 21.2 %collective-permute-start.15 = (bf16[256,1024]{1,0:T(8,128)(2,1)S(1)}, bf16[256,1024]{1,0:T(8,128)(2,1)S(1)}, u32[]{:S(2)}, u32[]{:S(2)}) collective-permute-start(bf16[256,1024]{1,0:T(8,128)(2,1)S(1)} %pick.1.refs_0_), channel_id=1, source_target_pairs={{0,3},{1,0},{2,1},{3,2},{4,7},{5,4},{6,5},{7,6},{8,11},{9,8},{10,9... | collective-permute-start | bytes 1572872 | tf_op jit(solution)/shard_map/ppermute | solution.py:36
  19.6 23.2 %collective-permute-start.3 = (bf16[256,1024]{1,0:T(8,128)(2,1)S(1)}, bf16[256,1024]{1,0:T(8,128)(2,1)S(1)}, u32[]{:S(2)}, u32[]{:S(2)}) collective-permute-start(bf16[256,1024]{1,0:T(8,128)(2,1)S(1)} %collective-permute-done.2.refs_1_), channel_id=1, source_target_pairs={{0,24},{1,25},{2,26},{3,27},{4,28},{5,29},{6,30},{7,31},{8,0},{9,1... | collective-permute-start | bytes 1572872 | tf_op jit(solution)/shard_map/ppermute | solution.py:36
  22.1 20.7 %collective-permute-start.14 = (bf16[256,1024]{1,0:T(8,128)(2,1)S(1)}, bf16[256,1024]{1,0:T(8,128)(2,1)S(1)}, u32[]{:S(2)}, u32[]{:S(2)}) collective-permute-start(bf16[256,1024]{1,0:T(8,128)(2,1)S(1)} %collective-permute-done.2.refs_1_), channel_id=1, source_target_pairs={{0,1},{1,2},{2,3},{3,0},{4,5},{5,6},{6,7},{7,4},{8,9},{9,10},{10,1... | collective-permute-start | bytes 1572872 | tf_op jit(solution)/shard_map/ppermute | solution.py:36
  23.1 22.7 %collective-permute-start.11 = (bf16[256,1024]{1,0:T(8,128)(2,1)S(1)}, bf16[256,1024]{1,0:T(8,128)(2,1)S(1)}, u32[]{:S(2)}, u32[]{:S(2)}) collective-permute-start(bf16[256,1024]{1,0:T(8,128)(2,1)S(1)} %collective-permute-done.10.refs_0_.refs_4_), channel_id=1, source_target_pairs={{0,1},{1,2},{2,3},{3,0},{4,5},{5,6},{6,7},{7,4},{8,9},{9,10},{10,1... | collective-permute-start | bytes 1572872 | tf_op jit(solution)/shard_map/ppermute | solution.py:36
  29.1 22.5 %collective-permute-start.13 = (bf16[256,1024]{1,0:T(8,128)(2,1)S(1)}, bf16[256,1024]{1,0:T(8,128)(2,1)S(1)}, u32[]{:S(2)}, u32[]{:S(2)}) collective-permute-start(bf16[256,1024]{1,0:T(8,128)(2,1)S(1)} %collective-permute-done.12.refs_3_), channel_id=1, source_target_pairs={{0,3},{1,0},{2,1},{3,2},{4,7},{5,4},{6,5},{7,6},{8,11},{9,8},{10,9... | collective-permute-start | bytes 1572872 | tf_op jit(solution)/shard_map/ppermute | solution.py:36
  40.3 13.8 %collective-permute-start.6 = (bf16[256,1024]{1,0:T(8,128)(2,1)S(1)}, bf16[256,1024]{1,0:T(8,128)(2,1)S(1)}, u32[]{:S(2)}, u32[]{:S(2)}) collective-permute-start(bf16[256,1024]{1,0:T(8,128)(2,1)S(1)} %pick.1.refs_0_), channel_id=1, source_target_pairs={{0,24},{1,25},{2,26},{3,27},{4,28},{5,29},{6,30},{7,31},{8,0},{9,1... | collective-permute-start | bytes 1572872 | tf_op jit(solution)/shard_map/ppermute | solution.py:36
  42.8 11.3 %collective-permute-start.5 = (bf16[256,1024]{1,0:T(8,128)(2,1)S(1)}, bf16[256,1024]{1,0:T(8,128)(2,1)S(1)}, u32[]{:S(2)}, u32[]{:S(2)}) collective-permute-start(bf16[256,1024]{1,0:T(8,128)(2,1)S(1)} %collective-permute-done.2.refs_1_), channel_id=1, source_target_pairs={{0,8},{1,9},{2,10},{3,11},{4,12},{5,13},{6,14},{7,15},{8,16},{9,17... | collective-permute-start | bytes 1572872 | tf_op jit(solution)/shard_map/ppermute | solution.py:36
  42.8 21.6 %collective-permute-start.1 = (bf16[256,1024]{1,0:T(8,128)(2,1)S(1)}, bf16[256,1024]{1,0:T(8,128)(2,1)S(1)}, u32[]{:S(2)}, u32[]{:S(2)}) collective-permute-start(bf16[256,1024]{1,0:T(8,128)(2,1)S(1)} %collective-permute-done.refs_0_.refs_2_), channel_id=1, source_target_pairs={{0,8},{1,9},{2,10},{3,11},{4,12},{5,13},{6,14},{7,15},{8,16},{9,17... | collective-permute-start | bytes 1572872 | tf_op jit(solution)/shard_map/ppermute | solution.py:36
  45.8 18.6 %collective-permute-start.4 = (bf16[256,1024]{1,0:T(8,128)(2,1)S(1)}, bf16[256,1024]{1,0:T(8,128)(2,1)S(1)}, u32[]{:S(2)}, u32[]{:S(2)}) collective-permute-start(bf16[256,1024]{1,0:T(8,128)(2,1)S(1)} %collective-permute-done.3.refs_3_.refs_1_), channel_id=1, source_target_pairs={{0,24},{1,25},{2,26},{3,27},{4,28},{5,29},{6,30},{7,31},{8,0},{9,1... | collective-permute-start | bytes 1572872 | tf_op jit(solution)/shard_map/ppermute | solution.py:36
  51.6 26.6 %collective-permute-start.25 = (bf16[6,256,256]{2,1,0:T(8,128)(2,1)S(1)}, bf16[6,256,256]{2,1,0:T(8,128)(2,1)S(1)}, u32[]{:S(2)}, u32[]{:S(2)}) collective-permute-start(bf16[6,256,256]{2,1,0:T(8,128)(2,1)S(1)} %get-tuple-element.26), channel_id=1, source_target_pairs={{0,24},{1,25},{2,26},{3,27},{4,28},{5,29},{6,30},{7,31},{8,0},{9,1... | collective-permute-start | bytes 2359304 | tf_op jit(solution)/shard_map/ppermute | solution.py:36
  54.1 27.1 %collective-permute-start.24 = (bf16[6,256,256]{2,1,0:T(8,128)(2,1)S(1)}, bf16[6,256,256]{2,1,0:T(8,128)(2,1)S(1)}, u32[]{:S(2)}, u32[]{:S(2)}) collective-permute-start(bf16[6,256,256]{2,1,0:T(8,128)(2,1)S(1)} %get-tuple-element.26), channel_id=1, source_target_pairs={{0,8},{1,9},{2,10},{3,11},{4,12},{5,13},{6,14},{7,15},{8,16},{9,17... | collective-permute-start | bytes 2359304 | tf_op jit(solution)/shard_map/ppermute | solution.py:36
  64.5 17.9 %collective-permute-start.22 = (bf16[6,256,256]{2,1,0:T(8,128)(2,1)S(1)}, bf16[6,256,256]{2,1,0:T(8,128)(2,1)S(1)}, u32[]{:S(2)}, u32[]{:S(2)}) collective-permute-start(bf16[6,256,256]{2,1,0:T(8,128)(2,1)S(1)} %get-tuple-element.25), channel_id=1, source_target_pairs={{0,3},{1,0},{2,1},{3,2},{4,7},{5,4},{6,5},{7,6},{8,11},{9,8},{10,9... | collective-permute-start | bytes 2359304 | tf_op jit(solution)/shard_map/ppermute | solution.py:36
  68.0 31.7 %collective-permute-start.21 = (bf16[6,256,256]{2,1,0:T(8,128)(2,1)S(1)}, bf16[6,256,256]{2,1,0:T(8,128)(2,1)S(1)}, u32[]{:S(2)}, u32[]{:S(2)}) collective-permute-start(bf16[6,256,256]{2,1,0:T(8,128)(2,1)S(1)} %get-tuple-element.25), channel_id=1, source_target_pairs={{0,1},{1,2},{2,3},{3,0},{4,5},{5,6},{6,7},{7,4},{8,9},{9,10},{10,1... | collective-permute-start | bytes 2359304 | tf_op jit(solution)/shard_map/ppermute | solution.py:36
  68.0 32.0 %collective-permute-start.16 = (bf16[6,256,256]{2,1,0:T(8,128)(2,1)S(1)}, bf16[6,256,256]{2,1,0:T(8,128)(2,1)S(1)}, u32[]{:S(2)}, u32[]{:S(2)}) collective-permute-start(bf16[6,256,256]{2,1,0:T(8,128)(2,1)S(1)} %get-tuple-element.22), channel_id=1, source_target_pairs={{0,8},{1,9},{2,10},{3,11},{4,12},{5,13},{6,14},{7,15},{8,16},{9,17... | collective-permute-start | bytes 2359304 | tf_op jit(solution)/shard_map/ppermute | solution.py:36
  78.2 23.4 %collective-permute-start.7 = (bf16[6,256,256]{2,1,0:T(8,128)(2,1)S(1)}, bf16[6,256,256]{2,1,0:T(8,128)(2,1)S(1)}, u32[]{:S(2)}, u32[]{:S(2)}) collective-permute-start(bf16[6,256,256]{2,1,0:T(8,128)(2,1)S(1)} %get-tuple-element.19), channel_id=1, source_target_pairs={{0,1},{1,2},{2,3},{3,0},{4,5},{5,6},{6,7},{7,4},{8,9},{9,10},{10,1... | collective-permute-start | bytes 2359304 | tf_op jit(solution)/shard_map/ppermute | solution.py:36
  81.3 21.4 %collective-permute-start.26 = (bf16[6,256,256]{2,1,0:T(8,128)(2,1)S(1)}, bf16[6,256,256]{2,1,0:T(8,128)(2,1)S(1)}, u32[]{:S(2)}, u32[]{:S(2)}) collective-permute-start(bf16[6,256,256]{2,1,0:T(8,128)(2,1)S(1)} %collective-permute-done.25.refs_4_), channel_id=1, source_target_pairs={{0,24},{1,25},{2,26},{3,27},{4,28},{5,29},{6,30},{7,31},{8,0},{9,1... | collective-permute-start | bytes 2359304 | tf_op jit(solution)/shard_map/ppermute | solution.py:36
  82.3 24.9 %collective-permute-start.23 = (bf16[6,256,256]{2,1,0:T(8,128)(2,1)S(1)}, bf16[6,256,256]{2,1,0:T(8,128)(2,1)S(1)}, u32[]{:S(2)}, u32[]{:S(2)}) collective-permute-start(bf16[6,256,256]{2,1,0:T(8,128)(2,1)S(1)} %collective-permute-done.22.refs_1_), channel_id=1, source_target_pairs={{0,3},{1,0},{2,1},{3,2},{4,7},{5,4},{6,5},{7,6},{8,11},{9,8},{10,9... | collective-permute-start | bytes 2359304 | tf_op jit(solution)/shard_map/ppermute | solution.py:36
  99.6 23.9 %collective-permute-start.17 = (bf16[6,256,256]{2,1,0:T(8,128)(2,1)S(1)}, bf16[6,256,256]{2,1,0:T(8,128)(2,1)S(1)}, u32[]{:S(2)}, u32[]{:S(2)}) collective-permute-start(bf16[6,256,256]{2,1,0:T(8,128)(2,1)S(1)} %get-tuple-element.22), channel_id=1, source_target_pairs={{0,24},{1,25},{2,26},{3,27},{4,28},{5,29},{6,30},{7,31},{8,0},{9,1... | collective-permute-start | bytes 2359304 | tf_op jit(solution)/shard_map/ppermute | solution.py:36
  100.0 23.6 %collective-permute-start.8 = (bf16[6,256,256]{2,1,0:T(8,128)(2,1)S(1)}, bf16[6,256,256]{2,1,0:T(8,128)(2,1)S(1)}, u32[]{:S(2)}, u32[]{:S(2)}) collective-permute-start(bf16[6,256,256]{2,1,0:T(8,128)(2,1)S(1)} %get-tuple-element.19), channel_id=1, source_target_pairs={{0,3},{1,0},{2,1},{3,2},{4,7},{5,4},{6,5},{7,6},{8,11},{9,8},{10,9... | collective-permute-start | bytes 2359304 | tf_op jit(solution)/shard_map/ppermute | solution.py:36
  101.6 22.0 %collective-permute-start.18 = (bf16[6,256,256]{2,1,0:T(8,128)(2,1)S(1)}, bf16[6,256,256]{2,1,0:T(8,128)(2,1)S(1)}, u32[]{:S(2)}, u32[]{:S(2)}) collective-permute-start(bf16[6,256,256]{2,1,0:T(8,128)(2,1)S(1)} %collective-permute-done.16.refs_3_), channel_id=1, source_target_pairs={{0,8},{1,9},{2,10},{3,11},{4,12},{5,13},{6,14},{7,15},{8,16},{9,17... | collective-permute-start | bytes 2359304 | tf_op jit(solution)/shard_map/ppermute | solution.py:36
  102.7 20.9 %collective-permute-start.9 = (bf16[6,256,256]{2,1,0:T(8,128)(2,1)S(1)}, bf16[6,256,256]{2,1,0:T(8,128)(2,1)S(1)}, u32[]{:S(2)}, u32[]{:S(2)}) collective-permute-start(bf16[6,256,256]{2,1,0:T(8,128)(2,1)S(1)} %collective-permute-done.7.refs_0_), channel_id=1, source_target_pairs={{0,1},{1,2},{2,3},{3,0},{4,5},{5,6},{6,7},{7,4},{8,9},{9,10},{10,1... | collective-permute-start | bytes 2359304 | tf_op jit(solution)/shard_map/ppermute | solution.py:36
  112.4 17.9 %collective-permute-start.27 = (f32[1024,256]{1,0:T(8,128)S(1)}, f32[1024,256]{1,0:T(8,128)S(1)}, u32[]{:S(2)}, u32[]{:S(2)}) collective-permute-start(f32[1024,256]{1,0:T(8,128)S(1)} %get-tuple-element.28), channel_id=1, source_target_pairs={{0,32},{32,0},{64,96},{96,64},{1,33},{33,1},{65,97},{97,65},{2,34}... | collective-permute-start | bytes 3145736 | tf_op jit(solution)/shard_map/ppermute | solution.py:277
  128.6 5.1 %collective-permute-start.19 = (f32[1024,256]{1,0:T(8,128)S(1)}, f32[1024,256]{1,0:T(8,128)S(1)}, u32[]{:S(2)}, u32[]{:S(2)}) collective-permute-start(f32[1024,256]{1,0:T(8,128)S(1)} %get-tuple-element.24), channel_id=1, source_target_pairs={{0,32},{32,0},{64,96},{96,64},{1,33},{33,1},{65,97},{97,65},{2,34}... | collective-permute-start | bytes 3145736 | tf_op jit(solution)/shard_map/ppermute | solution.py:277
  130.3 15.7 %collective-permute-start.28 = (f32[1024,128]{1,0:T(8,128)S(1)}, f32[1024,128]{1,0:T(8,128)S(1)}, u32[]{:S(2)}, u32[]{:S(2)}) collective-permute-start(f32[1024,128]{1,0:T(8,128)S(1)} %slice_add_fusion), channel_id=1, source_target_pairs={{0,64},{32,96},{64,0},{96,32},{1,65},{33,97},{65,1},{97,33},{2,66}... | collective-permute-start | bytes 1572872 | tf_op jit(solution)/shard_map/ppermute | solution.py:278
  133.8 23.4 %collective-permute-start.20 = (f32[1024,128]{1,0:T(8,128)S(1)}, f32[1024,128]{1,0:T(8,128)S(1)}, u32[]{:S(2)}, u32[]{:S(2)}) collective-permute-start(f32[1024,128]{1,0:T(8,128)S(1)} %slice_add_fusion.1), channel_id=1, source_target_pairs={{0,64},{32,96},{64,0},{96,32},{1,65},{33,97},{65,1},{97,33},{2,66}... | collective-permute-start | bytes 1572872 | tf_op jit(solution)/shard_map/ppermute | solution.py:278

commit v2 on v1

--- a/solution.py
+++ b/solution.py
@@ -16,6 +16,7 @@
 
 LIMIT = 6 << 20
 LINE = (-1, 1, 2)
+TAIL = 64
 
 
 def blk(x, z, y):
@@ -52,7 +53,7 @@
     g = lax.axis_index("grp")
 
     def copy(k):
-        owner = g ^ (2 * (k & 1) + (k >> 2))
+        owner = g ^ (2 * (k & 1) + 1 - (k >> 2))
         at = batches[2 * owner + ((k >> 1) & 1)]
         src = amp_ref.at[:, pl.ds(pl.multiple_of(at * BATCH, BATCH), BATCH)]
         return pltpu.make_async_copy(src, out_ref.at[:, pl.ds(k * BATCH, BATCH)], sems.at[k])
@@ -181,50 +182,77 @@
     )(*parts, *v, *before)
 
 
-def group_kernel(index, *refs):
-    ys, xs, (top, bottom, acc_ref, mine, theirs) = refs[:3], refs[3:6], refs[6:]
-    cols, rows = mine.shape[1], top.shape[0]
+def group_kernel(base, turned, *refs):
+    parts, (top, bottom, acc_ref, out) = refs[:3], refs[3:]
+    cols, rows = out.shape[1], top.shape[0]
     for k, v_ref in enumerate((top, bottom)):
         at = slice(k * rows, (k + 1) * rows)
         first = True
-        for j, dy in enumerate(LINE):
-            for i, dx in enumerate(LINE):
+        for j, far in enumerate(LINE):
+            for i, near in enumerate(LINE):
                 for dz in (0, 1):
-                    tile = v_ref[:, column((dx, dz, dy))]
-                    for out, part, slot, base in (
-                        (mine, ys[j], 2 * i + dz, index),
-                        (theirs, xs[i], 2 * j + dz, 2 + index),
-                    ):
-                        product = dot(tile, part[slot])
-                        if first:
-                            out[at, :] = acc_ref[at, base * cols : (base + 1) * cols] + product
-                        else:
-                            out[at, :] += product
+                    offset = (far, dz, near) if turned else (near, dz, far)
+                    product = dot(v_ref[:, column(offset)], parts[j][2 * i + dz])
+                    if first:
+                        out[at, :] = acc_ref[at, base * cols : (base + 1) * cols] + product
+                    else:
+                        out[at, :] += product
                     first = False
 
 
-def group(index, ys, xs, v, acc):
+def group(base, turned, parts, v, acc):
     rows = 2 * v[0].shape[0]
-    cols = ys[0].shape[2]
-    out = jax.ShapeDtypeStruct((rows, cols), F32)
-    return pl.pallas_call(
-        functools.partial(group_kernel, index),
-        out_shape=(out, out),
-        in_specs=vmem(9),
-        out_specs=vmem(2),
+    cols = parts[0].shape[2]
+    return pl.pallas_call(
+        functools.partial(group_kernel, base, turned),
+        out_shape=jax.ShapeDtypeStruct((rows, cols), F32),
+        in_specs=vmem(6),
+        out_specs=pl.BlockSpec(memory_space=pltpu.VMEM),
         cost_estimate=pl.CostEstimate(
-            flops=2 * rows * 18 * 256 * 512, bytes_accessed=18 << 20, transcendentals=0
+            flops=2 * rows * 18 * 256 * 256, bytes_accessed=18 << 19, transcendentals=0
         ),
         compiler_params=params(),
-    )(*ys, *xs, *v, acc)
+    )(*parts, *v, acc)
+
+
+def code_kernel(mine, got, out_ref):
+    rows = mine.shape[0]
+    powers = []
+    for r in range(rows // BLOCK):
+        at = slice(r * BLOCK, (r + 1) * BLOCK)
+        total = mine[at, BATCH:] + got[at, BATCH:]
+        peak = jnp.maximum(jnp.max(jnp.abs(total), axis=0, keepdims=True), 1e-30)
+        power = jnp.floor(jnp.log2(peak * 1.0001)) - 14.0
+        scaled = jnp.clip(jnp.round(total * jnp.exp2(-power)), -32767.0, 32767.0)
+        out_ref[at, :] = scaled.astype(jnp.int32).astype(jnp.int16)
+        powers.append(jnp.broadcast_to(power, (TAIL // 8, BATCH)))
+    out_ref[rows:, :] = jnp.concatenate(powers, axis=0).astype(jnp.int32).astype(jnp.int16)
+
+
+def code(mine, got):
+    return pl.pallas_call(
+        code_kernel,
+        out_shape=jax.ShapeDtypeStruct((mine.shape[0] + TAIL, BATCH), jnp.int16),
+        in_specs=vmem(2),
+        out_specs=pl.BlockSpec(memory_space=pltpu.VMEM),
+        cost_estimate=pl.CostEstimate(flops=1000, bytes_accessed=1 << 20, transcendentals=0),
+        compiler_params=params(),
+        name="code",
+    )(mine, got)
 
 
 def finish_kernel(*refs):
     out_ref = refs[-1]
     for k in range(2):
         mine, got, far = refs[3 * k : 3 * k + 3]
-        total = mine[:, :BATCH] + got[:, :BATCH] + far[...]
-        out_ref[k * BATCH : (k + 1) * BATCH, :] = total.T.astype(BF16)
+        rows = mine.shape[0]
+        powers = far[rows:, :].astype(jnp.int32).astype(F32)
+        for r in range(rows // BLOCK):
+            at = slice(r * BLOCK, (r + 1) * BLOCK)
+            scale = jnp.exp2(powers[r * (TAIL // 8) : r * (TAIL // 8) + 1])
+            other = far[at, :].astype(jnp.int32).astype(F32) * scale
+            total = mine[at, :BATCH] + got[at, :BATCH] + other
+            out_ref[k * BATCH : (k + 1) * BATCH, at] = total.T.astype(BF16)
 
 
 def finish(parts):
@@ -273,9 +301,12 @@
 
     parts = []
     for k in range(2):
-        mine, theirs = group(k, *pieces[k], v, acc)
+        ys, xs = pieces[k]
+        theirs = group(k, False, ys, v, acc)
         got = lax.ppermute(theirs, "grp", CORE)
-        far = lax.ppermute(mine[:, BATCH:] + got[:, BATCH:], "grp", ZHI)
+        mine = group(2 + k, True, xs, v, acc)
+        packed = code(mine, got)
+        far = lax.ppermute(packed, "grp", ZHI)
         parts += [mine, got, far]
     return finish(parts)
 

time: 159 us -> 171 us (1.075)
  the two profiles are of different devices: /device:TPU:1 before, /device:TPU:0 now
where the time goes in v2:
time: 171 us
  waiting for transfers between devices  91.2 us (53%)
  starting transfers between devices  45.9 us (27%)
  Pallas kernels  32.9 us (19%)
    ppermute x25, waiting for transfers between devices, send(): return lax.ppermute(array, 'blk', pairs)  83.1 us
    ppermute x25, starting transfers between devices, send(): return lax.ppermute(array, 'blk', pairs)  41.6 us
    pallas_call x2, Pallas kernels, keep(): pl.pallas_call(functools.partial(keep_kernel, first), out_shape=jax.Shape...  11.1 us
    pallas_call x4, Pallas kernels, group(): pl.pallas_call(functools.partial(group_kernel, base, turned), out_shape=j...  10.4 us
    pallas_call x2, Pallas kernels, cross(): pl.pallas_call(functools.partial(cross_kernel, offsets), out_shape=jax.Sh...  8.04 us
    ppermute x2, waiting for transfers between devices, on_device(): far = lax.ppermute(packed, 'grp', ZHI)  8.03 us
    ppermute x2, starting transfers between devices, on_device(): far = lax.ppermute(packed, 'grp', ZHI)  3.86 us
  transfers between devices with their start and end apart: 29, of which 16 were waited for; matrix products, arithmetic and copies ran while one was open for 0% of the time, Pallas kernels for 18%

profile of v2, /device:TPU:0, one launch (start us, length us, event | category | flops | bytes accessed | tf_op | source)
XLA Modules:
  0.0 170.9 jit_solution(9641371090465534383)
XLA Ops:
  0.0 0.7 copy-done.1
  0.7 1.7 pick.1.refs_0_
  2.4 2.1 %collective-permute-start.2 = (bf16[256,1024]{1,0:T(8,128)(2,1)S(1)}, bf16[256,1024]{1,0:T(8,128)(2,1)S(1)}, u32[]{:S(2)}, u32[]{:S(2)}) collective-permute-start(bf16[256,1024]{1,0:T(8,128)(2,1)S(1)} %pick.1.refs_0_), channel_id=1, source_target_pairs={{0,4},{1,5},{2,6},{3,7},{4,0},{5,1},{6,2},{7,3},{8,12},{9,13},{10,... | collective-permute-start | bytes 1572872 | tf_op jit(solution)/shard_map/ppermute | solution.py:37
  4.5 1.6 collective-permute-start
  6.1 1.5 collective-permute-start.12
  7.5 8.9 %collective-permute-done.2.refs_1_ = bf16[256,1024]{1,0:T(8,128)(2,1)S(1)} collective-permute-done((bf16[256,1024]{1,0:T(8,128)(2,1)S(1)}, bf16[256,1024]{1,0:T(8,128)(2,1)S(1)}, u32[]{:S(2)}, u32[]{:S(2)}) %collective-permute-start.2) | collective-permute-done | bytes 524320 | tf_op jit(solution)/shard_map/ppermute | solution.py:37
  16.4 2.8 %collective-permute-start.11 = (bf16[256,1024]{1,0:T(8,128)(2,1)S(1)}, bf16[256,1024]{1,0:T(8,128)(2,1)S(1)}, u32[]{:S(2)}, u32[]{:S(2)}) collective-permute-start(bf16[256,1024]{1,0:T(8,128)(2,1)S(1)} %collective-permute-done.2.refs_1_), channel_id=1, source_target_pairs={{0,24},{1,25},{2,26},{3,27},{4,28},{5,29},{6,30},{7,31},{8,0},{9,1... | collective-permute-start | bytes 1572872 | tf_op jit(solution)/shard_map/ppermute | solution.py:37
  19.2 0.8 collective-permute-start.15
  20.0 3.0 %collective-permute-start.3 = (bf16[256,1024]{1,0:T(8,128)(2,1)S(1)}, bf16[256,1024]{1,0:T(8,128)(2,1)S(1)}, u32[]{:S(2)}, u32[]{:S(2)}) collective-permute-start(bf16[256,1024]{1,0:T(8,128)(2,1)S(1)} %collective-permute-done.2.refs_1_), channel_id=1, source_target_pairs={{0,3},{1,0},{2,1},{3,2},{4,7},{5,4},{6,5},{7,6},{8,11},{9,8},{10,9... | collective-permute-start | bytes 1572872 | tf_op jit(solution)/shard_map/ppermute | solution.py:37
  23.0 0.0 collective-permute-done.refs_0_.refs_4_
  23.0 1.2 collective-permute-start.10
  24.2 0.0 collective-permute-done.12.refs_2_.refs_0_
  24.2 0.1 collective-permute-start.13
  24.3 7.2 %collective-permute-done.11.refs_1_.refs_3_ = bf16[256,1024]{1,0:T(8,128)(2,1)S(1)} collective-permute-done((bf16[256,1024]{1,0:T(8,128)(2,1)S(1)}, bf16[256,1024]{1,0:T(8,128)(2,1)S(1)}, u32[]{:S(2)}, u32[]{:S(2)}) %collective-permute-start.11) | collective-permute-done | bytes 524320 | tf_op jit(solution)/shard_map/ppermute | solution.py:37
  31.5 3.7 %collective-permute-start.14 = (bf16[256,1024]{1,0:T(8,128)(2,1)S(1)}, bf16[256,1024]{1,0:T(8,128)(2,1)S(1)}, u32[]{:S(2)}, u32[]{:S(2)}) collective-permute-start(bf16[256,1024]{1,0:T(8,128)(2,1)S(1)} %collective-permute-done.11.refs_1_.refs_3_), channel_id=1, source_target_pairs={{0,24},{1,25},{2,26},{3,27},{4,28},{5,29},{6,30},{7,31},{8,0},{9,1... | collective-permute-start | bytes 1572872 | tf_op jit(solution)/shard_map/ppermute | solution.py:37
  35.2 7.5 %collective-permute-done.15.refs_3_.refs_2_ = bf16[256,1024]{1,0:T(8,128)(2,1)S(1)} collective-permute-done((bf16[256,1024]{1,0:T(8,128)(2,1)S(1)}, bf16[256,1024]{1,0:T(8,128)(2,1)S(1)}, u32[]{:S(2)}, u32[]{:S(2)}) %collective-permute-start.15) | collective-permute-done | bytes 524320 | tf_op jit(solution)/shard_map/ppermute | solution.py:37
  42.7 3.0 %collective-permute-start.6 = (bf16[256,1024]{1,0:T(8,128)(2,1)S(1)}, bf16[256,1024]{1,0:T(8,128)(2,1)S(1)}, u32[]{:S(2)}, u32[]{:S(2)}) collective-permute-start(bf16[256,1024]{1,0:T(8,128)(2,1)S(1)} %pick.1.refs_0_), channel_id=1, source_target_pairs={{0,3},{1,0},{2,1},{3,2},{4,7},{5,4},{6,5},{7,6},{8,11},{9,8},{10,9... | collective-permute-start | bytes 1572872 | tf_op jit(solution)/shard_map/ppermute | solution.py:37
  45.7 0.0 collective-permute-done.3.refs_3_
  45.7 0.0 collective-permute-start.5
  45.7 0.6 collective-permute-start.1
  46.3 1.3 collective-permute-done.13.refs_4_.refs_0_
  47.6 1.4 collective-permute-start.4
  49.0 0.1 shard_map.53
  49.1 3.0 %collective-permute-done.14.refs_5_.refs_1_ = bf16[256,1024]{1,0:T(8,128)(2,1)S(1)} collective-permute-done((bf16[256,1024]{1,0:T(8,128)(2,1)S(1)}, bf16[256,1024]{1,0:T(8,128)(2,1)S(1)}, u32[]{:S(2)}, u32[]{:S(2)}) %collective-permute-start.14) | collective-permute-done | bytes 524320 | tf_op jit(solution)/shard_map/ppermute | solution.py:37
  52.2 3.1 %collective-permute-start.25 = (bf16[6,256,256]{2,1,0:T(8,128)(2,1)S(1)}, bf16[6,256,256]{2,1,0:T(8,128)(2,1)S(1)}, u32[]{:S(2)}, u32[]{:S(2)}) collective-permute-start(bf16[6,256,256]{2,1,0:T(8,128)(2,1)S(1)} %get-tuple-element.20), channel_id=1, source_target_pairs={{0,3},{1,0},{2,1},{3,2},{4,7},{5,4},{6,5},{7,6},{8,11},{9,8},{10,9... | collective-permute-start | bytes 2359304 | tf_op jit(solution)/shard_map/ppermute | solution.py:37
  55.3 2.8 %collective-permute-done.6.refs_2_.refs_5_ = bf16[256,1024]{1,0:T(8,128)(2,1)S(1)} collective-permute-done((bf16[256,1024]{1,0:T(8,128)(2,1)S(1)}, bf16[256,1024]{1,0:T(8,128)(2,1)S(1)}, u32[]{:S(2)}, u32[]{:S(2)}) %collective-permute-start.6) | collective-permute-done | bytes 524320 | tf_op jit(solution)/shard_map/ppermute | solution.py:37
  58.0 1.0 collective-permute-start.16
  59.1 2.7 %collective-permute-done.5.refs_1_.refs_2_ = bf16[256,1024]{1,0:T(8,128)(2,1)S(1)} collective-permute-done((bf16[256,1024]{1,0:T(8,128)(2,1)S(1)}, bf16[256,1024]{1,0:T(8,128)(2,1)S(1)}, u32[]{:S(2)}, u32[]{:S(2)}) %collective-permute-start.5) | collective-permute-done | bytes 524320 | tf_op jit(solution)/shard_map/ppermute | solution.py:37
  61.7 0.1 shard_map.46
  61.8 0.1 collective-permute-start.24
  61.9 11.1 %collective-permute-done.1.refs_0_.refs_6_ = bf16[256,1024]{1,0:T(8,128)(2,1)S(1)} collective-permute-done((bf16[256,1024]{1,0:T(8,128)(2,1)S(1)}, bf16[256,1024]{1,0:T(8,128)(2,1)S(1)}, u32[]{:S(2)}, u32[]{:S(2)}) %collective-permute-start.1) | collective-permute-done | bytes 524320 | tf_op jit(solution)/shard_map/ppermute | solution.py:37
  73.0 0.0 collective-permute-done.4.refs_1_.refs_7_
  73.0 3.8 %collective-permute-start.22 = (bf16[6,256,256]{2,1,0:T(8,128)(2,1)S(1)}, bf16[6,256,256]{2,1,0:T(8,128)(2,1)S(1)}, u32[]{:S(2)}, u32[]{:S(2)}) collective-permute-start(bf16[6,256,256]{2,1,0:T(8,128)(2,1)S(1)} %get-tuple-element.19), channel_id=1, source_target_pairs={{0,24},{1,25},{2,26},{3,27},{4,28},{5,29},{6,30},{7,31},{8,0},{9,1... | collective-permute-start | bytes 2359304 | tf_op jit(solution)/shard_map/ppermute | solution.py:37
  76.8 5.6 %collective-permute-done.25.refs_1_ = bf16[6,256,256]{2,1,0:T(8,128)(2,1)S(1)} collective-permute-done((bf16[6,256,256]{2,1,0:T(8,128)(2,1)S(1)}, bf16[6,256,256]{2,1,0:T(8,128)(2,1)S(1)}, u32[]{:S(2)}, u32[]{:S(2)}) %collective-permute-start.25) | collective-permute-done | bytes 786464 | tf_op jit(solution)/shard_map/ppermute | solution.py:37
  82.3 3.5 %collective-permute-start.26 = (bf16[6,256,256]{2,1,0:T(8,128)(2,1)S(1)}, bf16[6,256,256]{2,1,0:T(8,128)(2,1)S(1)}, u32[]{:S(2)}, u32[]{:S(2)}) collective-permute-start(bf16[6,256,256]{2,1,0:T(8,128)(2,1)S(1)} %collective-permute-done.25.refs_1_), channel_id=1, source_target_pairs={{0,3},{1,0},{2,1},{3,2},{4,7},{5,4},{6,5},{7,6},{8,11},{9,8},{10,9... | collective-permute-start | bytes 2359304 | tf_op jit(solution)/shard_map/ppermute | solution.py:37
  85.9 5.6 %shard_map.48.refs_6_.refs_8_.refs_3_ = bf16[512,8192]{1,0:T(8,128)(2,1)S(1)} custom-call(s32[8,64]{1,0:T(8,128)S(1)} %copy-done, bf16[1024,8192]{1,0:T(8,128)(2,1)} %v_ref.3), custom_call_target="tpu_custom_call" | custom-call | flops 1000 | bytes 8388608 | tf_op jit(solution)/shard_map/pallas_call | solution.py:108
  91.5 5.6 %shard_map.49.refs_7_.refs_9_.refs_4_ = bf16[512,8192]{1,0:T(8,128)(2,1)S(1)} custom-call(s32[8,64]{1,0:T(8,128)S(1)} %copy-done, bf16[1024,8192]{1,0:T(8,128)(2,1)} %v_ref.3), custom_call_target="tpu_custom_call" | custom-call | flops 1000 | bytes 8388608 | tf_op jit(solution)/shard_map/pallas_call | solution.py:108
  97.1 0.1 collective-permute-start.17
  97.2 2.0 %collective-permute-start.18 = (bf16[6,256,256]{2,1,0:T(8,128)(2,1)S(1)}, bf16[6,256,256]{2,1,0:T(8,128)(2,1)S(1)}, u32[]{:S(2)}, u32[]{:S(2)}) collective-permute-start(bf16[6,256,256]{2,1,0:T(8,128)(2,1)S(1)} %collective-permute-done.16.refs_0_), channel_id=1, source_target_pairs={{0,1},{1,2},{2,3},{3,0},{4,5},{5,6},{6,7},{7,4},{8,9},{9,10},{10,1... | collective-permute-start | bytes 2359304 | tf_op jit(solution)/shard_map/ppermute | solution.py:37
  99.2 3.5 %shard_map.50.refs_10_ = f32[1024,1024]{1,0:T(8,128)S(1)} custom-call(bf16[256,1024]{1,0:T(8,128)(2,1)S(1)} %pick.1.refs_0_, bf16[256,1024]{1,0:T(8,128)(2,1)S(1)} %collective-permute-done.2.refs_1_, bf16[256,1024]{1,0:T(8,128)(2,1)S(1)} %collective-permute-done.12.refs_2_.refs_0_, bf16[256,1024]{1,0:T(8,128)(2,1)S(1)} %collective-permute-done.15.refs_3_.refs_2_, ...), custom_call_target="tpu_custom_call" | custom-call | flops 3221225472 | bytes 6291456 | tf_op jit(solution)/shard_map/pallas_call | solution.py:173
  102.6 4.0 %collective-permute-done.24.refs_0_ = bf16[6,256,256]{2,1,0:T(8,128)(2,1)S(1)} collective-permute-done((bf16[6,256,256]{2,1,0:T(8,128)(2,1)S(1)}, bf16[6,256,256]{2,1,0:T(8,128)(2,1)S(1)}, u32[]{:S(2)}, u32[]{:S(2)}) %collective-permute-start.24) | collective-permute-done | bytes 786464 | tf_op jit(solution)/shard_map/ppermute | solution.py:37
  106.7 1.2 collective-permute-start.21
  107.9 1.5 collective-permute-start.7
  109.4 4.6 %shard_map.51.refs_5_ = f32[1024,1024]{1,0:T(8,128)S(1)} custom-call(bf16[256,1024]{1,0:T(8,128)(2,1)S(1)} %collective-permute-done.10.refs_0_.refs_1_, bf16[256,1024]{1,0:T(8,128)(2,1)S(1)} %collective-permute-done.11.refs_1_.refs_3_, bf16[256,1024]{1,0:T(8,128)(2,1)S(1)} %collective-permute-done.5.refs_1_.refs_2_, ...), custom_call_target="tpu_custom_call" | custom-call | flops 4294967296 | bytes 8388608 | tf_op jit(solution)/shard_map/pallas_call | solution.py:173
  114.0 1.8 %collective-permute-start.23 = (bf16[6,256,256]{2,1,0:T(8,128)(2,1)S(1)}, bf16[6,256,256]{2,1,0:T(8,128)(2,1)S(1)}, u32[]{:S(2)}, u32[]{:S(2)}) collective-permute-start(bf16[6,256,256]{2,1,0:T(8,128)(2,1)S(1)} %collective-permute-done.22.refs_1_), channel_id=1, source_target_pairs={{0,24},{1,25},{2,26},{3,27},{4,28},{5,29},{6,30},{7,31},{8,0},{9,1... | collective-permute-start | bytes 2359304 | tf_op jit(solution)/shard_map/ppermute | solution.py:37
  115.8 2.6 %shard_map.57 = f32[1024,256]{1,0:T(8,128)S(1)} custom-call(bf16[6,256,256]{2,1,0:T(8,128)(2,1)S(1)} %collective-permute-done.24.refs_0_, bf16[6,256,256]{2,1,0:T(8,128)(2,1)S(1)} %collective-permute-done.25.refs_1_, bf16[6,256,256]{2,1,0:T(8,128)(2,1)S(1)} %collective-permute-done.26.refs_2_, bf16[512,8192]{1,0:T(8,128)(2,1)S(1)} %shard_map.48.refs_6_.refs_8_.refs_3_, ...), custom_call_target="tpu_custom_call" | custom-call | flops 2415919104 | bytes 9437184 | tf_op jit(solution)/shard_map/pallas_call | solution.py:206
  118.4 0.1 collective-permute-start.27
  118.5 0.3 collective-permute-done.18.refs_2_
  118.8 2.6 %shard_map.55 = f32[1024,256]{1,0:T(8,128)S(1)} custom-call(bf16[6,256,256]{2,1,0:T(8,128)(2,1)S(1)} %collective-permute-done.16.refs_0_, bf16[6,256,256]{2,1,0:T(8,128)(2,1)S(1)} %collective-permute-done.17.refs_1_, bf16[6,256,256]{2,1,0:T(8,128)(2,1)S(1)} %collective-permute-done.18.refs_2_, bf16[512,8192]{1,0:T(8,128)(2,1)S(1)} %shard_map.48.refs_6_.refs_8_.refs_3_, ...), custom_call_target="tpu_custom_call" | custom-call | flops 2415919104 | bytes 9437184 | tf_op jit(solution)/shard_map/pallas_call | solution.py:206
  121.4 0.3 collective-permute-start.19
  121.7 5.4 %collective-permute-done.21.refs_0_ = bf16[6,256,256]{2,1,0:T(8,128)(2,1)S(1)} collective-permute-done((bf16[6,256,256]{2,1,0:T(8,128)(2,1)S(1)}, bf16[6,256,256]{2,1,0:T(8,128)(2,1)S(1)}, u32[]{:S(2)}, u32[]{:S(2)}) %collective-permute-start.21) | collective-permute-done | bytes 786464 | tf_op jit(solution)/shard_map/ppermute | solution.py:37
  127.1 1.7 %collective-permute-start.8 = (bf16[6,256,256]{2,1,0:T(8,128)(2,1)S(1)}, bf16[6,256,256]{2,1,0:T(8,128)(2,1)S(1)}, u32[]{:S(2)}, u32[]{:S(2)}) collective-permute-start(bf16[6,256,256]{2,1,0:T(8,128)(2,1)S(1)} %get-tuple-element.15), channel_id=1, source_target_pairs={{0,24},{1,25},{2,26},{3,27},{4,28},{5,29},{6,30},{7,31},{8,0},{9,1... | collective-permute-start | bytes 2359304 | tf_op jit(solution)/shard_map/ppermute | solution.py:37
  128.8 12.9 %collective-permute-done.7.refs_0_ = bf16[6,256,256]{2,1,0:T(8,128)(2,1)S(1)} collective-permute-done((bf16[6,256,256]{2,1,0:T(8,128)(2,1)S(1)}, bf16[6,256,256]{2,1,0:T(8,128)(2,1)S(1)}, u32[]{:S(2)}, u32[]{:S(2)}) %collective-permute-start.7) | collective-permute-done | bytes 786464 | tf_op jit(solution)/shard_map/ppermute | solution.py:37
  141.7 0.0 collective-permute-start.9
  141.7 2.6 %shard_map.56.mine.refs_3_ = f32[1024,256]{1,0:T(8,128)S(1)} custom-call(bf16[6,256,256]{2,1,0:T(8,128)(2,1)S(1)} %collective-permute-done.21.refs_0_, bf16[6,256,256]{2,1,0:T(8,128)(2,1)S(1)} %collective-permute-done.22.refs_1_, bf16[6,256,256]{2,1,0:T(8,128)(2,1)S(1)} %collective-permute-done.23.refs_2_, ...), custom_call_target="tpu_custom_call" | custom-call | flops 2415919104 | bytes 9437184 | tf_op jit(solution)/shard_map/pallas_call | solution.py:206
  144.3 10.6 %collective-permute-done.9.refs_2_ = bf16[6,256,256]{2,1,0:T(8,128)(2,1)S(1)} collective-permute-done((bf16[6,256,256]{2,1,0:T(8,128)(2,1)S(1)}, bf16[6,256,256]{2,1,0:T(8,128)(2,1)S(1)}, u32[]{:S(2)}, u32[]{:S(2)}) %collective-permute-start.9) | collective-permute-done | bytes 786464 | tf_op jit(solution)/shard_map/ppermute | solution.py:37
  154.9 2.6 %shard_map.52.mine.refs_0_ = f32[1024,256]{1,0:T(8,128)S(1)} custom-call(bf16[6,256,256]{2,1,0:T(8,128)(2,1)S(1)} %collective-permute-done.7.refs_0_, bf16[6,256,256]{2,1,0:T(8,128)(2,1)S(1)} %collective-permute-done.8.refs_1_, bf16[6,256,256]{2,1,0:T(8,128)(2,1)S(1)} %collective-permute-done.9.refs_2_, ...), custom_call_target="tpu_custom_call" | custom-call | flops 2415919104 | bytes 9437184 | tf_op jit(solution)/shard_map/pallas_call | solution.py:206
  157.5 0.2 code.3
  157.7 3.8 %collective-permute-start.28 = (s16[1088,128]{1,0:T(8,128)(2,1)S(1)}, s16[1088,128]{1,0:T(8,128)(2,1)S(1)}, u32[]{:S(2)}, u32[]{:S(2)}) collective-permute-start(s16[1088,128]{1,0:T(8,128)(2,1)S(1)} %code.3), channel_id=1, source_target_pairs={{0,64},{32,96},{64,0},{96,32},{1,65},{33,97},{65,1},{97,33},{2,66}... | collective-permute-start | bytes 835592 | tf_op jit(solution)/shard_map/ppermute | solution.py:309
  161.5 0.2 code.2
  161.6 0.1 collective-permute-start.20
  161.7 4.3 %collective-permute-done.28.refs_5_ = s16[1088,128]{1,0:T(8,128)(2,1)S(1)} collective-permute-done((s16[1088,128]{1,0:T(8,128)(2,1)S(1)}, s16[1088,128]{1,0:T(8,128)(2,1)S(1)}, u32[]{:S(2)}, u32[]{:S(2)}) %collective-permute-start.28) | collective-permute-done | bytes 278560 | tf_op jit(solution)/shard_map/ppermute | solution.py:309
  166.0 3.8 %collective-permute-done.20.refs_2_ = s16[1088,128]{1,0:T(8,128)(2,1)S(1)} collective-permute-done((s16[1088,128]{1,0:T(8,128)(2,1)S(1)}, s16[1088,128]{1,0:T(8,128)(2,1)S(1)}, u32[]{:S(2)}, u32[]{:S(2)}) %collective-permute-start.20) | collective-permute-done | bytes 278560 | tf_op jit(solution)/shard_map/ppermute | solution.py:309
  169.8 1.1 finish.1
  (14 shorter events, 0.1 us)
Async XLA Ops:
  0.0 0.7 copy-start.1
  0.7 85.2 %copy-start = (s32[8,64]{1,0:T(8,128)S(1)}, s32[8,64]{1,0:T(8,128)}, u32[]{:S(2)}) copy-start(s32[8,64]{1,0:T(8,128)} %mask_ref.3) | copy-start | bytes 6148
  2.4 14.0 %collective-permute-start.2 = (bf16[256,1024]{1,0:T(8,128)(2,1)S(1)}, bf16[256,1024]{1,0:T(8,128)(2,1)S(1)}, u32[]{:S(2)}, u32[]{:S(2)}) collective-permute-start(bf16[256,1024]{1,0:T(8,128)(2,1)S(1)} %pick.1.refs_0_), channel_id=1, source_target_pairs={{0,4},{1,5},{2,6},{3,7},{4,0},{5,1},{6,2},{7,3},{8,12},{9,13},{10,... | collective-permute-start | bytes 1572872 | tf_op jit(solution)/shard_map/ppermute | solution.py:37
  4.5 18.5 %collective-permute-start = (bf16[256,1024]{1,0:T(8,128)(2,1)S(1)}, bf16[256,1024]{1,0:T(8,128)(2,1)S(1)}, u32[]{:S(2)}, u32[]{:S(2)}) collective-permute-start(bf16[256,1024]{1,0:T(8,128)(2,1)S(1)} %pick.1.refs_0_), channel_id=1, source_target_pairs={{0,1},{1,2},{2,3},{3,0},{4,5},{5,6},{6,7},{7,4},{8,9},{9,10},{10,1... | collective-permute-start | bytes 1572872 | tf_op jit(solution)/shard_map/ppermute | solution.py:37
  6.1 18.2 %collective-permute-start.12 = (bf16[256,1024]{1,0:T(8,128)(2,1)S(1)}, bf16[256,1024]{1,0:T(8,128)(2,1)S(1)}, u32[]{:S(2)}, u32[]{:S(2)}) collective-permute-start(bf16[256,1024]{1,0:T(8,128)(2,1)S(1)} %pick.1.refs_0_), channel_id=1, source_target_pairs={{0,8},{1,9},{2,10},{3,11},{4,12},{5,13},{6,14},{7,15},{8,16},{9,17... | collective-permute-start | bytes 1572872 | tf_op jit(solution)/shard_map/ppermute | solution.py:37
  16.4 15.1 %collective-permute-start.11 = (bf16[256,1024]{1,0:T(8,128)(2,1)S(1)}, bf16[256,1024]{1,0:T(8,128)(2,1)S(1)}, u32[]{:S(2)}, u32[]{:S(2)}) collective-permute-start(bf16[256,1024]{1,0:T(8,128)(2,1)S(1)} %collective-permute-done.2.refs_1_), channel_id=1, source_target_pairs={{0,24},{1,25},{2,26},{3,27},{4,28},{5,29},{6,30},{7,31},{8,0},{9,1... | collective-permute-start | bytes 1572872 | tf_op jit(solution)/shard_map/ppermute | solution.py:37
  19.2 23.5 %collective-permute-start.15 = (bf16[256,1024]{1,0:T(8,128)(2,1)S(1)}, bf16[256,1024]{1,0:T(8,128)(2,1)S(1)}, u32[]{:S(2)}, u32[]{:S(2)}) collective-permute-start(bf16[256,1024]{1,0:T(8,128)(2,1)S(1)} %pick.1.refs_0_), channel_id=1, source_target_pairs={{0,24},{1,25},{2,26},{3,27},{4,28},{5,29},{6,30},{7,31},{8,0},{9,1... | collective-permute-start | bytes 1572872 | tf_op jit(solution)/shard_map/ppermute | solution.py:37
  20.0 25.7 %collective-permute-start.3 = (bf16[256,1024]{1,0:T(8,128)(2,1)S(1)}, bf16[256,1024]{1,0:T(8,128)(2,1)S(1)}, u32[]{:S(2)}, u32[]{:S(2)}) collective-permute-start(bf16[256,1024]{1,0:T(8,128)(2,1)S(1)} %collective-permute-done.2.refs_1_), channel_id=1, source_target_pairs={{0,3},{1,0},{2,1},{3,2},{4,7},{5,4},{6,5},{7,6},{8,11},{9,8},{10,9... | collective-permute-start | bytes 1572872 | tf_op jit(solution)/shard_map/ppermute | solution.py:37
  23.0 22.7 %collective-permute-start.10 = (bf16[256,1024]{1,0:T(8,128)(2,1)S(1)}, bf16[256,1024]{1,0:T(8,128)(2,1)S(1)}, u32[]{:S(2)}, u32[]{:S(2)}) collective-permute-start(bf16[256,1024]{1,0:T(8,128)(2,1)S(1)} %collective-permute-done.2.refs_1_), channel_id=1, source_target_pairs={{0,8},{1,9},{2,10},{3,11},{4,12},{5,13},{6,14},{7,15},{8,16},{9,17... | collective-permute-start | bytes 1572872 | tf_op jit(solution)/shard_map/ppermute | solution.py:37
  24.2 23.4 %collective-permute-start.13 = (bf16[256,1024]{1,0:T(8,128)(2,1)S(1)}, bf16[256,1024]{1,0:T(8,128)(2,1)S(1)}, u32[]{:S(2)}, u32[]{:S(2)}) collective-permute-start(bf16[256,1024]{1,0:T(8,128)(2,1)S(1)} %collective-permute-done.12.refs_2_.refs_0_), channel_id=1, source_target_pairs={{0,8},{1,9},{2,10},{3,11},{4,12},{5,13},{6,14},{7,15},{8,16},{9,17... | collective-permute-start | bytes 1572872 | tf_op jit(solution)/shard_map/ppermute | solution.py:37
  31.5 20.7 %collective-permute-start.14 = (bf16[256,1024]{1,0:T(8,128)(2,1)S(1)}, bf16[256,1024]{1,0:T(8,128)(2,1)S(1)}, u32[]{:S(2)}, u32[]{:S(2)}) collective-permute-start(bf16[256,1024]{1,0:T(8,128)(2,1)S(1)} %collective-permute-done.11.refs_1_.refs_3_), channel_id=1, source_target_pairs={{0,24},{1,25},{2,26},{3,27},{4,28},{5,29},{6,30},{7,31},{8,0},{9,1... | collective-permute-start | bytes 1572872 | tf_op jit(solution)/shard_map/ppermute | solution.py:37
  42.7 15.3 %collective-permute-start.6 = (bf16[256,1024]{1,0:T(8,128)(2,1)S(1)}, bf16[256,1024]{1,0:T(8,128)(2,1)S(1)}, u32[]{:S(2)}, u32[]{:S(2)}) collective-permute-start(bf16[256,1024]{1,0:T(8,128)(2,1)S(1)} %pick.1.refs_0_), channel_id=1, source_target_pairs={{0,3},{1,0},{2,1},{3,2},{4,7},{5,4},{6,5},{7,6},{8,11},{9,8},{10,9... | collective-permute-start | bytes 1572872 | tf_op jit(solution)/shard_map/ppermute | solution.py:37
  45.7 16.0 %collective-permute-start.5 = (bf16[256,1024]{1,0:T(8,128)(2,1)S(1)}, bf16[256,1024]{1,0:T(8,128)(2,1)S(1)}, u32[]{:S(2)}, u32[]{:S(2)}) collective-permute-start(bf16[256,1024]{1,0:T(8,128)(2,1)S(1)} %collective-permute-done.2.refs_1_), channel_id=1, source_target_pairs={{0,1},{1,2},{2,3},{3,0},{4,5},{5,6},{6,7},{7,4},{8,9},{9,10},{10,1... | collective-permute-start | bytes 1572872 | tf_op jit(solution)/shard_map/ppermute | solution.py:37
  45.7 27.2 %collective-permute-start.1 = (bf16[256,1024]{1,0:T(8,128)(2,1)S(1)}, bf16[256,1024]{1,0:T(8,128)(2,1)S(1)}, u32[]{:S(2)}, u32[]{:S(2)}) collective-permute-start(bf16[256,1024]{1,0:T(8,128)(2,1)S(1)} %collective-permute-done.refs_0_.refs_4_), channel_id=1, source_target_pairs={{0,1},{1,2},{2,3},{3,0},{4,5},{5,6},{6,7},{7,4},{8,9},{9,10},{10,1... | collective-permute-start | bytes 1572872 | tf_op jit(solution)/shard_map/ppermute | solution.py:37
  47.6 25.4 %collective-permute-start.4 = (bf16[256,1024]{1,0:T(8,128)(2,1)S(1)}, bf16[256,1024]{1,0:T(8,128)(2,1)S(1)}, u32[]{:S(2)}, u32[]{:S(2)}) collective-permute-start(bf16[256,1024]{1,0:T(8,128)(2,1)S(1)} %collective-permute-done.3.refs_3_), channel_id=1, source_target_pairs={{0,3},{1,0},{2,1},{3,2},{4,7},{5,4},{6,5},{7,6},{8,11},{9,8},{10,9... | collective-permute-start | bytes 1572872 | tf_op jit(solution)/shard_map/ppermute | solution.py:37
  52.2 30.2 %collective-permute-start.25 = (bf16[6,256,256]{2,1,0:T(8,128)(2,1)S(1)}, bf16[6,256,256]{2,1,0:T(8,128)(2,1)S(1)}, u32[]{:S(2)}, u32[]{:S(2)}) collective-permute-start(bf16[6,256,256]{2,1,0:T(8,128)(2,1)S(1)} %get-tuple-element.20), channel_id=1, source_target_pairs={{0,3},{1,0},{2,1},{3,2},{4,7},{5,4},{6,5},{7,6},{8,11},{9,8},{10,9... | collective-permute-start | bytes 2359304 | tf_op jit(solution)/shard_map/ppermute | solution.py:37
  58.0 39.1 %collective-permute-start.16 = (bf16[6,256,256]{2,1,0:T(8,128)(2,1)S(1)}, bf16[6,256,256]{2,1,0:T(8,128)(2,1)S(1)}, u32[]{:S(2)}, u32[]{:S(2)}) collective-permute-start(bf16[6,256,256]{2,1,0:T(8,128)(2,1)S(1)} %get-tuple-element.18), channel_id=1, source_target_pairs={{0,1},{1,2},{2,3},{3,0},{4,5},{5,6},{6,7},{7,4},{8,9},{9,10},{10,1... | collective-permute-start | bytes 2359304 | tf_op jit(solution)/shard_map/ppermute | solution.py:37
  61.8 44.9 %collective-permute-start.24 = (bf16[6,256,256]{2,1,0:T(8,128)(2,1)S(1)}, bf16[6,256,256]{2,1,0:T(8,128)(2,1)S(1)}, u32[]{:S(2)}, u32[]{:S(2)}) collective-permute-start(bf16[6,256,256]{2,1,0:T(8,128)(2,1)S(1)} %get-tuple-element.20), channel_id=1, source_target_pairs={{0,1},{1,2},{2,3},{3,0},{4,5},{5,6},{6,7},{7,4},{8,9},{9,10},{10,1... | collective-permute-start | bytes 2359304 | tf_op jit(solution)/shard_map/ppermute | solution.py:37
  73.0 34.9 %collective-permute-start.22 = (bf16[6,256,256]{2,1,0:T(8,128)(2,1)S(1)}, bf16[6,256,256]{2,1,0:T(8,128)(2,1)S(1)}, u32[]{:S(2)}, u32[]{:S(2)}) collective-permute-start(bf16[6,256,256]{2,1,0:T(8,128)(2,1)S(1)} %get-tuple-element.19), channel_id=1, source_target_pairs={{0,24},{1,25},{2,26},{3,27},{4,28},{5,29},{6,30},{7,31},{8,0},{9,1... | collective-permute-start | bytes 2359304 | tf_op jit(solution)/shard_map/ppermute | solution.py:37
  82.3 31.6 %collective-permute-start.26 = (bf16[6,256,256]{2,1,0:T(8,128)(2,1)S(1)}, bf16[6,256,256]{2,1,0:T(8,128)(2,1)S(1)}, u32[]{:S(2)}, u32[]{:S(2)}) collective-permute-start(bf16[6,256,256]{2,1,0:T(8,128)(2,1)S(1)} %collective-permute-done.25.refs_1_), channel_id=1, source_target_pairs={{0,3},{1,0},{2,1},{3,2},{4,7},{5,4},{6,5},{7,6},{8,11},{9,8},{10,9... | collective-permute-start | bytes 2359304 | tf_op jit(solution)/shard_map/ppermute | solution.py:37
  97.1 21.3 %collective-permute-start.17 = (bf16[6,256,256]{2,1,0:T(8,128)(2,1)S(1)}, bf16[6,256,256]{2,1,0:T(8,128)(2,1)S(1)}, u32[]{:S(2)}, u32[]{:S(2)}) collective-permute-start(bf16[6,256,256]{2,1,0:T(8,128)(2,1)S(1)} %get-tuple-element.18), channel_id=1, source_target_pairs={{0,3},{1,0},{2,1},{3,2},{4,7},{5,4},{6,5},{7,6},{8,11},{9,8},{10,9... | collective-permute-start | bytes 2359304 | tf_op jit(solution)/shard_map/ppermute | solution.py:37
  97.2 21.6 %collective-permute-start.18 = (bf16[6,256,256]{2,1,0:T(8,128)(2,1)S(1)}, bf16[6,256,256]{2,1,0:T(8,128)(2,1)S(1)}, u32[]{:S(2)}, u32[]{:S(2)}) collective-permute-start(bf16[6,256,256]{2,1,0:T(8,128)(2,1)S(1)} %collective-permute-done.16.refs_0_), channel_id=1, source_target_pairs={{0,1},{1,2},{2,3},{3,0},{4,5},{5,6},{6,7},{7,4},{8,9},{9,10},{10,1... | collective-permute-start | bytes 2359304 | tf_op jit(solution)/shard_map/ppermute | solution.py:37
  106.7 20.4 %collective-permute-start.21 = (bf16[6,256,256]{2,1,0:T(8,128)(2,1)S(1)}, bf16[6,256,256]{2,1,0:T(8,128)(2,1)S(1)}, u32[]{:S(2)}, u32[]{:S(2)}) collective-permute-start(bf16[6,256,256]{2,1,0:T(8,128)(2,1)S(1)} %get-tuple-element.19), channel_id=1, source_target_pairs={{0,8},{1,9},{2,10},{3,11},{4,12},{5,13},{6,14},{7,15},{8,16},{9,17... | collective-permute-start | bytes 2359304 | tf_op jit(solution)/shard_map/ppermute | solution.py:37
  107.9 33.8 %collective-permute-start.7 = (bf16[6,256,256]{2,1,0:T(8,128)(2,1)S(1)}, bf16[6,256,256]{2,1,0:T(8,128)(2,1)S(1)}, u32[]{:S(2)}, u32[]{:S(2)}) collective-permute-start(bf16[6,256,256]{2,1,0:T(8,128)(2,1)S(1)} %get-tuple-element.15), channel_id=1, source_target_pairs={{0,8},{1,9},{2,10},{3,11},{4,12},{5,13},{6,14},{7,15},{8,16},{9,17... | collective-permute-start | bytes 2359304 | tf_op jit(solution)/shard_map/ppermute | solution.py:37
  114.0 27.7 %collective-permute-start.23 = (bf16[6,256,256]{2,1,0:T(8,128)(2,1)S(1)}, bf16[6,256,256]{2,1,0:T(8,128)(2,1)S(1)}, u32[]{:S(2)}, u32[]{:S(2)}) collective-permute-start(bf16[6,256,256]{2,1,0:T(8,128)(2,1)S(1)} %collective-permute-done.22.refs_1_), channel_id=1, source_target_pairs={{0,24},{1,25},{2,26},{3,27},{4,28},{5,29},{6,30},{7,31},{8,0},{9,1... | collective-permute-start | bytes 2359304 | tf_op jit(solution)/shard_map/ppermute | solution.py:37
  118.4 39.1 %collective-permute-start.27 = (f32[1024,256]{1,0:T(8,128)S(1)}, f32[1024,256]{1,0:T(8,128)S(1)}, u32[]{:S(2)}, u32[]{:S(2)}) collective-permute-start(f32[1024,256]{1,0:T(8,128)S(1)} %shard_map.57), channel_id=1, source_target_pairs={{0,32},{32,0},{64,96},{96,64},{1,33},{33,1},{65,97},{97,65},{2,34}... | collective-permute-start | bytes 3145736 | tf_op jit(solution)/shard_map/ppermute | solution.py:306
  121.4 40.1 %collective-permute-start.19 = (f32[1024,256]{1,0:T(8,128)S(1)}, f32[1024,256]{1,0:T(8,128)S(1)}, u32[]{:S(2)}, u32[]{:S(2)}) collective-permute-start(f32[1024,256]{1,0:T(8,128)S(1)} %shard_map.55), channel_id=1, source_target_pairs={{0,32},{32,0},{64,96},{96,64},{1,33},{33,1},{65,97},{97,65},{2,34}... | collective-permute-start | bytes 3145736 | tf_op jit(solution)/shard_map/ppermute | solution.py:306
  127.1 17.2 %collective-permute-start.8 = (bf16[6,256,256]{2,1,0:T(8,128)(2,1)S(1)}, bf16[6,256,256]{2,1,0:T(8,128)(2,1)S(1)}, u32[]{:S(2)}, u32[]{:S(2)}) collective-permute-start(bf16[6,256,256]{2,1,0:T(8,128)(2,1)S(1)} %get-tuple-element.15), channel_id=1, source_target_pairs={{0,24},{1,25},{2,26},{3,27},{4,28},{5,29},{6,30},{7,31},{8,0},{9,1... | collective-permute-start | bytes 2359304 | tf_op jit(solution)/shard_map/ppermute | solution.py:37
  141.7 13.2 %collective-permute-start.9 = (bf16[6,256,256]{2,1,0:T(8,128)(2,1)S(1)}, bf16[6,256,256]{2,1,0:T(8,128)(2,1)S(1)}, u32[]{:S(2)}, u32[]{:S(2)}) collective-permute-start(bf16[6,256,256]{2,1,0:T(8,128)(2,1)S(1)} %collective-permute-done.7.refs_0_), channel_id=1, source_target_pairs={{0,8},{1,9},{2,10},{3,11},{4,12},{5,13},{6,14},{7,15},{8,16},{9,17... | collective-permute-start | bytes 2359304 | tf_op jit(solution)/shard_map/ppermute | solution.py:37
  157.7 8.3 %collective-permute-start.28 = (s16[1088,128]{1,0:T(8,128)(2,1)S(1)}, s16[1088,128]{1,0:T(8,128)(2,1)S(1)}, u32[]{:S(2)}, u32[]{:S(2)}) collective-permute-start(s16[1088,128]{1,0:T(8,128)(2,1)S(1)} %code.3), channel_id=1, source_target_pairs={{0,64},{32,96},{64,0},{96,32},{1,65},{33,97},{65,1},{97,33},{2,66}... | collective-permute-start | bytes 835592 | tf_op jit(solution)/shard_map/ppermute | solution.py:309
  161.6 8.1 %collective-permute-start.20 = (s16[1088,128]{1,0:T(8,128)(2,1)S(1)}, s16[1088,128]{1,0:T(8,128)(2,1)S(1)}, u32[]{:S(2)}, u32[]{:S(2)}) collective-permute-start(s16[1088,128]{1,0:T(8,128)(2,1)S(1)} %code.2), channel_id=1, source_target_pairs={{0,64},{32,96},{64,0},{96,32},{1,65},{33,97},{65,1},{97,33},{2,66}... | collective-permute-start | bytes 835592 | tf_op jit(solution)/shard_map/ppermute | solution.py:309

commit v3 on v2

--- a/solution.py
+++ b/solution.py
@@ -17,6 +17,7 @@
 LIMIT = 6 << 20
 LINE = (-1, 1, 2)
 TAIL = 64
+HALF = 512
 
 
 def blk(x, z, y):
@@ -78,7 +79,7 @@
         cost_estimate=pl.CostEstimate(flops=1000, bytes_accessed=1 << 20, transcendentals=0),
         compiler_params=params(),
         name="pick",
-    )(batches, off_chip(amplitudes))
+    )(off_chip(batches), off_chip(amplitudes))
 
 
 def keep_kernel(first, mask_ref, v_ref, out_ref, sems):
@@ -117,14 +118,14 @@
         ),
         cost_estimate=pl.CostEstimate(flops=1000, bytes_accessed=tiles << 21, transcendentals=0),
         compiler_params=params(),
-    )(mask, off_chip(v))
+    )(off_chip(mask), off_chip(v))
 
 
 def lay_kernel(slots, base, *refs):
     sources, outs = refs[: len(slots)], refs[-2:]
     for slot, source in zip(slots, sources):
         for k in range(2):
-            at = base + 2 * BATCH * k
+            at = 2 * BATCH * k + (base if source.shape[1] > HALF else 0)
             outs[k][slot] = source[:, at : at + 2 * BATCH]
 
 
@@ -141,6 +142,30 @@
     )(*arrays, *before)
 
 
+def halves_kernel(plan, *refs):
+    outs = refs[-len(plan) :]
+    for out, places in zip(outs, plan):
+        for k, (i, base) in enumerate(places):
+            piece = refs[i][:, base : base + HALF]
+            if len(places) == 1:
+                out[...] = piece
+            else:
+                out[k] = piece
+
+
+def halves(plan, arrays):
+    rows = arrays[0].shape[0]
+    lead = [() if len(places) == 1 else (len(places),) for places in plan]
+    return pl.pallas_call(
+        functools.partial(halves_kernel, plan),
+        out_shape=[jax.ShapeDtypeStruct(n + (rows, HALF), BF16) for n in lead],
+        in_specs=vmem(len(arrays)),
+        out_specs=vmem(len(plan)),
+        cost_estimate=pl.CostEstimate(flops=1000, bytes_accessed=1 << 20, transcendentals=0),
+        compiler_params=params(),
+    )(*arrays)
+
+
 def dot(a, b):
     return jnp.dot(a, b, preferred_element_type=F32)
 
@@ -153,42 +178,50 @@
     return pl.ds(pl.multiple_of(at * 256, 256), 256)
 
 
-def cross_kernel(offsets, *refs):
-    steps = len(offsets)
-    parts, (top, bottom), before, acc_ref = refs[:steps], refs[steps : steps + 2], refs[steps + 2 : -1], refs[-1]
+def cross_kernel(offsets, picks, n_arrays, *refs):
+    arrays, (top, bottom), before, acc_ref = (
+        refs[:n_arrays],
+        refs[n_arrays : n_arrays + 2],
+        refs[n_arrays + 2 : -1],
+        refs[-1],
+    )
     rows = top.shape[0]
-    for i, offset in enumerate(offsets):
+    for step, (offset, parts) in enumerate(zip(offsets, picks)):
+        width = acc_ref.shape[1] // len(parts)
         for k, v_ref in enumerate((top, bottom)):
             at = slice(k * rows, (k + 1) * rows)
-            product = dot(v_ref[:, column(offset)], parts[i][...])
-            if i > 0:
-                acc_ref[at, :] += product
-            else:
-                acc_ref[at, :] = before[0][at, :] + product if before else product
-
-
-def cross(offsets, parts, v, before=()):
+            tile = v_ref[:, column(offset)]
+            for h, (i, slot) in enumerate(parts):
+                cols = slice(h * width, (h + 1) * width)
+                product = dot(tile, arrays[i][...] if slot is None else arrays[i][slot])
+                if step > 0:
+                    acc_ref[at, cols] += product
+                else:
+                    acc_ref[at, cols] = before[0][at, cols] + product if before else product
+
+
+def cross(offsets, picks, arrays, v, before=()):
     rows = 2 * v[0].shape[0]
-    steps = len(parts)
-    return pl.pallas_call(
-        functools.partial(cross_kernel, offsets),
+    steps = len(offsets)
+    return pl.pallas_call(
+        functools.partial(cross_kernel, offsets, picks, len(arrays)),
         out_shape=jax.ShapeDtypeStruct((rows, NB * BATCH), F32),
-        in_specs=vmem(steps + 2 + len(before)),
+        in_specs=vmem(len(arrays) + 2 + len(before)),
         out_specs=pl.BlockSpec(memory_space=pltpu.VMEM),
         cost_estimate=pl.CostEstimate(
             flops=2 * rows * steps * 256 * 1024, bytes_accessed=steps << 20, transcendentals=0
         ),
         compiler_params=params(),
-    )(*parts, *v, *before)
-
-
-def group_kernel(base, turned, *refs):
-    parts, (top, bottom, acc_ref, out) = refs[:3], refs[3:]
+    )(*arrays, *v, *before)
+
+
+def group_kernel(base, turned, fars, *refs):
+    parts, (top, bottom, acc_ref, out) = refs[: len(fars)], refs[len(fars) :]
     cols, rows = out.shape[1], top.shape[0]
     for k, v_ref in enumerate((top, bottom)):
         at = slice(k * rows, (k + 1) * rows)
         first = True
-        for j, far in enumerate(LINE):
+        for j, far in enumerate(fars):
             for i, near in enumerate(LINE):
                 for dz in (0, 1):
                     offset = (far, dz, near) if turned else (near, dz, far)
@@ -200,16 +233,16 @@
                     first = False
 
 
-def group(base, turned, parts, v, acc):
+def group(base, turned, fars, parts, v, acc):
     rows = 2 * v[0].shape[0]
     cols = parts[0].shape[2]
     return pl.pallas_call(
-        functools.partial(group_kernel, base, turned),
+        functools.partial(group_kernel, base, turned, fars),
         out_shape=jax.ShapeDtypeStruct((rows, cols), F32),
-        in_specs=vmem(6),
+        in_specs=vmem(len(parts) + 3),
         out_specs=pl.BlockSpec(memory_space=pltpu.VMEM),
         cost_estimate=pl.CostEstimate(
-            flops=2 * rows * 18 * 256 * 256, bytes_accessed=18 << 19, transcendentals=0
+            flops=2 * rows * 6 * len(parts) * 256 * 256, bytes_accessed=18 << 19, transcendentals=0
         ),
         compiler_params=params(),
     )(*parts, *v, acc)
@@ -273,15 +306,21 @@
     near = send(own, ZX)
     xp0, yp0 = send(own, XM), send(own, YM)
     xm0, ym0 = send(own, XP), send(own, YP)
-    xp1, yp1 = send(near, XM), send(near, YM)
-    xm1, ym1 = send(near, XP), send(near, YP)
-    x20, y20 = send(xm0, XP), send(ym0, YP)
+    near_a, near_b = halves([[(0, 0)], [(0, HALF)]], [near])
+    xp1, yp1 = send(near_a, XM), send(near_b, YM)
+    xm1, ym1 = send(near_a, XP), send(near_b, YP)
+    plan = [[(0, 0)], [(1, HALF)], [(0, HALF)], [(1, 0)], [(0, HALF), (2, HALF)], [(1, 0), (3, 0)]]
+    xa, yb, xb, ya, zx, zy = halves(plan, [xm0, ym0, xp0, yp0])
+    x20, y20 = send(xa, XP), send(yb, YP)
     x21, y21 = send(xp1, XM), send(yp1, YM)
+    x20b, y20a = send(xb, XP), send(ya, YP)
+    zx, zy = send(zx, ZX), send(zy, ZX)
+    zd = send(halves([[(0, 0), (1, 0)]], [x20b, y20a])[0], ZX)
 
     early_x = lay((0, 1, 2, 3), 0, [xm0, xm1, xp0, xp1])
-    early_y = lay((0, 1, 2, 3), 512, [ym0, ym1, yp0, yp1])
+    early_y = lay((0, 1, 2, 3), HALF, [ym0, ym1, yp0, yp1])
     along_x = lay((4, 5), 0, [x20, x21], early_x)
-    along_y = lay((4, 5), 512, [y20, y21], early_y)
+    along_y = lay((4, 5), HALF, [y20, y21], early_y)
 
     pieces = []
     for k in range(2):
@@ -294,17 +333,37 @@
         pieces.append(([ym, yp, y2], [xm, xp, x2]))
 
     v = [keep(4 * k, 4, integrals, block_mask) for k in range(2)]
-    near_at = [(-1, 0, 0), (1, 0, 0), (0, 0, -1), (0, 0, 1)]
-    far_at = [(dx, 1, dy) for dx, dz, dy in near_at] + [(2, 0, 0), (2, 1, 0), (0, 0, 2), (0, 1, 2)]
-    acc = cross([(0, 0, 0), (0, 1, 0)] + near_at, [own, near, xm0, xp0, ym0, yp0], v)
-    acc = cross(far_at, [xm1, xp1, ym1, yp1, x20, x21, y20, y21], v, [acc])
+    near_at = [(0, 0, 0), (0, 1, 0), (-1, 0, 0), (1, 0, 0), (0, 0, -1), (0, 0, 1)]
+    arrays = [own, near, xm0, xp0, ym0, yp0]
+    acc = cross(near_at, [[(i, None)] for i in range(6)], arrays, v)
+    far_at = [(-1, 1, 0), (1, 1, 0), (0, 1, -1), (0, 1, 1), (2, 0, 0), (2, 1, 0), (0, 0, 2), (0, 1, 2)]
+    arrays = [zx, zy, zd, xm1, xp1, ym1, yp1, x20, x20b, x21, y20a, y20, y21]
+    picks = [
+        [(3, None), (0, 0)],
+        [(4, None), (0, 1)],
+        [(1, 0), (5, None)],
+        [(1, 1), (6, None)],
+        [(7, None), (8, None)],
+        [(9, None), (2, 0)],
+        [(10, None), (11, None)],
+        [(2, 1), (12, None)],
+    ]
+    acc = cross(far_at, picks, arrays, v, [acc])
 
     parts = []
     for k in range(2):
         ys, xs = pieces[k]
-        theirs = group(k, False, ys, v, acc)
+        if k == 0:
+            theirs = group(0, False, LINE, ys, v, acc)
+        else:
+            begun = group(1, False, (1,), ys[1:2], v, acc)
+            theirs = group(0, False, (-1, 2), ys[::2], v, begun)
         got = lax.ppermute(theirs, "grp", CORE)
-        mine = group(2 + k, True, xs, v, acc)
+        if k == 0:
+            mine = group(2, True, LINE, xs, v, acc)
+        else:
+            begun = group(3, True, (1,), xs[1:2], v, acc)
+            mine = group(0, True, (-1, 2), xs[::2], v, begun)
         packed = code(mine, got)
         far = lax.ppermute(packed, "grp", ZHI)
         parts += [mine, got, far]

time: 171 us -> 151 us (0.88)
  waiting for transfers between devices: 91.2 us -> 67.6 us
  starting transfers between devices: 45.9 us -> 48.9 us
    ppermute x25 -> x30, waiting for transfers between devices: 83.1 us -> 60.3 us  [send(): return lax.ppermute(array, 'blk', pairs)]
    ppermute x25 -> x30, starting transfers between devices: 41.6 us -> 44.8 us  [send(): return lax.ppermute(array, 'blk', pairs)]
    pallas_call x6 -> x11, Pallas kernels: 18.5 us -> 19 us  [the longest x6 10.8 us: group(): pl.pallas_call(functools.partial(group_kernel, base, turned, fars), out_s...]
  transfers between devices with their start and end apart: 29 -> 34, of which waited for: 16 -> 13; matrix products, arithmetic and copies ran while one was open for 0% -> 0% of each run, Pallas kernels for 18% -> 21%
where the time goes in v3:
time: 151 us
  waiting for transfers between devices  67.6 us (45%)
  starting transfers between devices  48.9 us (32%)
  Pallas kernels  33.8 us (22%)
    ppermute x30, waiting for transfers between devices, send(): return lax.ppermute(array, 'blk', pairs)  60.3 us
    ppermute x30, starting transfers between devices, send(): return lax.ppermute(array, 'blk', pairs)  44.8 us
    pallas_call x2, Pallas kernels, keep(): pl.pallas_call(functools.partial(keep_kernel, first), out_shape=jax.Shape...  11.4 us
    pallas_call x6, Pallas kernels, group(): pl.pallas_call(functools.partial(group_kernel, base, turned, fars), out_s...  10.8 us
    pallas_call x2, Pallas kernels, cross(): pl.pallas_call(functools.partial(cross_kernel, offsets, picks, len(arrays...  8.01 us
    ppermute x2, waiting for transfers between devices, on_device(): far = lax.ppermute(packed, 'grp', ZHI)  7.31 us
    ppermute x2, starting transfers between devices, on_device(): far = lax.ppermute(packed, 'grp', ZHI)  3.69 us
  transfers between devices with their start and end apart: 34, of which 13 were waited for; matrix products, arithmetic and copies ran while one was open for 0% of the time, Pallas kernels for 21%

profile of v3, /device:TPU:0, one launch (start us, length us, event | category | flops | bytes accessed | tf_op | source)
XLA Modules:
  0.0 150.6 jit_solution(3903449324133358442)
XLA Ops:
  0.0 1.8 %pick.1.refs_0_ = bf16[256,1024]{1,0:T(8,128)(2,1)S(1)} custom-call(s32[8]{0:T(128)} %batches.1, bf16[256,1024]{1,0:T(8,128)(2,1)} %amp_ref.1), custom_call_target="tpu_custom_call" | custom-call | flops 1000 | bytes 1048576 | tf_op jit(solution)/shard_map/pick/pallas_call | solution.py:69
  1.8 2.1 %collective-permute-start.5 = (bf16[256,1024]{1,0:T(8,128)(2,1)S(1)}, bf16[256,1024]{1,0:T(8,128)(2,1)S(1)}, u32[]{:S(2)}, u32[]{:S(2)}) collective-permute-start(bf16[256,1024]{1,0:T(8,128)(2,1)S(1)} %pick.1.refs_0_), channel_id=1, source_target_pairs={{0,4},{1,5},{2,6},{3,7},{4,0},{5,1},{6,2},{7,3},{8,12},{9,13},{10,... | collective-permute-start | bytes 1572872 | tf_op jit(solution)/shard_map/ppermute | solution.py:38
  3.9 1.5 collective-permute-start
  5.4 1.6 %collective-permute-start.1 = (bf16[256,1024]{1,0:T(8,128)(2,1)S(1)}, bf16[256,1024]{1,0:T(8,128)(2,1)S(1)}, u32[]{:S(2)}, u32[]{:S(2)}) collective-permute-start(bf16[256,1024]{1,0:T(8,128)(2,1)S(1)} %pick.1.refs_0_), channel_id=1, source_target_pairs={{0,1},{1,2},{2,3},{3,0},{4,5},{5,6},{6,7},{7,4},{8,9},{9,10},{10,1... | collective-permute-start | bytes 1572872 | tf_op jit(solution)/shard_map/ppermute | solution.py:38
  7.0 1.7 %collective-permute-start.2 = (bf16[256,1024]{1,0:T(8,128)(2,1)S(1)}, bf16[256,1024]{1,0:T(8,128)(2,1)S(1)}, u32[]{:S(2)}, u32[]{:S(2)}) collective-permute-start(bf16[256,1024]{1,0:T(8,128)(2,1)S(1)} %pick.1.refs_0_), channel_id=1, source_target_pairs={{0,24},{1,25},{2,26},{3,27},{4,28},{5,29},{6,30},{7,31},{8,0},{9,1... | collective-permute-start | bytes 1572872 | tf_op jit(solution)/shard_map/ppermute | solution.py:38
  8.8 1.7 %collective-permute-start.3 = (bf16[256,1024]{1,0:T(8,128)(2,1)S(1)}, bf16[256,1024]{1,0:T(8,128)(2,1)S(1)}, u32[]{:S(2)}, u32[]{:S(2)}) collective-permute-start(bf16[256,1024]{1,0:T(8,128)(2,1)S(1)} %pick.1.refs_0_), channel_id=1, source_target_pairs={{0,3},{1,0},{2,1},{3,2},{4,7},{5,4},{6,5},{7,6},{8,11},{9,8},{10,9... | collective-permute-start | bytes 1572872 | tf_op jit(solution)/shard_map/ppermute | solution.py:38
  10.4 5.4 %collective-permute-done.5.refs_0_.refs_1_ = bf16[256,1024]{1,0:T(8,128)(2,1)S(1)} collective-permute-done((bf16[256,1024]{1,0:T(8,128)(2,1)S(1)}, bf16[256,1024]{1,0:T(8,128)(2,1)S(1)}, u32[]{:S(2)}, u32[]{:S(2)}) %collective-permute-start.5) | collective-permute-done | bytes 524320 | tf_op jit(solution)/shard_map/ppermute | solution.py:38
  15.9 2.8 %collective-permute-start.18 = (bf16[256,512]{1,0:T(8,128)(2,1)S(1)}, bf16[256,512]{1,0:T(8,128)(2,1)S(1)}, u32[]{:S(2)}, u32[]{:S(2)}) collective-permute-start(bf16[256,512]{1,0:T(8,128)(2,1)S(1)} %get-tuple-element.30), channel_id=1, source_target_pairs={{0,24},{1,25},{2,26},{3,27},{4,28},{5,29},{6,30},{7,31},{8,0},{9,1... | collective-permute-start | bytes 786440 | tf_op jit(solution)/shard_map/ppermute | solution.py:38
  18.7 1.1 collective-permute-done.1.refs_1_.refs_0_.refs_4_
  19.8 2.0 %collective-permute-done.2.refs_2_.refs_3_ = bf16[256,1024]{1,0:T(8,128)(2,1)S(1)} collective-permute-done((bf16[256,1024]{1,0:T(8,128)(2,1)S(1)}, bf16[256,1024]{1,0:T(8,128)(2,1)S(1)}, u32[]{:S(2)}, u32[]{:S(2)}) %collective-permute-start.2) | collective-permute-done | bytes 524320 | tf_op jit(solution)/shard_map/ppermute | solution.py:38
  21.8 0.1 shard_map.46
  21.9 1.6 %collective-permute-start.14 = (bf16[256,512]{1,0:T(8,128)(2,1)S(1)}, bf16[256,512]{1,0:T(8,128)(2,1)S(1)}, u32[]{:S(2)}, u32[]{:S(2)}) collective-permute-start(bf16[256,512]{1,0:T(8,128)(2,1)S(1)} %get-tuple-element.28), channel_id=1, source_target_pairs={{0,8},{1,9},{2,10},{3,11},{4,12},{5,13},{6,14},{7,15},{8,16},{9,17... | collective-permute-start | bytes 786440 | tf_op jit(solution)/shard_map/ppermute | solution.py:38
  23.5 1.6 %collective-permute-start.15 = (bf16[256,512]{1,0:T(8,128)(2,1)S(1)}, bf16[256,512]{1,0:T(8,128)(2,1)S(1)}, u32[]{:S(2)}, u32[]{:S(2)}) collective-permute-start(bf16[256,512]{1,0:T(8,128)(2,1)S(1)} %get-tuple-element.29), channel_id=1, source_target_pairs={{0,1},{1,2},{2,3},{3,0},{4,5},{5,6},{6,7},{7,4},{8,9},{9,10},{10,1... | collective-permute-start | bytes 786440 | tf_op jit(solution)/shard_map/ppermute | solution.py:38
  25.1 1.0 collective-permute-start.19
  26.1 1.0 collective-permute-start.17
  27.1 2.3 %collective-permute-start.20 = (bf16[256,512]{1,0:T(8,128)(2,1)S(1)}, bf16[256,512]{1,0:T(8,128)(2,1)S(1)}, u32[]{:S(2)}, u32[]{:S(2)}) collective-permute-start(bf16[256,512]{1,0:T(8,128)(2,1)S(1)} %collective-permute-done.18.refs_4_.refs_3_), channel_id=1, source_target_pairs={{0,24},{1,25},{2,26},{3,27},{4,28},{5,29},{6,30},{7,31},{8,0},{9,1... | collective-permute-start | bytes 786440 | tf_op jit(solution)/shard_map/ppermute | solution.py:38
  29.4 3.0 %collective-permute-done.14.refs_0_.refs_8_ = bf16[256,512]{1,0:T(8,128)(2,1)S(1)} collective-permute-done((bf16[256,512]{1,0:T(8,128)(2,1)S(1)}, bf16[256,512]{1,0:T(8,128)(2,1)S(1)}, u32[]{:S(2)}, u32[]{:S(2)}) %collective-permute-start.14) | collective-permute-done | bytes 262176 | tf_op jit(solution)/shard_map/ppermute | solution.py:38
  32.4 1.6 %collective-permute-start.4 = (bf16[256,512]{1,0:T(8,128)(2,1)S(1)}, bf16[256,512]{1,0:T(8,128)(2,1)S(1)}, u32[]{:S(2)}, u32[]{:S(2)}) collective-permute-start(bf16[256,512]{1,0:T(8,128)(2,1)S(1)} %get-tuple-element.21), channel_id=1, source_target_pairs={{0,1},{1,2},{2,3},{3,0},{4,5},{5,6},{6,7},{7,4},{8,9},{9,10},{10,1... | collective-permute-start | bytes 786440 | tf_op jit(solution)/shard_map/ppermute | solution.py:38
  34.0 1.7 %collective-permute-start.6 = (bf16[256,512]{1,0:T(8,128)(2,1)S(1)}, bf16[256,512]{1,0:T(8,128)(2,1)S(1)}, u32[]{:S(2)}, u32[]{:S(2)}) collective-permute-start(bf16[256,512]{1,0:T(8,128)(2,1)S(1)} %get-tuple-element.22), channel_id=1, source_target_pairs={{0,3},{1,0},{2,1},{3,2},{4,7},{5,4},{6,5},{7,6},{8,11},{9,8},{10,9... | collective-permute-start | bytes 786440 | tf_op jit(solution)/shard_map/ppermute | solution.py:38
  35.6 1.6 %collective-permute-done.19.refs_7_.refs_0_ = bf16[256,512]{1,0:T(8,128)(2,1)S(1)} collective-permute-done((bf16[256,512]{1,0:T(8,128)(2,1)S(1)}, bf16[256,512]{1,0:T(8,128)(2,1)S(1)}, u32[]{:S(2)}, u32[]{:S(2)}) %collective-permute-start.19) | collective-permute-done | bytes 262176 | tf_op jit(solution)/shard_map/ppermute | solution.py:38
  37.2 1.6 %collective-permute-start.8 = (bf16[256,512]{1,0:T(8,128)(2,1)S(1)}, bf16[256,512]{1,0:T(8,128)(2,1)S(1)}, u32[]{:S(2)}, u32[]{:S(2)}) collective-permute-start(bf16[256,512]{1,0:T(8,128)(2,1)S(1)} %get-tuple-element.22), channel_id=1, source_target_pairs={{0,1},{1,2},{2,3},{3,0},{4,5},{5,6},{6,7},{7,4},{8,9},{9,10},{10,1... | collective-permute-start | bytes 786440 | tf_op jit(solution)/shard_map/ppermute | solution.py:38
  38.8 1.2 collective-permute-done.17.refs_3_.refs_1_
  40.0 0.6 collective-permute-start.12
  40.6 1.4 collective-permute-start.13
  42.0 0.1 shard_map.56
  42.2 3.1 %collective-permute-start.30 = (bf16[6,256,256]{2,1,0:T(8,128)(2,1)S(1)}, bf16[6,256,256]{2,1,0:T(8,128)(2,1)S(1)}, u32[]{:S(2)}, u32[]{:S(2)}) collective-permute-start(bf16[6,256,256]{2,1,0:T(8,128)(2,1)S(1)} %get-tuple-element.36), channel_id=1, source_target_pairs={{0,3},{1,0},{2,1},{3,2},{4,7},{5,4},{6,5},{7,6},{8,11},{9,8},{10,9... | collective-permute-start | bytes 2359304 | tf_op jit(solution)/shard_map/ppermute | solution.py:38
  45.2 0.5 collective-permute-start.7
  45.7 1.6 %collective-permute-start.21 = (bf16[6,256,256]{2,1,0:T(8,128)(2,1)S(1)}, bf16[6,256,256]{2,1,0:T(8,128)(2,1)S(1)}, u32[]{:S(2)}, u32[]{:S(2)}) collective-permute-start(bf16[6,256,256]{2,1,0:T(8,128)(2,1)S(1)} %get-tuple-element.34), channel_id=1, source_target_pairs={{0,1},{1,2},{2,3},{3,0},{4,5},{5,6},{6,7},{7,4},{8,9},{9,10},{10,1... | collective-permute-start | bytes 2359304 | tf_op jit(solution)/shard_map/ppermute | solution.py:38
  47.3 17.0 %collective-permute-done.7.refs_1_.refs_12_ = bf16[256,512]{1,0:T(8,128)(2,1)S(1)} collective-permute-done((bf16[256,512]{1,0:T(8,128)(2,1)S(1)}, bf16[256,512]{1,0:T(8,128)(2,1)S(1)}, u32[]{:S(2)}, u32[]{:S(2)}) %collective-permute-start.7) | collective-permute-done | bytes 262176 | tf_op jit(solution)/shard_map/ppermute | solution.py:38
  64.3 0.9 collective-permute-start.16
  65.2 0.1 shard_map.48
  65.4 1.0 collective-permute-start.29
  66.4 0.8 collective-permute-start.27
  67.2 2.3 %collective-permute-start.31 = (bf16[6,256,256]{2,1,0:T(8,128)(2,1)S(1)}, bf16[6,256,256]{2,1,0:T(8,128)(2,1)S(1)}, u32[]{:S(2)}, u32[]{:S(2)}) collective-permute-start(bf16[6,256,256]{2,1,0:T(8,128)(2,1)S(1)} %collective-permute-done.30.refs_0_), channel_id=1, source_target_pairs={{0,3},{1,0},{2,1},{3,2},{4,7},{5,4},{6,5},{7,6},{8,11},{9,8},{10,9... | collective-permute-start | bytes 2359304 | tf_op jit(solution)/shard_map/ppermute | solution.py:38
  69.5 5.7 %shard_map.50.refs_6_.refs_13_.refs_3_.refs_1_.refs_2_ = bf16[512,8192]{1,0:T(8,128)(2,1)S(1)} custom-call(s32[8,64]{1,0:T(8,128)} %mask_ref.3, bf16[1024,8192]{1,0:T(8,128)(2,1)} %v_ref.3), custom_call_target="tpu_custom_call" | custom-call | flops 1000 | bytes 8388608 | tf_op jit(solution)/shard_map/pallas_call | solution.py:109
  75.2 5.7 %shard_map.51.refs_7_.refs_14_.refs_4_.refs_2_.refs_3_ = bf16[512,8192]{1,0:T(8,128)(2,1)S(1)} custom-call(s32[8,64]{1,0:T(8,128)} %mask_ref.3, bf16[1024,8192]{1,0:T(8,128)(2,1)} %v_ref.3), custom_call_target="tpu_custom_call" | custom-call | flops 1000 | bytes 8388608 | tf_op jit(solution)/shard_map/pallas_call | solution.py:109
  80.9 2.0 %collective-permute-start.22 = (bf16[6,256,256]{2,1,0:T(8,128)(2,1)S(1)}, bf16[6,256,256]{2,1,0:T(8,128)(2,1)S(1)}, u32[]{:S(2)}, u32[]{:S(2)}) collective-permute-start(bf16[6,256,256]{2,1,0:T(8,128)(2,1)S(1)} %get-tuple-element.34), channel_id=1, source_target_pairs={{0,3},{1,0},{2,1},{3,2},{4,7},{5,4},{6,5},{7,6},{8,11},{9,8},{10,9... | collective-permute-start | bytes 2359304 | tf_op jit(solution)/shard_map/ppermute | solution.py:38
  82.9 0.1 collective-permute-start.23
  83.0 3.5 %shard_map.53.refs_15_ = f32[1024,1024]{1,0:T(8,128)S(1)} custom-call(bf16[256,1024]{1,0:T(8,128)(2,1)S(1)} %pick.1.refs_0_, bf16[256,1024]{1,0:T(8,128)(2,1)S(1)} %collective-permute-done.5.refs_0_.refs_1_, bf16[256,1024]{1,0:T(8,128)(2,1)S(1)} %collective-permute-done.refs_0_.refs_2_, bf16[256,1024]{1,0:T(8,128)(2,1)S(1)} %collective-permute-done.2.refs_2_.refs_3_, ...), custom_call_target="tpu_custom_call" | custom-call | flops 3221225472 | bytes 6291456 | tf_op jit(solution)/shard_map/pallas_call | solution.py:206
  86.5 1.8 %collective-permute-start.26 = (bf16[6,256,256]{2,1,0:T(8,128)(2,1)S(1)}, bf16[6,256,256]{2,1,0:T(8,128)(2,1)S(1)}, u32[]{:S(2)}, u32[]{:S(2)}) collective-permute-start(bf16[6,256,256]{2,1,0:T(8,128)(2,1)S(1)} %get-tuple-element.35), channel_id=1, source_target_pairs={{0,8},{1,9},{2,10},{3,11},{4,12},{5,13},{6,14},{7,15},{8,16},{9,17... | collective-permute-start | bytes 2359304 | tf_op jit(solution)/shard_map/ppermute | solution.py:38
  88.3 0.1 collective-permute-start.9
  88.4 4.6 %shard_map.54.refs_5_.refs_3_ = f32[1024,1024]{1,0:T(8,128)S(1)} custom-call(bf16[2,256,512]{2,1,0:T(8,128)(2,1)S(1)} %collective-permute-done.12.refs_0_, bf16[2,256,512]{2,1,0:T(8,128)(2,1)S(1)} %collective-permute-done.13.refs_1_, bf16[2,256,512]{2,1,0:T(8,128)(2,1)S(1)} %collective-permute-done.16.refs_2_, ...), custom_call_target="tpu_custom_call" | custom-call | flops 4294967296 | bytes 8388608 | tf_op jit(solution)/shard_map/pallas_call | solution.py:206
  93.0 1.0 shard_map.61.refs_4_
  94.0 3.2 %collective-permute-start.28 = (bf16[6,256,256]{2,1,0:T(8,128)(2,1)S(1)}, bf16[6,256,256]{2,1,0:T(8,128)(2,1)S(1)}, u32[]{:S(2)}, u32[]{:S(2)}) collective-permute-start(bf16[6,256,256]{2,1,0:T(8,128)(2,1)S(1)} %collective-permute-done.27.refs_0_), channel_id=1, source_target_pairs={{0,24},{1,25},{2,26},{3,27},{4,28},{5,29},{6,30},{7,31},{8,0},{9,1... | collective-permute-start | bytes 2359304 | tf_op jit(solution)/shard_map/ppermute | solution.py:38
  97.2 1.8 %shard_map.62 = f32[1024,256]{1,0:T(8,128)S(1)} custom-call(bf16[6,256,256]{2,1,0:T(8,128)(2,1)S(1)} %collective-permute-done.29.refs_0_, bf16[6,256,256]{2,1,0:T(8,128)(2,1)S(1)} %collective-permute-done.31.refs_1_, bf16[512,8192]{1,0:T(8,128)(2,1)S(1)} %shard_map.50.refs_6_.refs_13_.refs_3_.refs_1_.refs_2_, ...), custom_call_target="tpu_custom_call" | custom-call | flops 1610612736 | bytes 9437184 | tf_op jit(solution)/shard_map/pallas_call | solution.py:239
  99.0 0.1 collective-permute-start.32
  99.1 0.2 collective-permute-done.23.refs_2_
  99.3 2.6 %shard_map.58 = f32[1024,256]{1,0:T(8,128)S(1)} custom-call(bf16[6,256,256]{2,1,0:T(8,128)(2,1)S(1)} %collective-permute-done.21.refs_0_, bf16[6,256,256]{2,1,0:T(8,128)(2,1)S(1)} %collective-permute-done.22.refs_1_, bf16[6,256,256]{2,1,0:T(8,128)(2,1)S(1)} %collective-permute-done.23.refs_2_, ...), custom_call_target="tpu_custom_call" | custom-call | flops 2415919104 | bytes 9437184 | tf_op jit(solution)/shard_map/pallas_call | solution.py:239
  101.9 0.3 collective-permute-start.24
  102.3 5.9 %collective-permute-done.26.refs_0_ = bf16[6,256,256]{2,1,0:T(8,128)(2,1)S(1)} collective-permute-done((bf16[6,256,256]{2,1,0:T(8,128)(2,1)S(1)}, bf16[6,256,256]{2,1,0:T(8,128)(2,1)S(1)}, u32[]{:S(2)}, u32[]{:S(2)}) %collective-permute-start.26) | collective-permute-done | bytes 786464 | tf_op jit(solution)/shard_map/ppermute | solution.py:38
  108.2 0.0 collective-permute-start.10
  108.2 12.9 %collective-permute-done.9.refs_0_ = bf16[6,256,256]{2,1,0:T(8,128)(2,1)S(1)} collective-permute-done((bf16[6,256,256]{2,1,0:T(8,128)(2,1)S(1)}, bf16[6,256,256]{2,1,0:T(8,128)(2,1)S(1)}, u32[]{:S(2)}, u32[]{:S(2)}) %collective-permute-start.9) | collective-permute-done | bytes 786464 | tf_op jit(solution)/shard_map/ppermute | solution.py:38
  121.1 1.8 %collective-permute-start.11 = (bf16[6,256,256]{2,1,0:T(8,128)(2,1)S(1)}, bf16[6,256,256]{2,1,0:T(8,128)(2,1)S(1)}, u32[]{:S(2)}, u32[]{:S(2)}) collective-permute-start(bf16[6,256,256]{2,1,0:T(8,128)(2,1)S(1)} %collective-permute-done.9.refs_0_), channel_id=1, source_target_pairs={{0,8},{1,9},{2,10},{3,11},{4,12},{5,13},{6,14},{7,15},{8,16},{9,17... | collective-permute-start | bytes 2359304 | tf_op jit(solution)/shard_map/ppermute | solution.py:38
  122.9 1.0 shard_map.59.refs_4_
  123.9 1.8 %shard_map.60.mine.refs_3_ = f32[1024,256]{1,0:T(8,128)S(1)} custom-call(bf16[6,256,256]{2,1,0:T(8,128)(2,1)S(1)} %collective-permute-done.26.refs_0_, bf16[6,256,256]{2,1,0:T(8,128)(2,1)S(1)} %collective-permute-done.28.refs_1_, bf16[512,8192]{1,0:T(8,128)(2,1)S(1)} %shard_map.50.refs_6_.refs_13_.refs_3_.refs_1_.refs_2_, ...), custom_call_target="tpu_custom_call" | custom-call | flops 1610612736 | bytes 9437184 | tf_op jit(solution)/shard_map/pallas_call | solution.py:239
  125.7 9.8 %collective-permute-done.11.refs_2_ = bf16[6,256,256]{2,1,0:T(8,128)(2,1)S(1)} collective-permute-done((bf16[6,256,256]{2,1,0:T(8,128)(2,1)S(1)}, bf16[6,256,256]{2,1,0:T(8,128)(2,1)S(1)}, u32[]{:S(2)}, u32[]{:S(2)}) %collective-permute-start.11) | collective-permute-done | bytes 786464 | tf_op jit(solution)/shard_map/ppermute | solution.py:38
  135.5 2.6 %shard_map.55.mine.refs_0_ = f32[1024,256]{1,0:T(8,128)S(1)} custom-call(bf16[6,256,256]{2,1,0:T(8,128)(2,1)S(1)} %collective-permute-done.9.refs_0_, bf16[6,256,256]{2,1,0:T(8,128)(2,1)S(1)} %collective-permute-done.10.refs_1_, bf16[6,256,256]{2,1,0:T(8,128)(2,1)S(1)} %collective-permute-done.11.refs_2_, ...), custom_call_target="tpu_custom_call" | custom-call | flops 2415919104 | bytes 9437184 | tf_op jit(solution)/shard_map/pallas_call | solution.py:239
  138.2 0.2 code.3
  138.3 2.9 %collective-permute-start.33 = (s16[1088,128]{1,0:T(8,128)(2,1)S(1)}, s16[1088,128]{1,0:T(8,128)(2,1)S(1)}, u32[]{:S(2)}, u32[]{:S(2)}) collective-permute-start(s16[1088,128]{1,0:T(8,128)(2,1)S(1)} %code.3), channel_id=1, source_target_pairs={{0,64},{32,96},{64,0},{96,32},{1,65},{33,97},{65,1},{97,33},{2,66}... | collective-permute-start | bytes 835592 | tf_op jit(solution)/shard_map/ppermute | solution.py:368
  141.2 0.2 code.2
  141.4 0.8 collective-permute-start.25
  142.2 4.3 %collective-permute-done.33.refs_5_ = s16[1088,128]{1,0:T(8,128)(2,1)S(1)} collective-permute-done((s16[1088,128]{1,0:T(8,128)(2,1)S(1)}, s16[1088,128]{1,0:T(8,128)(2,1)S(1)}, u32[]{:S(2)}, u32[]{:S(2)}) %collective-permute-start.33) | collective-permute-done | bytes 278560 | tf_op jit(solution)/shard_map/ppermute | solution.py:368
  146.5 3.0 %collective-permute-done.25.refs_2_ = s16[1088,128]{1,0:T(8,128)(2,1)S(1)} collective-permute-done((s16[1088,128]{1,0:T(8,128)(2,1)S(1)}, s16[1088,128]{1,0:T(8,128)(2,1)S(1)}, u32[]{:S(2)}, u32[]{:S(2)}) %collective-permute-start.25) | collective-permute-done | bytes 278560 | tf_op jit(solution)/shard_map/ppermute | solution.py:368
  149.5 1.1 finish.1
  (25 shorter events, 0.2 us)
Async XLA Ops:
  1.8 14.0 %collective-permute-start.5 = (bf16[256,1024]{1,0:T(8,128)(2,1)S(1)}, bf16[256,1024]{1,0:T(8,128)(2,1)S(1)}, u32[]{:S(2)}, u32[]{:S(2)}) collective-permute-start(bf16[256,1024]{1,0:T(8,128)(2,1)S(1)} %pick.1.refs_0_), channel_id=1, source_target_pairs={{0,4},{1,5},{2,6},{3,7},{4,0},{5,1},{6,2},{7,3},{8,12},{9,13},{10,... | collective-permute-start | bytes 1572872 | tf_op jit(solution)/shard_map/ppermute | solution.py:38
  3.9 14.8 %collective-permute-start = (bf16[256,1024]{1,0:T(8,128)(2,1)S(1)}, bf16[256,1024]{1,0:T(8,128)(2,1)S(1)}, u32[]{:S(2)}, u32[]{:S(2)}) collective-permute-start(bf16[256,1024]{1,0:T(8,128)(2,1)S(1)} %pick.1.refs_0_), channel_id=1, source_target_pairs={{0,8},{1,9},{2,10},{3,11},{4,12},{5,13},{6,14},{7,15},{8,16},{9,17... | collective-permute-start | bytes 1572872 | tf_op jit(solution)/shard_map/ppermute | solution.py:38
  5.4 14.4 %collective-permute-start.1 = (bf16[256,1024]{1,0:T(8,128)(2,1)S(1)}, bf16[256,1024]{1,0:T(8,128)(2,1)S(1)}, u32[]{:S(2)}, u32[]{:S(2)}) collective-permute-start(bf16[256,1024]{1,0:T(8,128)(2,1)S(1)} %pick.1.refs_0_), channel_id=1, source_target_pairs={{0,1},{1,2},{2,3},{3,0},{4,5},{5,6},{6,7},{7,4},{8,9},{9,10},{10,1... | collective-permute-start | bytes 1572872 | tf_op jit(solution)/shard_map/ppermute | solution.py:38
  7.0 14.8 %collective-permute-start.2 = (bf16[256,1024]{1,0:T(8,128)(2,1)S(1)}, bf16[256,1024]{1,0:T(8,128)(2,1)S(1)}, u32[]{:S(2)}, u32[]{:S(2)}) collective-permute-start(bf16[256,1024]{1,0:T(8,128)(2,1)S(1)} %pick.1.refs_0_), channel_id=1, source_target_pairs={{0,24},{1,25},{2,26},{3,27},{4,28},{5,29},{6,30},{7,31},{8,0},{9,1... | collective-permute-start | bytes 1572872 | tf_op jit(solution)/shard_map/ppermute | solution.py:38
  8.8 13.1 %collective-permute-start.3 = (bf16[256,1024]{1,0:T(8,128)(2,1)S(1)}, bf16[256,1024]{1,0:T(8,128)(2,1)S(1)}, u32[]{:S(2)}, u32[]{:S(2)}) collective-permute-start(bf16[256,1024]{1,0:T(8,128)(2,1)S(1)} %pick.1.refs_0_), channel_id=1, source_target_pairs={{0,3},{1,0},{2,1},{3,2},{4,7},{5,4},{6,5},{7,6},{8,11},{9,8},{10,9... | collective-permute-start | bytes 1572872 | tf_op jit(solution)/shard_map/ppermute | solution.py:38
  15.9 11.2 %collective-permute-start.18 = (bf16[256,512]{1,0:T(8,128)(2,1)S(1)}, bf16[256,512]{1,0:T(8,128)(2,1)S(1)}, u32[]{:S(2)}, u32[]{:S(2)}) collective-permute-start(bf16[256,512]{1,0:T(8,128)(2,1)S(1)} %get-tuple-element.30), channel_id=1, source_target_pairs={{0,24},{1,25},{2,26},{3,27},{4,28},{5,29},{6,30},{7,31},{8,0},{9,1... | collective-permute-start | bytes 786440 | tf_op jit(solution)/shard_map/ppermute | solution.py:38
  21.9 10.5 %collective-permute-start.14 = (bf16[256,512]{1,0:T(8,128)(2,1)S(1)}, bf16[256,512]{1,0:T(8,128)(2,1)S(1)}, u32[]{:S(2)}, u32[]{:S(2)}) collective-permute-start(bf16[256,512]{1,0:T(8,128)(2,1)S(1)} %get-tuple-element.28), channel_id=1, source_target_pairs={{0,8},{1,9},{2,10},{3,11},{4,12},{5,13},{6,14},{7,15},{8,16},{9,17... | collective-permute-start | bytes 786440 | tf_op jit(solution)/shard_map/ppermute | solution.py:38
  23.5 10.5 %collective-permute-start.15 = (bf16[256,512]{1,0:T(8,128)(2,1)S(1)}, bf16[256,512]{1,0:T(8,128)(2,1)S(1)}, u32[]{:S(2)}, u32[]{:S(2)}) collective-permute-start(bf16[256,512]{1,0:T(8,128)(2,1)S(1)} %get-tuple-element.29), channel_id=1, source_target_pairs={{0,1},{1,2},{2,3},{3,0},{4,5},{5,6},{6,7},{7,4},{8,9},{9,10},{10,1... | collective-permute-start | bytes 786440 | tf_op jit(solution)/shard_map/ppermute | solution.py:38
  25.1 12.1 %collective-permute-start.19 = (bf16[256,512]{1,0:T(8,128)(2,1)S(1)}, bf16[256,512]{1,0:T(8,128)(2,1)S(1)}, u32[]{:S(2)}, u32[]{:S(2)}) collective-permute-start(bf16[256,512]{1,0:T(8,128)(2,1)S(1)} %get-tuple-element.31), channel_id=1, source_target_pairs={{0,8},{1,9},{2,10},{3,11},{4,12},{5,13},{6,14},{7,15},{8,16},{9,17... | collective-permute-start | bytes 786440 | tf_op jit(solution)/shard_map/ppermute | solution.py:38
  26.1 13.9 %collective-permute-start.17 = (bf16[256,512]{1,0:T(8,128)(2,1)S(1)}, bf16[256,512]{1,0:T(8,128)(2,1)S(1)}, u32[]{:S(2)}, u32[]{:S(2)}) collective-permute-start(bf16[256,512]{1,0:T(8,128)(2,1)S(1)} %get-tuple-element.30), channel_id=1, source_target_pairs={{0,8},{1,9},{2,10},{3,11},{4,12},{5,13},{6,14},{7,15},{8,16},{9,17... | collective-permute-start | bytes 786440 | tf_op jit(solution)/shard_map/ppermute | solution.py:38
  27.1 13.5 %collective-permute-start.20 = (bf16[256,512]{1,0:T(8,128)(2,1)S(1)}, bf16[256,512]{1,0:T(8,128)(2,1)S(1)}, u32[]{:S(2)}, u32[]{:S(2)}) collective-permute-start(bf16[256,512]{1,0:T(8,128)(2,1)S(1)} %collective-permute-done.18.refs_4_.refs_3_), channel_id=1, source_target_pairs={{0,24},{1,25},{2,26},{3,27},{4,28},{5,29},{6,30},{7,31},{8,0},{9,1... | collective-permute-start | bytes 786440 | tf_op jit(solution)/shard_map/ppermute | solution.py:38
  32.4 9.8 %collective-permute-start.4 = (bf16[256,512]{1,0:T(8,128)(2,1)S(1)}, bf16[256,512]{1,0:T(8,128)(2,1)S(1)}, u32[]{:S(2)}, u32[]{:S(2)}) collective-permute-start(bf16[256,512]{1,0:T(8,128)(2,1)S(1)} %get-tuple-element.21), channel_id=1, source_target_pairs={{0,1},{1,2},{2,3},{3,0},{4,5},{5,6},{6,7},{7,4},{8,9},{9,10},{10,1... | collective-permute-start | bytes 786440 | tf_op jit(solution)/shard_map/ppermute | solution.py:38
  34.0 11.3 %collective-permute-start.6 = (bf16[256,512]{1,0:T(8,128)(2,1)S(1)}, bf16[256,512]{1,0:T(8,128)(2,1)S(1)}, u32[]{:S(2)}, u32[]{:S(2)}) collective-permute-start(bf16[256,512]{1,0:T(8,128)(2,1)S(1)} %get-tuple-element.22), channel_id=1, source_target_pairs={{0,3},{1,0},{2,1},{3,2},{4,7},{5,4},{6,5},{7,6},{8,11},{9,8},{10,9... | collective-permute-start | bytes 786440 | tf_op jit(solution)/shard_map/ppermute | solution.py:38
  37.2 8.5 %collective-permute-start.8 = (bf16[256,512]{1,0:T(8,128)(2,1)S(1)}, bf16[256,512]{1,0:T(8,128)(2,1)S(1)}, u32[]{:S(2)}, u32[]{:S(2)}) collective-permute-start(bf16[256,512]{1,0:T(8,128)(2,1)S(1)} %get-tuple-element.22), channel_id=1, source_target_pairs={{0,1},{1,2},{2,3},{3,0},{4,5},{5,6},{6,7},{7,4},{8,9},{9,10},{10,1... | collective-permute-start | bytes 786440 | tf_op jit(solution)/shard_map/ppermute | solution.py:38
  40.0 25.3 %collective-permute-start.12 = (bf16[2,256,512]{2,1,0:T(8,128)(2,1)S(1)}, bf16[2,256,512]{2,1,0:T(8,128)(2,1)S(1)}, u32[]{:S(2)}, u32[]{:S(2)}) collective-permute-start(bf16[2,256,512]{2,1,0:T(8,128)(2,1)S(1)} %get-tuple-element.26), channel_id=1, source_target_pairs={{0,4},{1,5},{2,6},{3,7},{4,0},{5,1},{6,2},{7,3},{8,12},{9,13},{10,... | collective-permute-start | bytes 1572872 | tf_op jit(solution)/shard_map/ppermute | solution.py:38
  40.6 25.7 %collective-permute-start.13 = (bf16[2,256,512]{2,1,0:T(8,128)(2,1)S(1)}, bf16[2,256,512]{2,1,0:T(8,128)(2,1)S(1)}, u32[]{:S(2)}, u32[]{:S(2)}) collective-permute-start(bf16[2,256,512]{2,1,0:T(8,128)(2,1)S(1)} %get-tuple-element.27), channel_id=1, source_target_pairs={{0,4},{1,5},{2,6},{3,7},{4,0},{5,1},{6,2},{7,3},{8,12},{9,13},{10,... | collective-permute-start | bytes 1572872 | tf_op jit(solution)/shard_map/ppermute | solution.py:38
  42.2 25.0 %collective-permute-start.30 = (bf16[6,256,256]{2,1,0:T(8,128)(2,1)S(1)}, bf16[6,256,256]{2,1,0:T(8,128)(2,1)S(1)}, u32[]{:S(2)}, u32[]{:S(2)}) collective-permute-start(bf16[6,256,256]{2,1,0:T(8,128)(2,1)S(1)} %get-tuple-element.36), channel_id=1, source_target_pairs={{0,3},{1,0},{2,1},{3,2},{4,7},{5,4},{6,5},{7,6},{8,11},{9,8},{10,9... | collective-permute-start | bytes 2359304 | tf_op jit(solution)/shard_map/ppermute | solution.py:38
  45.2 19.1 %collective-permute-start.7 = (bf16[256,512]{1,0:T(8,128)(2,1)S(1)}, bf16[256,512]{1,0:T(8,128)(2,1)S(1)}, u32[]{:S(2)}, u32[]{:S(2)}) collective-permute-start(bf16[256,512]{1,0:T(8,128)(2,1)S(1)} %collective-permute-done.6.refs_3_.refs_6_), channel_id=1, source_target_pairs={{0,3},{1,0},{2,1},{3,2},{4,7},{5,4},{6,5},{7,6},{8,11},{9,8},{10,9... | collective-permute-start | bytes 786440 | tf_op jit(solution)/shard_map/ppermute | solution.py:38
  45.7 37.2 %collective-permute-start.21 = (bf16[6,256,256]{2,1,0:T(8,128)(2,1)S(1)}, bf16[6,256,256]{2,1,0:T(8,128)(2,1)S(1)}, u32[]{:S(2)}, u32[]{:S(2)}) collective-permute-start(bf16[6,256,256]{2,1,0:T(8,128)(2,1)S(1)} %get-tuple-element.34), channel_id=1, source_target_pairs={{0,1},{1,2},{2,3},{3,0},{4,5},{5,6},{6,7},{7,4},{8,9},{9,10},{10,1... | collective-permute-start | bytes 2359304 | tf_op jit(solution)/shard_map/ppermute | solution.py:38
  64.3 16.6 %collective-permute-start.16 = (bf16[2,256,512]{2,1,0:T(8,128)(2,1)S(1)}, bf16[2,256,512]{2,1,0:T(8,128)(2,1)S(1)}, u32[]{:S(2)}, u32[]{:S(2)}) collective-permute-start(bf16[2,256,512]{2,1,0:T(8,128)(2,1)S(1)} %shard_map.52), channel_id=1, source_target_pairs={{0,4},{1,5},{2,6},{3,7},{4,0},{5,1},{6,2},{7,3},{8,12},{9,13},{10,... | collective-permute-start | bytes 1572872 | tf_op jit(solution)/shard_map/ppermute | solution.py:38
  65.4 21.1 %collective-permute-start.29 = (bf16[6,256,256]{2,1,0:T(8,128)(2,1)S(1)}, bf16[6,256,256]{2,1,0:T(8,128)(2,1)S(1)}, u32[]{:S(2)}, u32[]{:S(2)}) collective-permute-start(bf16[6,256,256]{2,1,0:T(8,128)(2,1)S(1)} %get-tuple-element.36), channel_id=1, source_target_pairs={{0,1},{1,2},{2,3},{3,0},{4,5},{5,6},{6,7},{7,4},{8,9},{9,10},{10,1... | collective-permute-start | bytes 2359304 | tf_op jit(solution)/shard_map/ppermute | solution.py:38
  66.4 21.9 %collective-permute-start.27 = (bf16[6,256,256]{2,1,0:T(8,128)(2,1)S(1)}, bf16[6,256,256]{2,1,0:T(8,128)(2,1)S(1)}, u32[]{:S(2)}, u32[]{:S(2)}) collective-permute-start(bf16[6,256,256]{2,1,0:T(8,128)(2,1)S(1)} %get-tuple-element.35), channel_id=1, source_target_pairs={{0,24},{1,25},{2,26},{3,27},{4,28},{5,29},{6,30},{7,31},{8,0},{9,1... | collective-permute-start | bytes 2359304 | tf_op jit(solution)/shard_map/ppermute | solution.py:38
  67.2 26.8 %collective-permute-start.31 = (bf16[6,256,256]{2,1,0:T(8,128)(2,1)S(1)}, bf16[6,256,256]{2,1,0:T(8,128)(2,1)S(1)}, u32[]{:S(2)}, u32[]{:S(2)}) collective-permute-start(bf16[6,256,256]{2,1,0:T(8,128)(2,1)S(1)} %collective-permute-done.30.refs_0_), channel_id=1, source_target_pairs={{0,3},{1,0},{2,1},{3,2},{4,7},{5,4},{6,5},{7,6},{8,11},{9,8},{10,9... | collective-permute-start | bytes 2359304 | tf_op jit(solution)/shard_map/ppermute | solution.py:38
  80.9 18.1 %collective-permute-start.22 = (bf16[6,256,256]{2,1,0:T(8,128)(2,1)S(1)}, bf16[6,256,256]{2,1,0:T(8,128)(2,1)S(1)}, u32[]{:S(2)}, u32[]{:S(2)}) collective-permute-start(bf16[6,256,256]{2,1,0:T(8,128)(2,1)S(1)} %get-tuple-element.34), channel_id=1, source_target_pairs={{0,3},{1,0},{2,1},{3,2},{4,7},{5,4},{6,5},{7,6},{8,11},{9,8},{10,9... | collective-permute-start | bytes 2359304 | tf_op jit(solution)/shard_map/ppermute | solution.py:38
  82.9 16.4 %collective-permute-start.23 = (bf16[6,256,256]{2,1,0:T(8,128)(2,1)S(1)}, bf16[6,256,256]{2,1,0:T(8,128)(2,1)S(1)}, u32[]{:S(2)}, u32[]{:S(2)}) collective-permute-start(bf16[6,256,256]{2,1,0:T(8,128)(2,1)S(1)} %collective-permute-done.21.refs_0_), channel_id=1, source_target_pairs={{0,1},{1,2},{2,3},{3,0},{4,5},{5,6},{6,7},{7,4},{8,9},{9,10},{10,1... | collective-permute-start | bytes 2359304 | tf_op jit(solution)/shard_map/ppermute | solution.py:38
  86.5 21.7 %collective-permute-start.26 = (bf16[6,256,256]{2,1,0:T(8,128)(2,1)S(1)}, bf16[6,256,256]{2,1,0:T(8,128)(2,1)S(1)}, u32[]{:S(2)}, u32[]{:S(2)}) collective-permute-start(bf16[6,256,256]{2,1,0:T(8,128)(2,1)S(1)} %get-tuple-element.35), channel_id=1, source_target_pairs={{0,8},{1,9},{2,10},{3,11},{4,12},{5,13},{6,14},{7,15},{8,16},{9,17... | collective-permute-start | bytes 2359304 | tf_op jit(solution)/shard_map/ppermute | solution.py:38
  88.3 32.8 %collective-permute-start.9 = (bf16[6,256,256]{2,1,0:T(8,128)(2,1)S(1)}, bf16[6,256,256]{2,1,0:T(8,128)(2,1)S(1)}, u32[]{:S(2)}, u32[]{:S(2)}) collective-permute-start(bf16[6,256,256]{2,1,0:T(8,128)(2,1)S(1)} %get-tuple-element.25), channel_id=1, source_target_pairs={{0,8},{1,9},{2,10},{3,11},{4,12},{5,13},{6,14},{7,15},{8,16},{9,17... | collective-permute-start | bytes 2359304 | tf_op jit(solution)/shard_map/ppermute | solution.py:38
  94.0 29.9 %collective-permute-start.28 = (bf16[6,256,256]{2,1,0:T(8,128)(2,1)S(1)}, bf16[6,256,256]{2,1,0:T(8,128)(2,1)S(1)}, u32[]{:S(2)}, u32[]{:S(2)}) collective-permute-start(bf16[6,256,256]{2,1,0:T(8,128)(2,1)S(1)} %collective-permute-done.27.refs_0_), channel_id=1, source_target_pairs={{0,24},{1,25},{2,26},{3,27},{4,28},{5,29},{6,30},{7,31},{8,0},{9,1... | collective-permute-start | bytes 2359304 | tf_op jit(solution)/shard_map/ppermute | solution.py:38
  99.0 39.2 %collective-permute-start.32 = (f32[1024,256]{1,0:T(8,128)S(1)}, f32[1024,256]{1,0:T(8,128)S(1)}, u32[]{:S(2)}, u32[]{:S(2)}) collective-permute-start(f32[1024,256]{1,0:T(8,128)S(1)} %shard_map.62), channel_id=1, source_target_pairs={{0,32},{32,0},{64,96},{96,64},{1,33},{33,1},{65,97},{97,65},{2,34}... | collective-permute-start | bytes 3145736 | tf_op jit(solution)/shard_map/ppermute | solution.py:361
  101.9 39.3 %collective-permute-start.24 = (f32[1024,256]{1,0:T(8,128)S(1)}, f32[1024,256]{1,0:T(8,128)S(1)}, u32[]{:S(2)}, u32[]{:S(2)}) collective-permute-start(f32[1024,256]{1,0:T(8,128)S(1)} %shard_map.58), channel_id=1, source_target_pairs={{0,32},{32,0},{64,96},{96,64},{1,33},{33,1},{65,97},{97,65},{2,34}... | collective-permute-start | bytes 3145736 | tf_op jit(solution)/shard_map/ppermute | solution.py:361
  108.2 17.5 %collective-permute-start.10 = (bf16[6,256,256]{2,1,0:T(8,128)(2,1)S(1)}, bf16[6,256,256]{2,1,0:T(8,128)(2,1)S(1)}, u32[]{:S(2)}, u32[]{:S(2)}) collective-permute-start(bf16[6,256,256]{2,1,0:T(8,128)(2,1)S(1)} %get-tuple-element.25), channel_id=1, source_target_pairs={{0,24},{1,25},{2,26},{3,27},{4,28},{5,29},{6,30},{7,31},{8,0},{9,1... | collective-permute-start | bytes 2359304 | tf_op jit(solution)/shard_map/ppermute | solution.py:38
  121.1 14.4 %collective-permute-start.11 = (bf16[6,256,256]{2,1,0:T(8,128)(2,1)S(1)}, bf16[6,256,256]{2,1,0:T(8,128)(2,1)S(1)}, u32[]{:S(2)}, u32[]{:S(2)}) collective-permute-start(bf16[6,256,256]{2,1,0:T(8,128)(2,1)S(1)} %collective-permute-done.9.refs_0_), channel_id=1, source_target_pairs={{0,8},{1,9},{2,10},{3,11},{4,12},{5,13},{6,14},{7,15},{8,16},{9,17... | collective-permute-start | bytes 2359304 | tf_op jit(solution)/shard_map/ppermute | solution.py:38
  138.3 8.1 %collective-permute-start.33 = (s16[1088,128]{1,0:T(8,128)(2,1)S(1)}, s16[1088,128]{1,0:T(8,128)(2,1)S(1)}, u32[]{:S(2)}, u32[]{:S(2)}) collective-permute-start(s16[1088,128]{1,0:T(8,128)(2,1)S(1)} %code.3), channel_id=1, source_target_pairs={{0,64},{32,96},{64,0},{96,32},{1,65},{33,97},{65,1},{97,33},{2,66}... | collective-permute-start | bytes 835592 | tf_op jit(solution)/shard_map/ppermute | solution.py:368
  141.4 8.1 %collective-permute-start.25 = (s16[1088,128]{1,0:T(8,128)(2,1)S(1)}, s16[1088,128]{1,0:T(8,128)(2,1)S(1)}, u32[]{:S(2)}, u32[]{:S(2)}) collective-permute-start(s16[1088,128]{1,0:T(8,128)(2,1)S(1)} %code.2), channel_id=1, source_target_pairs={{0,64},{32,96},{64,0},{96,32},{1,65},{33,97},{65,1},{97,33},{2,66}... | collective-permute-start | bytes 835592 | tf_op jit(solution)/shard_map/ppermute | solution.py:368

commit v4 on v3

--- a/solution.py
+++ b/solution.py
@@ -274,31 +274,34 @@
     )(mine, got)
 
 
+def total(mine, got, far, at):
+    rows = mine.shape[0]
+    spot = rows + at.start // BLOCK * (TAIL // 8)
+    scale = jnp.exp2(far[spot : spot + 1, :].astype(jnp.int32).astype(F32))
+    other = far[at, :].astype(jnp.int32).astype(F32) * scale
+    return (mine[at, :BATCH] + got[at, :BATCH] + other).T.astype(BF16)
+
+
 def finish_kernel(*refs):
-    out_ref = refs[-1]
-    for k in range(2):
-        mine, got, far = refs[3 * k : 3 * k + 3]
-        rows = mine.shape[0]
-        powers = far[rows:, :].astype(jnp.int32).astype(F32)
-        for r in range(rows // BLOCK):
-            at = slice(r * BLOCK, (r + 1) * BLOCK)
-            scale = jnp.exp2(powers[r * (TAIL // 8) : r * (TAIL // 8) + 1])
-            other = far[at, :].astype(jnp.int32).astype(F32) * scale
-            total = mine[at, :BATCH] + got[at, :BATCH] + other
-            out_ref[k * BATCH : (k + 1) * BATCH, at] = total.T.astype(BF16)
-
-
-def finish(parts):
+    out_ref, (mine, got, far) = refs[-1], refs[-4:-1]
+    first = out_ref.shape[0] - BATCH
+    if first:
+        out_ref[:first, :] = refs[0][...]
+    for r in range(mine.shape[0] // BLOCK):
+        at = slice(r * BLOCK, (r + 1) * BLOCK)
+        out_ref[first:, at] = total(mine, got, far, at)
+
+
+def finish(parts, before=()):
     rows = parts[0].shape[0]
     return pl.pallas_call(
         finish_kernel,
-        out_shape=jax.ShapeDtypeStruct((2 * BATCH, rows), BF16),
-        in_specs=vmem(6),
+        out_shape=jax.ShapeDtypeStruct(((1 + len(before)) * BATCH, rows), BF16),
+        in_specs=vmem(3 + len(before)),
         out_specs=pl.BlockSpec(memory_space=pltpu.VMEM),
         cost_estimate=pl.CostEstimate(flops=1000000, bytes_accessed=3 << 20, transcendentals=0),
         compiler_params=params(),
-        name="finish",
-    )(*parts)
+    )(*before, *parts)
 
 
 def on_device(integrals, block_mask, amplitudes, pair_batches):
@@ -367,7 +370,7 @@
         packed = code(mine, got)
         far = lax.ppermute(packed, "grp", ZHI)
         parts += [mine, got, far]
-    return finish(parts)
+    return finish(parts[3:], [finish(parts[:3])])
 
 
 def solution(mesh):

time: 151 us -> 151 us (level)
  waiting for transfers between devices: 67.6 us -> 70.5 us
  starting transfers between devices: 48.9 us -> 46.4 us
    ppermute x30, starting transfers between devices: 44.8 us -> 42 us  [send(): return lax.ppermute(array, 'blk', pairs)]
    ppermute x30, waiting for transfers between devices: 60.3 us -> 62.7 us  [send(): return lax.ppermute(array, 'blk', pairs)]
  transfers between devices with their start and end apart: 34 -> 34, of which waited for: 13 -> 15; matrix products, arithmetic and copies ran while one was open for 0% -> 0% of each run, Pallas kernels for 21% -> 21%
where the time goes in v4:
time: 151 us
  waiting for transfers between devices  70.5 us (47%)
  starting transfers between devices  46.4 us (31%)
  Pallas kernels  33.9 us (22%)
    ppermute x30, waiting for transfers between devices, send(): return lax.ppermute(array, 'blk', pairs)  62.7 us
    ppermute x30, starting transfers between devices, send(): return lax.ppermute(array, 'blk', pairs)  42 us
    pallas_call x2, Pallas kernels, keep(): pl.pallas_call(functools.partial(keep_kernel, first), out_shape=jax.Shape...  11.4 us
    pallas_call x6, Pallas kernels, group(): pl.pallas_call(functools.partial(group_kernel, base, turned, fars), out_s...  10.8 us
    pallas_call x2, Pallas kernels, cross(): pl.pallas_call(functools.partial(cross_kernel, offsets, picks, len(arrays...  8.01 us
    ppermute x2, waiting for transfers between devices, on_device(): far = lax.ppermute(packed, 'grp', ZHI)  7.85 us
    ppermute x2, starting transfers between devices, on_device(): far = lax.ppermute(packed, 'grp', ZHI)  3.76 us
  transfers between devices with their start and end apart: 34, of which 15 were waited for; matrix products, arithmetic and copies ran while one was open for 0% of the time, Pallas kernels for 21%

profile of v4, /device:TPU:0, one launch (start us, length us, event | category | flops | bytes accessed | tf_op | source)
XLA Modules:
  0.0 151.1 jit_solution(5155947511062526337)
XLA Ops:
  0.0 1.8 %pick.1.refs_0_ = bf16[256,1024]{1,0:T(8,128)(2,1)S(1)} custom-call(s32[8]{0:T(128)} %batches.1, bf16[256,1024]{1,0:T(8,128)(2,1)} %amp_ref.1), custom_call_target="tpu_custom_call" | custom-call | flops 1000 | bytes 1048576 | tf_op jit(solution)/shard_map/pick/pallas_call | solution.py:69
  1.8 2.1 %collective-permute-start.5 = (bf16[256,1024]{1,0:T(8,128)(2,1)S(1)}, bf16[256,1024]{1,0:T(8,128)(2,1)S(1)}, u32[]{:S(2)}, u32[]{:S(2)}) collective-permute-start(bf16[256,1024]{1,0:T(8,128)(2,1)S(1)} %pick.1.refs_0_), channel_id=1, source_target_pairs={{0,4},{1,5},{2,6},{3,7},{4,0},{5,1},{6,2},{7,3},{8,12},{9,13},{10,... | collective-permute-start | bytes 1572872 | tf_op jit(solution)/shard_map/ppermute | solution.py:38
  3.9 1.5 collective-permute-start
  5.4 1.6 %collective-permute-start.1 = (bf16[256,1024]{1,0:T(8,128)(2,1)S(1)}, bf16[256,1024]{1,0:T(8,128)(2,1)S(1)}, u32[]{:S(2)}, u32[]{:S(2)}) collective-permute-start(bf16[256,1024]{1,0:T(8,128)(2,1)S(1)} %pick.1.refs_0_), channel_id=1, source_target_pairs={{0,1},{1,2},{2,3},{3,0},{4,5},{5,6},{6,7},{7,4},{8,9},{9,10},{10,1... | collective-permute-start | bytes 1572872 | tf_op jit(solution)/shard_map/ppermute | solution.py:38
  7.0 1.7 %collective-permute-start.2 = (bf16[256,1024]{1,0:T(8,128)(2,1)S(1)}, bf16[256,1024]{1,0:T(8,128)(2,1)S(1)}, u32[]{:S(2)}, u32[]{:S(2)}) collective-permute-start(bf16[256,1024]{1,0:T(8,128)(2,1)S(1)} %pick.1.refs_0_), channel_id=1, source_target_pairs={{0,24},{1,25},{2,26},{3,27},{4,28},{5,29},{6,30},{7,31},{8,0},{9,1... | collective-permute-start | bytes 1572872 | tf_op jit(solution)/shard_map/ppermute | solution.py:38
  8.8 1.7 %collective-permute-start.3 = (bf16[256,1024]{1,0:T(8,128)(2,1)S(1)}, bf16[256,1024]{1,0:T(8,128)(2,1)S(1)}, u32[]{:S(2)}, u32[]{:S(2)}) collective-permute-start(bf16[256,1024]{1,0:T(8,128)(2,1)S(1)} %pick.1.refs_0_), channel_id=1, source_target_pairs={{0,3},{1,0},{2,1},{3,2},{4,7},{5,4},{6,5},{7,6},{8,11},{9,8},{10,9... | collective-permute-start | bytes 1572872 | tf_op jit(solution)/shard_map/ppermute | solution.py:38
  10.4 5.4 %collective-permute-done.5.refs_0_.refs_1_ = bf16[256,1024]{1,0:T(8,128)(2,1)S(1)} collective-permute-done((bf16[256,1024]{1,0:T(8,128)(2,1)S(1)}, bf16[256,1024]{1,0:T(8,128)(2,1)S(1)}, u32[]{:S(2)}, u32[]{:S(2)}) %collective-permute-start.5) | collective-permute-done | bytes 524320 | tf_op jit(solution)/shard_map/ppermute | solution.py:38
  15.9 2.8 %collective-permute-start.18 = (bf16[256,512]{1,0:T(8,128)(2,1)S(1)}, bf16[256,512]{1,0:T(8,128)(2,1)S(1)}, u32[]{:S(2)}, u32[]{:S(2)}) collective-permute-start(bf16[256,512]{1,0:T(8,128)(2,1)S(1)} %get-tuple-element.30), channel_id=1, source_target_pairs={{0,24},{1,25},{2,26},{3,27},{4,28},{5,29},{6,30},{7,31},{8,0},{9,1... | collective-permute-start | bytes 786440 | tf_op jit(solution)/shard_map/ppermute | solution.py:38
  18.7 1.1 collective-permute-done.1.refs_1_.refs_0_.refs_4_
  19.8 2.0 %collective-permute-done.2.refs_2_.refs_3_ = bf16[256,1024]{1,0:T(8,128)(2,1)S(1)} collective-permute-done((bf16[256,1024]{1,0:T(8,128)(2,1)S(1)}, bf16[256,1024]{1,0:T(8,128)(2,1)S(1)}, u32[]{:S(2)}, u32[]{:S(2)}) %collective-permute-start.2) | collective-permute-done | bytes 524320 | tf_op jit(solution)/shard_map/ppermute | solution.py:38
  21.8 0.1 shard_map.46
  21.9 1.6 %collective-permute-start.14 = (bf16[256,512]{1,0:T(8,128)(2,1)S(1)}, bf16[256,512]{1,0:T(8,128)(2,1)S(1)}, u32[]{:S(2)}, u32[]{:S(2)}) collective-permute-start(bf16[256,512]{1,0:T(8,128)(2,1)S(1)} %get-tuple-element.28), channel_id=1, source_target_pairs={{0,8},{1,9},{2,10},{3,11},{4,12},{5,13},{6,14},{7,15},{8,16},{9,17... | collective-permute-start | bytes 786440 | tf_op jit(solution)/shard_map/ppermute | solution.py:38
  23.5 1.6 %collective-permute-start.15 = (bf16[256,512]{1,0:T(8,128)(2,1)S(1)}, bf16[256,512]{1,0:T(8,128)(2,1)S(1)}, u32[]{:S(2)}, u32[]{:S(2)}) collective-permute-start(bf16[256,512]{1,0:T(8,128)(2,1)S(1)} %get-tuple-element.29), channel_id=1, source_target_pairs={{0,1},{1,2},{2,3},{3,0},{4,5},{5,6},{6,7},{7,4},{8,9},{9,10},{10,1... | collective-permute-start | bytes 786440 | tf_op jit(solution)/shard_map/ppermute | solution.py:38
  25.1 1.0 collective-permute-start.19
  26.1 1.0 collective-permute-start.17
  27.1 2.3 %collective-permute-start.20 = (bf16[256,512]{1,0:T(8,128)(2,1)S(1)}, bf16[256,512]{1,0:T(8,128)(2,1)S(1)}, u32[]{:S(2)}, u32[]{:S(2)}) collective-permute-start(bf16[256,512]{1,0:T(8,128)(2,1)S(1)} %collective-permute-done.18.refs_4_.refs_3_), channel_id=1, source_target_pairs={{0,24},{1,25},{2,26},{3,27},{4,28},{5,29},{6,30},{7,31},{8,0},{9,1... | collective-permute-start | bytes 786440 | tf_op jit(solution)/shard_map/ppermute | solution.py:38
  29.4 3.0 %collective-permute-done.14.refs_0_.refs_8_ = bf16[256,512]{1,0:T(8,128)(2,1)S(1)} collective-permute-done((bf16[256,512]{1,0:T(8,128)(2,1)S(1)}, bf16[256,512]{1,0:T(8,128)(2,1)S(1)}, u32[]{:S(2)}, u32[]{:S(2)}) %collective-permute-start.14) | collective-permute-done | bytes 262176 | tf_op jit(solution)/shard_map/ppermute | solution.py:38
  32.4 1.6 %collective-permute-start.4 = (bf16[256,512]{1,0:T(8,128)(2,1)S(1)}, bf16[256,512]{1,0:T(8,128)(2,1)S(1)}, u32[]{:S(2)}, u32[]{:S(2)}) collective-permute-start(bf16[256,512]{1,0:T(8,128)(2,1)S(1)} %get-tuple-element.21), channel_id=1, source_target_pairs={{0,1},{1,2},{2,3},{3,0},{4,5},{5,6},{6,7},{7,4},{8,9},{9,10},{10,1... | collective-permute-start | bytes 786440 | tf_op jit(solution)/shard_map/ppermute | solution.py:38
  34.0 1.7 %collective-permute-start.6 = (bf16[256,512]{1,0:T(8,128)(2,1)S(1)}, bf16[256,512]{1,0:T(8,128)(2,1)S(1)}, u32[]{:S(2)}, u32[]{:S(2)}) collective-permute-start(bf16[256,512]{1,0:T(8,128)(2,1)S(1)} %get-tuple-element.22), channel_id=1, source_target_pairs={{0,3},{1,0},{2,1},{3,2},{4,7},{5,4},{6,5},{7,6},{8,11},{9,8},{10,9... | collective-permute-start | bytes 786440 | tf_op jit(solution)/shard_map/ppermute | solution.py:38
  35.6 1.6 %collective-permute-done.19.refs_7_.refs_0_ = bf16[256,512]{1,0:T(8,128)(2,1)S(1)} collective-permute-done((bf16[256,512]{1,0:T(8,128)(2,1)S(1)}, bf16[256,512]{1,0:T(8,128)(2,1)S(1)}, u32[]{:S(2)}, u32[]{:S(2)}) %collective-permute-start.19) | collective-permute-done | bytes 262176 | tf_op jit(solution)/shard_map/ppermute | solution.py:38
  37.2 1.6 %collective-permute-start.8 = (bf16[256,512]{1,0:T(8,128)(2,1)S(1)}, bf16[256,512]{1,0:T(8,128)(2,1)S(1)}, u32[]{:S(2)}, u32[]{:S(2)}) collective-permute-start(bf16[256,512]{1,0:T(8,128)(2,1)S(1)} %get-tuple-element.22), channel_id=1, source_target_pairs={{0,1},{1,2},{2,3},{3,0},{4,5},{5,6},{6,7},{7,4},{8,9},{9,10},{10,1... | collective-permute-start | bytes 786440 | tf_op jit(solution)/shard_map/ppermute | solution.py:38
  38.8 1.2 collective-permute-done.17.refs_3_.refs_1_
  40.0 0.6 collective-permute-start.12
  40.6 1.4 collective-permute-start.13
  42.0 0.1 shard_map.56
  42.2 1.6 %collective-permute-start.21 = (bf16[6,256,256]{2,1,0:T(8,128)(2,1)S(1)}, bf16[6,256,256]{2,1,0:T(8,128)(2,1)S(1)}, u32[]{:S(2)}, u32[]{:S(2)}) collective-permute-start(bf16[6,256,256]{2,1,0:T(8,128)(2,1)S(1)} %get-tuple-element.34), channel_id=1, source_target_pairs={{0,1},{1,2},{2,3},{3,0},{4,5},{5,6},{6,7},{7,4},{8,9},{9,10},{10,1... | collective-permute-start | bytes 2359304 | tf_op jit(solution)/shard_map/ppermute | solution.py:38
  43.8 1.7 %collective-permute-start.7 = (bf16[256,512]{1,0:T(8,128)(2,1)S(1)}, bf16[256,512]{1,0:T(8,128)(2,1)S(1)}, u32[]{:S(2)}, u32[]{:S(2)}) collective-permute-start(bf16[256,512]{1,0:T(8,128)(2,1)S(1)} %collective-permute-done.6.refs_3_.refs_6_), channel_id=1, source_target_pairs={{0,3},{1,0},{2,1},{3,2},{4,7},{5,4},{6,5},{7,6},{8,11},{9,8},{10,9... | collective-permute-start | bytes 786440 | tf_op jit(solution)/shard_map/ppermute | solution.py:38
  45.5 1.5 collective-permute-done.8.refs_1_.refs_5_
  47.0 1.8 %collective-permute-start.30 = (bf16[6,256,256]{2,1,0:T(8,128)(2,1)S(1)}, bf16[6,256,256]{2,1,0:T(8,128)(2,1)S(1)}, u32[]{:S(2)}, u32[]{:S(2)}) collective-permute-start(bf16[6,256,256]{2,1,0:T(8,128)(2,1)S(1)} %get-tuple-element.36), channel_id=1, source_target_pairs={{0,3},{1,0},{2,1},{3,2},{4,7},{5,4},{6,5},{7,6},{8,11},{9,8},{10,9... | collective-permute-start | bytes 2359304 | tf_op jit(solution)/shard_map/ppermute | solution.py:38
  48.9 4.1 %collective-permute-done.7.refs_1_.refs_12_ = bf16[256,512]{1,0:T(8,128)(2,1)S(1)} collective-permute-done((bf16[256,512]{1,0:T(8,128)(2,1)S(1)}, bf16[256,512]{1,0:T(8,128)(2,1)S(1)}, u32[]{:S(2)}, u32[]{:S(2)}) %collective-permute-start.7) | collective-permute-done | bytes 262176 | tf_op jit(solution)/shard_map/ppermute | solution.py:38
  53.0 0.6 collective-permute-start.16
  53.6 0.1 shard_map.48
  53.7 1.1 collective-permute-done.12.refs_0_
  54.8 0.6 collective-permute-start.27
  55.4 10.7 %collective-permute-done.13.refs_1_ = bf16[2,256,512]{2,1,0:T(8,128)(2,1)S(1)} collective-permute-done((bf16[2,256,512]{2,1,0:T(8,128)(2,1)S(1)}, bf16[2,256,512]{2,1,0:T(8,128)(2,1)S(1)}, u32[]{:S(2)}, u32[]{:S(2)}) %collective-permute-start.13) | collective-permute-done | bytes 524320 | tf_op jit(solution)/shard_map/ppermute | solution.py:38
  66.0 3.0 %collective-permute-start.22 = (bf16[6,256,256]{2,1,0:T(8,128)(2,1)S(1)}, bf16[6,256,256]{2,1,0:T(8,128)(2,1)S(1)}, u32[]{:S(2)}, u32[]{:S(2)}) collective-permute-start(bf16[6,256,256]{2,1,0:T(8,128)(2,1)S(1)} %get-tuple-element.34), channel_id=1, source_target_pairs={{0,3},{1,0},{2,1},{3,2},{4,7},{5,4},{6,5},{7,6},{8,11},{9,8},{10,9... | collective-permute-start | bytes 2359304 | tf_op jit(solution)/shard_map/ppermute | solution.py:38
  69.0 5.7 %shard_map.50.refs_6_.refs_13_.refs_3_.refs_1_.refs_2_ = bf16[512,8192]{1,0:T(8,128)(2,1)S(1)} custom-call(s32[8,64]{1,0:T(8,128)} %mask_ref.3, bf16[1024,8192]{1,0:T(8,128)(2,1)} %v_ref.3), custom_call_target="tpu_custom_call" | custom-call | flops 1000 | bytes 8388608 | tf_op jit(solution)/shard_map/pallas_call | solution.py:109
  74.7 5.7 %shard_map.51.refs_7_.refs_14_.refs_4_.refs_2_.refs_3_ = bf16[512,8192]{1,0:T(8,128)(2,1)S(1)} custom-call(s32[8,64]{1,0:T(8,128)} %mask_ref.3, bf16[1024,8192]{1,0:T(8,128)(2,1)} %v_ref.3), custom_call_target="tpu_custom_call" | custom-call | flops 1000 | bytes 8388608 | tf_op jit(solution)/shard_map/pallas_call | solution.py:109
  80.5 0.7 collective-permute-start.29
  81.1 2.9 %collective-permute-start.31 = (bf16[6,256,256]{2,1,0:T(8,128)(2,1)S(1)}, bf16[6,256,256]{2,1,0:T(8,128)(2,1)S(1)}, u32[]{:S(2)}, u32[]{:S(2)}) collective-permute-start(bf16[6,256,256]{2,1,0:T(8,128)(2,1)S(1)} %collective-permute-done.30.refs_0_), channel_id=1, source_target_pairs={{0,3},{1,0},{2,1},{3,2},{4,7},{5,4},{6,5},{7,6},{8,11},{9,8},{10,9... | collective-permute-start | bytes 2359304 | tf_op jit(solution)/shard_map/ppermute | solution.py:38
  84.0 3.5 %shard_map.53.refs_15_ = f32[1024,1024]{1,0:T(8,128)S(1)} custom-call(bf16[256,1024]{1,0:T(8,128)(2,1)S(1)} %pick.1.refs_0_, bf16[256,1024]{1,0:T(8,128)(2,1)S(1)} %collective-permute-done.5.refs_0_.refs_1_, bf16[256,1024]{1,0:T(8,128)(2,1)S(1)} %collective-permute-done.refs_0_.refs_2_, bf16[256,1024]{1,0:T(8,128)(2,1)S(1)} %collective-permute-done.2.refs_2_.refs_3_, ...), custom_call_target="tpu_custom_call" | custom-call | flops 3221225472 | bytes 6291456 | tf_op jit(solution)/shard_map/pallas_call | solution.py:206
  87.5 0.1 collective-permute-start.26
  87.6 0.5 collective-permute-start.9
  88.1 4.6 %shard_map.54.refs_5_.refs_3_ = f32[1024,1024]{1,0:T(8,128)S(1)} custom-call(bf16[2,256,512]{2,1,0:T(8,128)(2,1)S(1)} %collective-permute-done.12.refs_0_, bf16[2,256,512]{2,1,0:T(8,128)(2,1)S(1)} %collective-permute-done.13.refs_1_, bf16[2,256,512]{2,1,0:T(8,128)(2,1)S(1)} %collective-permute-done.16.refs_2_, ...), custom_call_target="tpu_custom_call" | custom-call | flops 4294967296 | bytes 8388608 | tf_op jit(solution)/shard_map/pallas_call | solution.py:206
  92.7 1.0 shard_map.62.refs_4_
  93.7 2.8 %collective-permute-start.28 = (bf16[6,256,256]{2,1,0:T(8,128)(2,1)S(1)}, bf16[6,256,256]{2,1,0:T(8,128)(2,1)S(1)}, u32[]{:S(2)}, u32[]{:S(2)}) collective-permute-start(bf16[6,256,256]{2,1,0:T(8,128)(2,1)S(1)} %collective-permute-done.27.refs_0_), channel_id=1, source_target_pairs={{0,24},{1,25},{2,26},{3,27},{4,28},{5,29},{6,30},{7,31},{8,0},{9,1... | collective-permute-start | bytes 2359304 | tf_op jit(solution)/shard_map/ppermute | solution.py:38
  96.5 2.6 %shard_map.58 = f32[1024,256]{1,0:T(8,128)S(1)} custom-call(bf16[6,256,256]{2,1,0:T(8,128)(2,1)S(1)} %collective-permute-done.21.refs_0_, bf16[6,256,256]{2,1,0:T(8,128)(2,1)S(1)} %collective-permute-done.22.refs_1_, bf16[6,256,256]{2,1,0:T(8,128)(2,1)S(1)} %collective-permute-done.23.refs_2_, ...), custom_call_target="tpu_custom_call" | custom-call | flops 2415919104 | bytes 9437184 | tf_op jit(solution)/shard_map/pallas_call | solution.py:239
  99.2 0.1 collective-permute-start.24
  99.3 1.8 %shard_map.63 = f32[1024,256]{1,0:T(8,128)S(1)} custom-call(bf16[6,256,256]{2,1,0:T(8,128)(2,1)S(1)} %collective-permute-done.29.refs_0_, bf16[6,256,256]{2,1,0:T(8,128)(2,1)S(1)} %collective-permute-done.31.refs_1_, bf16[512,8192]{1,0:T(8,128)(2,1)S(1)} %shard_map.50.refs_6_.refs_13_.refs_3_.refs_1_.refs_2_, ...), custom_call_target="tpu_custom_call" | custom-call | flops 1610612736 | bytes 9437184 | tf_op jit(solution)/shard_map/pallas_call | solution.py:239
  101.1 0.6 collective-permute-start.32
  101.6 6.5 %collective-permute-done.26.refs_0_ = bf16[6,256,256]{2,1,0:T(8,128)(2,1)S(1)} collective-permute-done((bf16[6,256,256]{2,1,0:T(8,128)(2,1)S(1)}, bf16[6,256,256]{2,1,0:T(8,128)(2,1)S(1)}, u32[]{:S(2)}, u32[]{:S(2)}) %collective-permute-start.26) | collective-permute-done | bytes 786464 | tf_op jit(solution)/shard_map/ppermute | solution.py:38
  108.1 14.0 %collective-permute-done.9.refs_0_ = bf16[6,256,256]{2,1,0:T(8,128)(2,1)S(1)} collective-permute-done((bf16[6,256,256]{2,1,0:T(8,128)(2,1)S(1)}, bf16[6,256,256]{2,1,0:T(8,128)(2,1)S(1)}, u32[]{:S(2)}, u32[]{:S(2)}) %collective-permute-start.9) | collective-permute-done | bytes 786464 | tf_op jit(solution)/shard_map/ppermute | solution.py:38
  122.1 1.0 shard_map.60.refs_4_
  123.1 1.8 %shard_map.61.mine.refs_1_ = f32[1024,256]{1,0:T(8,128)S(1)} custom-call(bf16[6,256,256]{2,1,0:T(8,128)(2,1)S(1)} %collective-permute-done.26.refs_0_, bf16[6,256,256]{2,1,0:T(8,128)(2,1)S(1)} %collective-permute-done.28.refs_1_, bf16[512,8192]{1,0:T(8,128)(2,1)S(1)} %shard_map.50.refs_6_.refs_13_.refs_3_.refs_1_.refs_2_, ...), custom_call_target="tpu_custom_call" | custom-call | flops 1610612736 | bytes 9437184 | tf_op jit(solution)/shard_map/pallas_call | solution.py:239
  125.0 10.4 %collective-permute-done.11.refs_2_ = bf16[6,256,256]{2,1,0:T(8,128)(2,1)S(1)} collective-permute-done((bf16[6,256,256]{2,1,0:T(8,128)(2,1)S(1)}, bf16[6,256,256]{2,1,0:T(8,128)(2,1)S(1)}, u32[]{:S(2)}, u32[]{:S(2)}) %collective-permute-start.11) | collective-permute-done | bytes 786464 | tf_op jit(solution)/shard_map/ppermute | solution.py:38
  135.3 2.6 %shard_map.55.mine.refs_0_ = f32[1024,256]{1,0:T(8,128)S(1)} custom-call(bf16[6,256,256]{2,1,0:T(8,128)(2,1)S(1)} %collective-permute-done.9.refs_0_, bf16[6,256,256]{2,1,0:T(8,128)(2,1)S(1)} %collective-permute-done.10.refs_1_, bf16[6,256,256]{2,1,0:T(8,128)(2,1)S(1)} %collective-permute-done.11.refs_2_, ...), custom_call_target="tpu_custom_call" | custom-call | flops 2415919104 | bytes 9437184 | tf_op jit(solution)/shard_map/pallas_call | solution.py:239
  138.0 0.2 code.2
  138.1 3.7 %collective-permute-start.25 = (s16[1088,128]{1,0:T(8,128)(2,1)S(1)}, s16[1088,128]{1,0:T(8,128)(2,1)S(1)}, u32[]{:S(2)}, u32[]{:S(2)}) collective-permute-start(s16[1088,128]{1,0:T(8,128)(2,1)S(1)} %code.2), channel_id=1, source_target_pairs={{0,64},{32,96},{64,0},{96,32},{1,65},{33,97},{65,1},{97,33},{2,66}... | collective-permute-start | bytes 835592 | tf_op jit(solution)/shard_map/ppermute | solution.py:371
  141.8 0.2 code.3
  142.0 0.1 collective-permute-start.33
  142.1 4.3 %collective-permute-done.25.refs_2_ = s16[1088,128]{1,0:T(8,128)(2,1)S(1)} collective-permute-done((s16[1088,128]{1,0:T(8,128)(2,1)S(1)}, s16[1088,128]{1,0:T(8,128)(2,1)S(1)}, u32[]{:S(2)}, u32[]{:S(2)}) %collective-permute-start.25) | collective-permute-done | bytes 278560 | tf_op jit(solution)/shard_map/ppermute | solution.py:371
  146.3 0.2 shard_map.59.refs_0_
  146.5 3.6 %collective-permute-done.33.refs_3_ = s16[1088,128]{1,0:T(8,128)(2,1)S(1)} collective-permute-done((s16[1088,128]{1,0:T(8,128)(2,1)S(1)}, s16[1088,128]{1,0:T(8,128)(2,1)S(1)}, u32[]{:S(2)}, u32[]{:S(2)}) %collective-permute-start.33) | collective-permute-done | bytes 278560 | tf_op jit(solution)/shard_map/ppermute | solution.py:371
  150.1 1.0 shard_map.64
  (26 shorter events, 0.2 us)
Async XLA Ops:
  1.8 14.0 %collective-permute-start.5 = (bf16[256,1024]{1,0:T(8,128)(2,1)S(1)}, bf16[256,1024]{1,0:T(8,128)(2,1)S(1)}, u32[]{:S(2)}, u32[]{:S(2)}) collective-permute-start(bf16[256,1024]{1,0:T(8,128)(2,1)S(1)} %pick.1.refs_0_), channel_id=1, source_target_pairs={{0,4},{1,5},{2,6},{3,7},{4,0},{5,1},{6,2},{7,3},{8,12},{9,13},{10,... | collective-permute-start | bytes 1572872 | tf_op jit(solution)/shard_map/ppermute | solution.py:38
  3.9 14.8 %collective-permute-start = (bf16[256,1024]{1,0:T(8,128)(2,1)S(1)}, bf16[256,1024]{1,0:T(8,128)(2,1)S(1)}, u32[]{:S(2)}, u32[]{:S(2)}) collective-permute-start(bf16[256,1024]{1,0:T(8,128)(2,1)S(1)} %pick.1.refs_0_), channel_id=1, source_target_pairs={{0,8},{1,9},{2,10},{3,11},{4,12},{5,13},{6,14},{7,15},{8,16},{9,17... | collective-permute-start | bytes 1572872 | tf_op jit(solution)/shard_map/ppermute | solution.py:38
  5.4 14.4 %collective-permute-start.1 = (bf16[256,1024]{1,0:T(8,128)(2,1)S(1)}, bf16[256,1024]{1,0:T(8,128)(2,1)S(1)}, u32[]{:S(2)}, u32[]{:S(2)}) collective-permute-start(bf16[256,1024]{1,0:T(8,128)(2,1)S(1)} %pick.1.refs_0_), channel_id=1, source_target_pairs={{0,1},{1,2},{2,3},{3,0},{4,5},{5,6},{6,7},{7,4},{8,9},{9,10},{10,1... | collective-permute-start | bytes 1572872 | tf_op jit(solution)/shard_map/ppermute | solution.py:38
  7.0 14.8 %collective-permute-start.2 = (bf16[256,1024]{1,0:T(8,128)(2,1)S(1)}, bf16[256,1024]{1,0:T(8,128)(2,1)S(1)}, u32[]{:S(2)}, u32[]{:S(2)}) collective-permute-start(bf16[256,1024]{1,0:T(8,128)(2,1)S(1)} %pick.1.refs_0_), channel_id=1, source_target_pairs={{0,24},{1,25},{2,26},{3,27},{4,28},{5,29},{6,30},{7,31},{8,0},{9,1... | collective-permute-start | bytes 1572872 | tf_op jit(solution)/shard_map/ppermute | solution.py:38
  8.8 13.1 %collective-permute-start.3 = (bf16[256,1024]{1,0:T(8,128)(2,1)S(1)}, bf16[256,1024]{1,0:T(8,128)(2,1)S(1)}, u32[]{:S(2)}, u32[]{:S(2)}) collective-permute-start(bf16[256,1024]{1,0:T(8,128)(2,1)S(1)} %pick.1.refs_0_), channel_id=1, source_target_pairs={{0,3},{1,0},{2,1},{3,2},{4,7},{5,4},{6,5},{7,6},{8,11},{9,8},{10,9... | collective-permute-start | bytes 1572872 | tf_op jit(solution)/shard_map/ppermute | solution.py:38
  15.9 11.2 %collective-permute-start.18 = (bf16[256,512]{1,0:T(8,128)(2,1)S(1)}, bf16[256,512]{1,0:T(8,128)(2,1)S(1)}, u32[]{:S(2)}, u32[]{:S(2)}) collective-permute-start(bf16[256,512]{1,0:T(8,128)(2,1)S(1)} %get-tuple-element.30), channel_id=1, source_target_pairs={{0,24},{1,25},{2,26},{3,27},{4,28},{5,29},{6,30},{7,31},{8,0},{9,1... | collective-permute-start | bytes 786440 | tf_op jit(solution)/shard_map/ppermute | solution.py:38
  21.9 10.5 %collective-permute-start.14 = (bf16[256,512]{1,0:T(8,128)(2,1)S(1)}, bf16[256,512]{1,0:T(8,128)(2,1)S(1)}, u32[]{:S(2)}, u32[]{:S(2)}) collective-permute-start(bf16[256,512]{1,0:T(8,128)(2,1)S(1)} %get-tuple-element.28), channel_id=1, source_target_pairs={{0,8},{1,9},{2,10},{3,11},{4,12},{5,13},{6,14},{7,15},{8,16},{9,17... | collective-permute-start | bytes 786440 | tf_op jit(solution)/shard_map/ppermute | solution.py:38
  23.5 10.5 %collective-permute-start.15 = (bf16[256,512]{1,0:T(8,128)(2,1)S(1)}, bf16[256,512]{1,0:T(8,128)(2,1)S(1)}, u32[]{:S(2)}, u32[]{:S(2)}) collective-permute-start(bf16[256,512]{1,0:T(8,128)(2,1)S(1)} %get-tuple-element.29), channel_id=1, source_target_pairs={{0,1},{1,2},{2,3},{3,0},{4,5},{5,6},{6,7},{7,4},{8,9},{9,10},{10,1... | collective-permute-start | bytes 786440 | tf_op jit(solution)/shard_map/ppermute | solution.py:38
  25.1 12.1 %collective-permute-start.19 = (bf16[256,512]{1,0:T(8,128)(2,1)S(1)}, bf16[256,512]{1,0:T(8,128)(2,1)S(1)}, u32[]{:S(2)}, u32[]{:S(2)}) collective-permute-start(bf16[256,512]{1,0:T(8,128)(2,1)S(1)} %get-tuple-element.31), channel_id=1, source_target_pairs={{0,8},{1,9},{2,10},{3,11},{4,12},{5,13},{6,14},{7,15},{8,16},{9,17... | collective-permute-start | bytes 786440 | tf_op jit(solution)/shard_map/ppermute | solution.py:38
  26.1 13.9 %collective-permute-start.17 = (bf16[256,512]{1,0:T(8,128)(2,1)S(1)}, bf16[256,512]{1,0:T(8,128)(2,1)S(1)}, u32[]{:S(2)}, u32[]{:S(2)}) collective-permute-start(bf16[256,512]{1,0:T(8,128)(2,1)S(1)} %get-tuple-element.30), channel_id=1, source_target_pairs={{0,8},{1,9},{2,10},{3,11},{4,12},{5,13},{6,14},{7,15},{8,16},{9,17... | collective-permute-start | bytes 786440 | tf_op jit(solution)/shard_map/ppermute | solution.py:38
  27.1 13.5 %collective-permute-start.20 = (bf16[256,512]{1,0:T(8,128)(2,1)S(1)}, bf16[256,512]{1,0:T(8,128)(2,1)S(1)}, u32[]{:S(2)}, u32[]{:S(2)}) collective-permute-start(bf16[256,512]{1,0:T(8,128)(2,1)S(1)} %collective-permute-done.18.refs_4_.refs_3_), channel_id=1, source_target_pairs={{0,24},{1,25},{2,26},{3,27},{4,28},{5,29},{6,30},{7,31},{8,0},{9,1... | collective-permute-start | bytes 786440 | tf_op jit(solution)/shard_map/ppermute | solution.py:38
  32.4 9.8 %collective-permute-start.4 = (bf16[256,512]{1,0:T(8,128)(2,1)S(1)}, bf16[256,512]{1,0:T(8,128)(2,1)S(1)}, u32[]{:S(2)}, u32[]{:S(2)}) collective-permute-start(bf16[256,512]{1,0:T(8,128)(2,1)S(1)} %get-tuple-element.21), channel_id=1, source_target_pairs={{0,1},{1,2},{2,3},{3,0},{4,5},{5,6},{6,7},{7,4},{8,9},{9,10},{10,1... | collective-permute-start | bytes 786440 | tf_op jit(solution)/shard_map/ppermute | solution.py:38
  34.0 9.8 %collective-permute-start.6 = (bf16[256,512]{1,0:T(8,128)(2,1)S(1)}, bf16[256,512]{1,0:T(8,128)(2,1)S(1)}, u32[]{:S(2)}, u32[]{:S(2)}) collective-permute-start(bf16[256,512]{1,0:T(8,128)(2,1)S(1)} %get-tuple-element.22), channel_id=1, source_target_pairs={{0,3},{1,0},{2,1},{3,2},{4,7},{5,4},{6,5},{7,6},{8,11},{9,8},{10,9... | collective-permute-start | bytes 786440 | tf_op jit(solution)/shard_map/ppermute | solution.py:38
  37.2 9.8 %collective-permute-start.8 = (bf16[256,512]{1,0:T(8,128)(2,1)S(1)}, bf16[256,512]{1,0:T(8,128)(2,1)S(1)}, u32[]{:S(2)}, u32[]{:S(2)}) collective-permute-start(bf16[256,512]{1,0:T(8,128)(2,1)S(1)} %get-tuple-element.22), channel_id=1, source_target_pairs={{0,1},{1,2},{2,3},{3,0},{4,5},{5,6},{6,7},{7,4},{8,9},{9,10},{10,1... | collective-permute-start | bytes 786440 | tf_op jit(solution)/shard_map/ppermute | solution.py:38
  40.0 14.8 %collective-permute-start.12 = (bf16[2,256,512]{2,1,0:T(8,128)(2,1)S(1)}, bf16[2,256,512]{2,1,0:T(8,128)(2,1)S(1)}, u32[]{:S(2)}, u32[]{:S(2)}) collective-permute-start(bf16[2,256,512]{2,1,0:T(8,128)(2,1)S(1)} %get-tuple-element.26), channel_id=1, source_target_pairs={{0,4},{1,5},{2,6},{3,7},{4,0},{5,1},{6,2},{7,3},{8,12},{9,13},{10,... | collective-permute-start | bytes 1572872 | tf_op jit(solution)/shard_map/ppermute | solution.py:38
  40.6 25.4 %collective-permute-start.13 = (bf16[2,256,512]{2,1,0:T(8,128)(2,1)S(1)}, bf16[2,256,512]{2,1,0:T(8,128)(2,1)S(1)}, u32[]{:S(2)}, u32[]{:S(2)}) collective-permute-start(bf16[2,256,512]{2,1,0:T(8,128)(2,1)S(1)} %get-tuple-element.27), channel_id=1, source_target_pairs={{0,4},{1,5},{2,6},{3,7},{4,0},{5,1},{6,2},{7,3},{8,12},{9,13},{10,... | collective-permute-start | bytes 1572872 | tf_op jit(solution)/shard_map/ppermute | solution.py:38
  42.2 26.9 %collective-permute-start.21 = (bf16[6,256,256]{2,1,0:T(8,128)(2,1)S(1)}, bf16[6,256,256]{2,1,0:T(8,128)(2,1)S(1)}, u32[]{:S(2)}, u32[]{:S(2)}) collective-permute-start(bf16[6,256,256]{2,1,0:T(8,128)(2,1)S(1)} %get-tuple-element.34), channel_id=1, source_target_pairs={{0,1},{1,2},{2,3},{3,0},{4,5},{5,6},{6,7},{7,4},{8,9},{9,10},{10,1... | collective-permute-start | bytes 2359304 | tf_op jit(solution)/shard_map/ppermute | solution.py:38
  43.8 9.2 %collective-permute-start.7 = (bf16[256,512]{1,0:T(8,128)(2,1)S(1)}, bf16[256,512]{1,0:T(8,128)(2,1)S(1)}, u32[]{:S(2)}, u32[]{:S(2)}) collective-permute-start(bf16[256,512]{1,0:T(8,128)(2,1)S(1)} %collective-permute-done.6.refs_3_.refs_6_), channel_id=1, source_target_pairs={{0,3},{1,0},{2,1},{3,2},{4,7},{5,4},{6,5},{7,6},{8,11},{9,8},{10,9... | collective-permute-start | bytes 786440 | tf_op jit(solution)/shard_map/ppermute | solution.py:38
  47.0 34.1 %collective-permute-start.30 = (bf16[6,256,256]{2,1,0:T(8,128)(2,1)S(1)}, bf16[6,256,256]{2,1,0:T(8,128)(2,1)S(1)}, u32[]{:S(2)}, u32[]{:S(2)}) collective-permute-start(bf16[6,256,256]{2,1,0:T(8,128)(2,1)S(1)} %get-tuple-element.36), channel_id=1, source_target_pairs={{0,3},{1,0},{2,1},{3,2},{4,7},{5,4},{6,5},{7,6},{8,11},{9,8},{10,9... | collective-permute-start | bytes 2359304 | tf_op jit(solution)/shard_map/ppermute | solution.py:38
  53.0 27.5 %collective-permute-start.16 = (bf16[2,256,512]{2,1,0:T(8,128)(2,1)S(1)}, bf16[2,256,512]{2,1,0:T(8,128)(2,1)S(1)}, u32[]{:S(2)}, u32[]{:S(2)}) collective-permute-start(bf16[2,256,512]{2,1,0:T(8,128)(2,1)S(1)} %shard_map.52), channel_id=1, source_target_pairs={{0,4},{1,5},{2,6},{3,7},{4,0},{5,1},{6,2},{7,3},{8,12},{9,13},{10,... | collective-permute-start | bytes 1572872 | tf_op jit(solution)/shard_map/ppermute | solution.py:38
  54.8 32.7 %collective-permute-start.27 = (bf16[6,256,256]{2,1,0:T(8,128)(2,1)S(1)}, bf16[6,256,256]{2,1,0:T(8,128)(2,1)S(1)}, u32[]{:S(2)}, u32[]{:S(2)}) collective-permute-start(bf16[6,256,256]{2,1,0:T(8,128)(2,1)S(1)} %get-tuple-element.35), channel_id=1, source_target_pairs={{0,24},{1,25},{2,26},{3,27},{4,28},{5,29},{6,30},{7,31},{8,0},{9,1... | collective-permute-start | bytes 2359304 | tf_op jit(solution)/shard_map/ppermute | solution.py:38
  66.0 21.6 %collective-permute-start.22 = (bf16[6,256,256]{2,1,0:T(8,128)(2,1)S(1)}, bf16[6,256,256]{2,1,0:T(8,128)(2,1)S(1)}, u32[]{:S(2)}, u32[]{:S(2)}) collective-permute-start(bf16[6,256,256]{2,1,0:T(8,128)(2,1)S(1)} %get-tuple-element.34), channel_id=1, source_target_pairs={{0,3},{1,0},{2,1},{3,2},{4,7},{5,4},{6,5},{7,6},{8,11},{9,8},{10,9... | collective-permute-start | bytes 2359304 | tf_op jit(solution)/shard_map/ppermute | solution.py:38
  69.0 24.7 %collective-permute-start.23 = (bf16[6,256,256]{2,1,0:T(8,128)(2,1)S(1)}, bf16[6,256,256]{2,1,0:T(8,128)(2,1)S(1)}, u32[]{:S(2)}, u32[]{:S(2)}) collective-permute-start(bf16[6,256,256]{2,1,0:T(8,128)(2,1)S(1)} %collective-permute-done.21.refs_0_), channel_id=1, source_target_pairs={{0,1},{1,2},{2,3},{3,0},{4,5},{5,6},{6,7},{7,4},{8,9},{9,10},{10,1... | collective-permute-start | bytes 2359304 | tf_op jit(solution)/shard_map/ppermute | solution.py:38
  80.5 18.7 %collective-permute-start.29 = (bf16[6,256,256]{2,1,0:T(8,128)(2,1)S(1)}, bf16[6,256,256]{2,1,0:T(8,128)(2,1)S(1)}, u32[]{:S(2)}, u32[]{:S(2)}) collective-permute-start(bf16[6,256,256]{2,1,0:T(8,128)(2,1)S(1)} %get-tuple-element.36), channel_id=1, source_target_pairs={{0,1},{1,2},{2,3},{3,0},{4,5},{5,6},{6,7},{7,4},{8,9},{9,10},{10,1... | collective-permute-start | bytes 2359304 | tf_op jit(solution)/shard_map/ppermute | solution.py:38
  81.1 18.1 %collective-permute-start.31 = (bf16[6,256,256]{2,1,0:T(8,128)(2,1)S(1)}, bf16[6,256,256]{2,1,0:T(8,128)(2,1)S(1)}, u32[]{:S(2)}, u32[]{:S(2)}) collective-permute-start(bf16[6,256,256]{2,1,0:T(8,128)(2,1)S(1)} %collective-permute-done.30.refs_0_), channel_id=1, source_target_pairs={{0,3},{1,0},{2,1},{3,2},{4,7},{5,4},{6,5},{7,6},{8,11},{9,8},{10,9... | collective-permute-start | bytes 2359304 | tf_op jit(solution)/shard_map/ppermute | solution.py:38
  87.5 20.6 %collective-permute-start.26 = (bf16[6,256,256]{2,1,0:T(8,128)(2,1)S(1)}, bf16[6,256,256]{2,1,0:T(8,128)(2,1)S(1)}, u32[]{:S(2)}, u32[]{:S(2)}) collective-permute-start(bf16[6,256,256]{2,1,0:T(8,128)(2,1)S(1)} %get-tuple-element.35), channel_id=1, source_target_pairs={{0,8},{1,9},{2,10},{3,11},{4,12},{5,13},{6,14},{7,15},{8,16},{9,17... | collective-permute-start | bytes 2359304 | tf_op jit(solution)/shard_map/ppermute | solution.py:38
  87.6 34.5 %collective-permute-start.9 = (bf16[6,256,256]{2,1,0:T(8,128)(2,1)S(1)}, bf16[6,256,256]{2,1,0:T(8,128)(2,1)S(1)}, u32[]{:S(2)}, u32[]{:S(2)}) collective-permute-start(bf16[6,256,256]{2,1,0:T(8,128)(2,1)S(1)} %get-tuple-element.25), channel_id=1, source_target_pairs={{0,8},{1,9},{2,10},{3,11},{4,12},{5,13},{6,14},{7,15},{8,16},{9,17... | collective-permute-start | bytes 2359304 | tf_op jit(solution)/shard_map/ppermute | solution.py:38
  93.7 29.4 %collective-permute-start.28 = (bf16[6,256,256]{2,1,0:T(8,128)(2,1)S(1)}, bf16[6,256,256]{2,1,0:T(8,128)(2,1)S(1)}, u32[]{:S(2)}, u32[]{:S(2)}) collective-permute-start(bf16[6,256,256]{2,1,0:T(8,128)(2,1)S(1)} %collective-permute-done.27.refs_0_), channel_id=1, source_target_pairs={{0,24},{1,25},{2,26},{3,27},{4,28},{5,29},{6,30},{7,31},{8,0},{9,1... | collective-permute-start | bytes 2359304 | tf_op jit(solution)/shard_map/ppermute | solution.py:38
  99.2 38.8 %collective-permute-start.24 = (f32[1024,256]{1,0:T(8,128)S(1)}, f32[1024,256]{1,0:T(8,128)S(1)}, u32[]{:S(2)}, u32[]{:S(2)}) collective-permute-start(f32[1024,256]{1,0:T(8,128)S(1)} %shard_map.58), channel_id=1, source_target_pairs={{0,32},{32,0},{64,96},{96,64},{1,33},{33,1},{65,97},{97,65},{2,34}... | collective-permute-start | bytes 3145736 | tf_op jit(solution)/shard_map/ppermute | solution.py:364
  101.1 40.7 %collective-permute-start.32 = (f32[1024,256]{1,0:T(8,128)S(1)}, f32[1024,256]{1,0:T(8,128)S(1)}, u32[]{:S(2)}, u32[]{:S(2)}) collective-permute-start(f32[1024,256]{1,0:T(8,128)S(1)} %shard_map.63), channel_id=1, source_target_pairs={{0,32},{32,0},{64,96},{96,64},{1,33},{33,1},{65,97},{97,65},{2,34}... | collective-permute-start | bytes 3145736 | tf_op jit(solution)/shard_map/ppermute | solution.py:364
  108.1 16.8 %collective-permute-start.10 = (bf16[6,256,256]{2,1,0:T(8,128)(2,1)S(1)}, bf16[6,256,256]{2,1,0:T(8,128)(2,1)S(1)}, u32[]{:S(2)}, u32[]{:S(2)}) collective-permute-start(bf16[6,256,256]{2,1,0:T(8,128)(2,1)S(1)} %get-tuple-element.25), channel_id=1, source_target_pairs={{0,24},{1,25},{2,26},{3,27},{4,28},{5,29},{6,30},{7,31},{8,0},{9,1... | collective-permute-start | bytes 2359304 | tf_op jit(solution)/shard_map/ppermute | solution.py:38
  122.1 13.2 %collective-permute-start.11 = (bf16[6,256,256]{2,1,0:T(8,128)(2,1)S(1)}, bf16[6,256,256]{2,1,0:T(8,128)(2,1)S(1)}, u32[]{:S(2)}, u32[]{:S(2)}) collective-permute-start(bf16[6,256,256]{2,1,0:T(8,128)(2,1)S(1)} %collective-permute-done.9.refs_0_), channel_id=1, source_target_pairs={{0,8},{1,9},{2,10},{3,11},{4,12},{5,13},{6,14},{7,15},{8,16},{9,17... | collective-permute-start | bytes 2359304 | tf_op jit(solution)/shard_map/ppermute | solution.py:38
  138.1 8.2 %collective-permute-start.25 = (s16[1088,128]{1,0:T(8,128)(2,1)S(1)}, s16[1088,128]{1,0:T(8,128)(2,1)S(1)}, u32[]{:S(2)}, u32[]{:S(2)}) collective-permute-start(s16[1088,128]{1,0:T(8,128)(2,1)S(1)} %code.2), channel_id=1, source_target_pairs={{0,64},{32,96},{64,0},{96,32},{1,65},{33,97},{65,1},{97,33},{2,66}... | collective-permute-start | bytes 835592 | tf_op jit(solution)/shard_map/ppermute | solution.py:371
  142.0 8.1 %collective-permute-start.33 = (s16[1088,128]{1,0:T(8,128)(2,1)S(1)}, s16[1088,128]{1,0:T(8,128)(2,1)S(1)}, u32[]{:S(2)}, u32[]{:S(2)}) collective-permute-start(s16[1088,128]{1,0:T(8,128)(2,1)S(1)} %code.3), channel_id=1, source_target_pairs={{0,64},{32,96},{64,0},{96,32},{1,65},{33,97},{65,1},{97,33},{2,66}... | collective-permute-start | bytes 835592 | tf_op jit(solution)/shard_map/ppermute | solution.py:371
